TPU v7x, 32 devices: a whole 2x2x4 slice. The times are simulated.
32 devices in a mesh: rep: 2 (over core), shard: 16 (over z, y, x).
Axes of the slice: x: 2, y: 2, z: 4, core: 2. Of those that a mesh axis runs over, the one named last changes fastest.
Arguments:
- tokens: bfloat16 [32, 1024, 768], P('rep', 'shard'), may hold values from -6 to 6
- cotangent: bfloat16 [32, 1024, 768], P('rep', 'shard'), may hold values from -6 to 6
- lengths: int32 [2, 16], P('rep'), may hold values from 512 to 1024, as said below
- order: int32 [2, 16], P('rep'), may hold values from 0 to 15, each once within a row
- norm_weight: bfloat16 [768], P('shard'), may hold values from 0.099609375 to 1.8984375
- in_weight: bfloat16 [768, 3352], P('shard'), may hold values from -0.21875 to 0.21875
- conv_weight: bfloat16 [1792, 4], P('shard'), may hold values from -3 to 3
- conv_bias: bfloat16 [1792], P('shard'), may hold values from -3 to 3
- step_bias: float32 [24], replicated, may hold values from -5.5 to -2.5
- decay_log: float32 [24], replicated, may hold values from 0 to 2.77
- skip_gain: float32 [24], replicated, may hold values from 0.5 to 1.5
- gate_norm_weight: bfloat16 [1536], P('shard'), may hold values from 0.099609375 to 1.8984375
- out_weight: bfloat16 [1536, 768], P('shard'), may hold values from -0.15625 to 0.15625
Outputs:
- output: bfloat16 [32, 1024, 768], P('rep', 'shard')
- input_grad: bfloat16 [32, 1024, 768], P('rep', 'shard')
- grad_norm: float32 [768], P('shard')
- grad_in: float32 [768, 3352], P('shard')
- grad_conv: float32 [1792, 4], P('shard')
- grad_conv_bias: float32 [1792], P('shard')
- grad_step_bias: float32 [24], replicated
- grad_decay_log: float32 [24], replicated
- grad_skip: float32 [24], replicated
- grad_gate_norm: float32 [1536], P('shard')
- grad_out: float32 [1536, 768], P('shard')
Inputs may be any that keep to these rules, and one draw needn't show every extreme that they name: Each row of order holds every number from 0 to 15 once: slot k of group r holds sequence order[r, k]. lengths[r, s] counts the valid leading positions of sequence s of group r; each row has one entry equal to 1024 and one equal to 512.
All inputs are finite; a program needn't handle non-finite values.
Results may differ from a plain program's by a relative error of at most 0.012.
The roundings to bfloat16 on the way count: a program that leaves them out, or rounds other values in their place, can miss the bound.
Values may be sent and summed in bfloat16 or wider, within the bound.
A program may use at most 192 MiB of HBM per device.

v0:
```python
import jax
import jax.numpy as jnp
from jax import lax
from jax.sharding import PartitionSpec as P

HEADS = 24
HEADDIM = 64
STATE = 128
CONV = 4
SPAN = 256
DI = 1536
XBC = 1792


epsilon = 1e-05


def decay_terms(log_block, step_block):
    cumul = jnp.cumsum(log_block, axis=0)
    cumul_heads = cumul.T
    positions = log_block.shape[0]
    causal = jnp.arange(positions)[:, None] >= jnp.arange(positions)[None, :]
    spread = jnp.where(causal[None], cumul_heads[:, :, None] - cumul_heads[:, None, :], 0.0)
    factor = jnp.where(causal[None], jnp.exp(spread), 0.0) * step_block.T[:, None, :]
    carry_weight = jnp.exp(cumul[-1][None, :] - cumul) * step_block
    return (factor, carry_weight, jnp.exp(cumul), jnp.exp(cumul[-1]))


def norm_part(tok_float, norm_gain):
    return (
        tok_float
        * lax.rsqrt(jnp.mean(tok_float * tok_float, axis=-1, keepdims=True) + epsilon)
        * norm_gain
    )


def conv_part(conv_in, conv_taps, conv_shift):
    length = conv_in.shape[0]
    padded = jnp.concatenate(
        [jnp.zeros((CONV - 1, conv_in.shape[1]), jnp.float32), conv_in], axis=0
    )
    total = conv_shift[None, :] + jnp.zeros_like(conv_in)
    for tap in range(CONV):
        total = total + conv_taps[:, tap][None, :] * padded[tap : tap + length]
    return jax.nn.silu(total)


def step_part(step_raw, step_bias, decay_log):
    step_size = jax.nn.softplus(step_raw + step_bias[None, :])
    return (step_size, -jnp.exp(decay_log)[None, :] * step_size)


def gate_part(scan_out, heads_in, skip_gain, gate_raw, gate_gain):
    mixed = scan_out + jnp.repeat(skip_gain, HEADDIM)[None, :] * heads_in
    gated = mixed * jax.nn.silu(gate_raw)
    return gated * lax.rsqrt(jnp.mean(gated * gated, axis=-1, keepdims=True) + epsilon) * gate_gain


def block_forward(state, inputs):
    heads_blk, keys_blk, query_blk, step_blk, log_blk = inputs
    factor, carry_weight, growth, growth_last = decay_terms(log_blk, step_blk)
    scores = jnp.einsum("tn,sn->ts", query_blk, keys_blk, preferred_element_type=jnp.float32)
    mixing = (scores[None] * factor).astype(jnp.bfloat16)
    within = jnp.einsum("hts,shp->thp", mixing, heads_blk, preferred_element_type=jnp.float32)
    across = jnp.einsum(
        "tn,hpn->thp", query_blk, state.astype(jnp.bfloat16), preferred_element_type=jnp.float32
    )
    result = within + growth[:, :, None] * across
    weighted = (heads_blk.astype(jnp.float32) * carry_weight[:, :, None]).astype(jnp.bfloat16)
    contrib = jnp.einsum("sn,shp->hpn", keys_blk, weighted, preferred_element_type=jnp.float32)
    return (growth_last[:, None, None] * state + contrib, (result, state))


def block_backward(later, inputs):
    heads_blk, keys_blk, query_blk, step_blk, log_blk, grad_blk, state = inputs
    terms, decay_pull = jax.vjp(decay_terms, log_blk, step_blk)
    factor, carry_weight, growth, growth_last = terms
    scores = jnp.einsum("tn,sn->ts", query_blk, keys_blk, preferred_element_type=jnp.float32)
    mixing = (scores[None] * factor).astype(jnp.bfloat16)
    state_low = state.astype(jnp.bfloat16)
    across = jnp.einsum("tn,hpn->thp", query_blk, state_low, preferred_element_type=jnp.float32)
    heads_float = heads_blk.astype(jnp.float32)
    weighted = (heads_float * carry_weight[:, :, None]).astype(jnp.bfloat16)
    grad_within = grad_blk.astype(jnp.bfloat16)
    grad_across = (growth[:, :, None] * grad_blk).astype(jnp.bfloat16)
    grad_mixing = jnp.einsum(
        "thp,shp->hts", grad_within, heads_blk, preferred_element_type=jnp.float32
    )
    grad_heads = jnp.einsum("hts,thp->shp", mixing, grad_within, preferred_element_type=jnp.float32)
    grad_query = jnp.einsum(
        "thp,hpn->tn", grad_across, state_low, preferred_element_type=jnp.float32
    )
    grad_state = jnp.einsum(
        "thp,tn->hpn", grad_across, query_blk, preferred_element_type=jnp.float32
    )
    grad_state = grad_state + growth_last[:, None, None] * later
    grad_growth = jnp.sum(grad_blk * across, axis=2)
    later_low = later.astype(jnp.bfloat16)
    grad_weighted = jnp.einsum(
        "hpn,sn->shp", later_low, keys_blk, preferred_element_type=jnp.float32
    )
    grad_keys = jnp.einsum("hpn,shp->sn", later_low, weighted, preferred_element_type=jnp.float32)
    grad_heads = grad_heads + grad_weighted * carry_weight[:, :, None]
    grad_carry = jnp.sum(grad_weighted * heads_float, axis=2)
    grad_last = jnp.sum(later * state, axis=(1, 2))
    grad_scores = jnp.sum(grad_mixing * factor, axis=0).astype(jnp.bfloat16)
    grad_query = grad_query + jnp.dot(grad_scores, keys_blk, preferred_element_type=jnp.float32)
    grad_keys = grad_keys + jnp.einsum(
        "ts,tn->sn", grad_scores, query_blk, preferred_element_type=jnp.float32
    )
    grad_log, grad_step = decay_pull(
        (grad_mixing * scores[None], grad_carry, grad_growth, grad_last)
    )
    return (grad_state, (grad_heads, grad_keys, grad_query, grad_step, grad_log))


def forward_seq(
    tok_float,
    keep,
    norm_full,
    in_full,
    conv_full,
    shift_full,
    gate_full,
    out_full,
    step_bias,
    decay_log,
    skip_gain,
):
    seq_len = tok_float.shape[0]
    normed, norm_pull = jax.vjp(norm_part, tok_float, norm_full.astype(jnp.float32))
    normed_low = normed.astype(jnp.bfloat16)
    projected = jnp.dot(normed_low, in_full, preferred_element_type=jnp.float32)
    gate_raw = projected[:, :DI]
    conv_in = projected[:, DI : DI + XBC]
    step_raw = projected[:, DI + XBC :]
    convolved, conv_pull = jax.vjp(
        conv_part, conv_in, conv_full.astype(jnp.float32), shift_full.astype(jnp.float32)
    )
    heads_in = convolved[:, :DI]
    heads_low = heads_in.astype(jnp.bfloat16)
    key_low = convolved[:, DI : DI + STATE].astype(jnp.bfloat16)
    query_low = convolved[:, DI + STATE :].astype(jnp.bfloat16)
    decays, step_pull = jax.vjp(step_part, step_raw, step_bias, decay_log)
    step_size, log_decay = decays
    count = seq_len // SPAN
    blocks = (
        heads_low.reshape(count, SPAN, HEADS, HEADDIM),
        key_low.reshape(count, SPAN, STATE),
        query_low.reshape(count, SPAN, STATE),
        step_size.reshape(count, SPAN, HEADS),
        log_decay.reshape(count, SPAN, HEADS),
    )
    start = jnp.zeros((HEADS, HEADDIM, STATE), jnp.float32)
    final_state, kept = lax.scan(block_forward, start, blocks)
    scan_blocks, states = kept
    scan_out = scan_blocks.reshape(seq_len, DI)
    gate_value, gate_pull = jax.vjp(
        gate_part, scan_out, heads_in, skip_gain, gate_raw, gate_full.astype(jnp.float32)
    )
    gate_low = gate_value.astype(jnp.bfloat16)
    branch = jnp.dot(gate_low, out_full, preferred_element_type=jnp.float32)
    result = (tok_float + keep[:, None] * branch).astype(jnp.bfloat16)
    saved = (keep, normed_low, norm_pull, conv_pull, step_pull, gate_pull, gate_low, blocks, states)
    return (result, saved)


def backward_seq(saved, cot_float, in_full, out_full):
    keep, normed_low, norm_pull, conv_pull, step_pull, gate_pull, gate_low, blocks, states = saved
    seq_len = cot_float.shape[0]
    count = seq_len // SPAN
    grad_branch = (keep[:, None] * cot_float).astype(jnp.bfloat16)
    grad_out_full = jnp.einsum(
        "ti,tj->ij", gate_low, grad_branch, preferred_element_type=jnp.float32
    )
    grad_gate = jnp.einsum("tj,ij->ti", grad_branch, out_full, preferred_element_type=jnp.float32)
    grad_scan, grad_heads_skip, grad_skip, grad_gate_raw, grad_gate_gain = gate_pull(grad_gate)
    grad_scan_blocks = grad_scan.reshape(count, SPAN, HEADS, HEADDIM)
    first_grad, grads = lax.scan(
        block_backward,
        jnp.zeros((HEADS, HEADDIM, STATE), jnp.float32),
        (blocks[0], blocks[1], blocks[2], blocks[3], blocks[4], grad_scan_blocks, states),
        reverse=True,
    )
    grad_heads, grad_keys, grad_query, grad_step, grad_log = grads
    grad_step_raw, grad_step_bias, grad_decay_log = step_pull(
        (grad_step.reshape(seq_len, HEADS), grad_log.reshape(seq_len, HEADS))
    )
    grad_convolved = jnp.concatenate(
        [
            grad_heads.reshape(seq_len, DI) + grad_heads_skip,
            grad_keys.reshape(seq_len, STATE),
            grad_query.reshape(seq_len, STATE),
        ],
        axis=1,
    )
    grad_conv_in, grad_taps, grad_shift = conv_pull(grad_convolved)
    grad_projected = jnp.concatenate([grad_gate_raw, grad_conv_in, grad_step_raw], axis=1).astype(
        jnp.bfloat16
    )
    grad_in_full = jnp.einsum(
        "ti,tj->ij", normed_low, grad_projected, preferred_element_type=jnp.float32
    )
    grad_normed = jnp.einsum(
        "tj,ij->ti", grad_projected, in_full, preferred_element_type=jnp.float32
    )
    grad_tok, grad_norm_gain = norm_pull(grad_normed)
    input_grad = (cot_float + grad_tok).astype(jnp.bfloat16)
    weight_grads = (
        grad_norm_gain,
        grad_in_full,
        grad_taps,
        grad_shift,
        grad_gate_gain,
        grad_out_full,
    )
    return (input_grad, weight_grads, (grad_step_bias, grad_decay_log, grad_skip))


def on_device(
    tokens,
    cotangent,
    lengths,
    order,
    norm_weight,
    in_weight,
    conv_weight,
    conv_bias,
    step_bias,
    decay_log,
    skip_gain,
    gate_norm_weight,
    out_weight,
):
    peers = lax.axis_size("shard")
    rank = lax.axis_index("shard")
    slots = jnp.arange(peers, dtype=jnp.int32)
    order_row = order[0]
    inverse = jnp.sum(jnp.where(order_row[None, :] == slots[:, None], slots[None, :], 0), axis=1)
    piece = tokens.shape[1]
    width = tokens.shape[2]
    sent_tokens = jnp.take(tokens, inverse, axis=0).reshape(peers, 1, piece, width)
    sent_cot = jnp.take(cotangent, inverse, axis=0).reshape(peers, 1, piece, width)
    got_tokens, got_cot = (
        lax.all_to_all(sent_tokens, "shard", split_axis=0, concat_axis=2, tiled=True),
        lax.all_to_all(sent_cot, "shard", split_axis=0, concat_axis=2, tiled=True),
    )
    seq_len = got_tokens.shape[2]
    length_row = lengths[0]
    gathered = (
        lax.all_gather(norm_weight, "shard", axis=0, tiled=True),
        lax.all_gather(in_weight, "shard", axis=0, tiled=True),
        lax.all_gather(conv_weight, "shard", axis=0, tiled=True),
        lax.all_gather(conv_bias, "shard", axis=0, tiled=True),
        lax.all_gather(gate_norm_weight, "shard", axis=0, tiled=True),
        lax.all_gather(out_weight, "shard", axis=0, tiled=True),
    )
    norm_full, in_full, conv_full, shift_full, gate_full, out_full = gathered
    valid = length_row[rank]
    keep = (jnp.arange(seq_len, dtype=jnp.int32) < valid).astype(jnp.float32)
    forward_out, saved = forward_seq(
        got_tokens[0, 0].astype(jnp.float32),
        keep,
        norm_full,
        in_full,
        conv_full,
        shift_full,
        gate_full,
        out_full,
        step_bias,
        decay_log,
        skip_gain,
    )
    result = forward_out[None]
    grad_seq, weight_grads, head_terms = backward_seq(
        saved, got_cot[0, 0].astype(jnp.float32), in_full, out_full
    )
    input_grad = grad_seq[None]
    back_out, back_grad = (
        lax.all_to_all(result, "shard", split_axis=1, concat_axis=0, tiled=True),
        lax.all_to_all(input_grad, "shard", split_axis=1, concat_axis=0, tiled=True),
    )
    output = jnp.take(back_out, order_row, axis=0)
    input_back = jnp.take(back_grad, order_row, axis=0)
    summed = lax.psum(
        (
            weight_grads[0],
            weight_grads[1],
            weight_grads[2],
            weight_grads[3],
            weight_grads[4],
            weight_grads[5],
        ),
        "rep",
    )
    pieces = (
        lax.psum_scatter(summed[0], "shard", scatter_dimension=0, tiled=True),
        lax.psum_scatter(summed[1], "shard", scatter_dimension=0, tiled=True),
        lax.psum_scatter(summed[2], "shard", scatter_dimension=0, tiled=True),
        lax.psum_scatter(summed[3], "shard", scatter_dimension=0, tiled=True),
        lax.psum_scatter(summed[4], "shard", scatter_dimension=0, tiled=True),
        lax.psum_scatter(summed[5], "shard", scatter_dimension=0, tiled=True),
    )
    head_sums = lax.psum((head_terms[0], head_terms[1], head_terms[2]), ("rep", "shard"))
    return (
        output,
        input_back,
        pieces[0],
        pieces[1],
        pieces[2],
        pieces[3],
        head_sums[0],
        head_sums[1],
        head_sums[2],
        pieces[4],
        pieces[5],
    )


def solution(mesh):
    placed = (
        P("rep", "shard", None),
        P("rep", "shard", None),
        P("rep", None),
        P("rep", None),
        P("shard"),
        P("shard", None),
        P("shard", None),
        P("shard"),
        P(),
        P(),
        P(),
        P("shard"),
        P("shard", None),
    )
    return jax.shard_map(
        on_device,
        mesh=mesh,
        in_specs=placed,
        out_specs=(
            P("rep", "shard", None),
            P("rep", "shard", None),
            P("shard"),
            P("shard", None),
            P("shard", None),
            P("shard"),
            P(),
            P(),
            P(),
            P("shard"),
            P("shard", None),
        ),
        check_vma=False,
    )
```

profile of v0, /device:TPU:0, one launch (start us, length us, event | category | flops | bytes accessed | tf_op | source)
XLA Modules:
  0.0 1287.2 jit_solution(3603219273039151114)
XLA Ops:
  15.6 65.5 %all_to_all.42 = bf16[16,1,64,768]{3,2,1,0:T(8,128)(2,1)S(1)} all-to-all(bf16[16,1,64,768]{3,2,1,0:T(8,128)(2,1)S(1)} %get-tuple-element.698), channel_id=1, replica_groups=mesh['rep'=2,'shard'=16] {'shard'}, dimensions={0} | all-to-all | bytes 3145728 | tf_op jit(solution)/shard_map/all_to_all | solution.py:245
  81.1 4.5 all-to-all-start.2
  89.8 115.9 %all-reduce.21 = (bf16[768]{0:T(1024)(128)(2,1)S(1)}, bf16[1792]{0:T(1024)(128)(2,1)S(1)}, bf16[1536]{0:T(1024)(128)(2,1)S(1)}) all-reduce(bf16[768]{0:T(1024)(128)(2,1)S(1)} %dynamic-update-slice, bf16[1792]{0:T(1024)(128)(2,1)S(1)} %dynamic-update-slice.1, ...), channel_id=1, replica_groups=mesh['rep'=2,'shard'=16] {'shard'}, use_global_device_ids=true, to_apply=%add.11 | all-reduce | flops 4096 | bytes 16384
  205.8 36.0 %all-gather = bf16[16,112,4]{1,2,0:T(4,128)(2,1)S(1)} all-gather(bf16[1,112,4]{1,2,0:T(4,128)(2,1)S(1)} %bitcast.455), channel_id=1, replica_groups=mesh['rep'=2,'shard'=16] {'shard'}, dimensions={0}, use_global_device_ids=true | all-gather | bytes 15232 | tf_op jit(solution)/shard_map/all_gather | solution.py:253
  248.4 11.4 fusion.140
  259.8 3.8 slice.133
  263.7 10.1 fusion.136
  278.8 6.2 reshape.413
  285.0 4.1 copy.211
  293.5 4.0 broadcast.186.clone2
  297.5 182.0 %while.40 = (s32[]{:T(128)}, f32[24,64,128]{2,1,0:T(8,128)S(1)}, f32[4,256,24,64]{1,0,3,2:T(4,128)}, f32[4,24,64,128]{3,2,1,0:T(8,128)}, f32[4,256,24]{1,2,0:T(8...) while((s32[]{:T(128)}, f32[24,64,128]{2,1,0:T(8,128)S(1)}, ...), condition=%wide.region_5.7_spmd.clone, body=%wide.region_2.0_spmd.clone.sunk | while | flops 432687168 | bytes 17880888 | solution.py:155
  301.0 3.4 fusion.191
  306.0 34.5 %dynamic_update_slice.73 = f32[4,256,24,64]{1,0,3,2:T(4,128)} dynamic-update-slice(f32[4,256,24,64]{1,0,3,2:T(4,128)} %get-tuple-element.896, f32[1,256,24,64]{1,0,3,2:T(1,128)S(1)} %copy.355, s32[]{:T(128)} %get-tuple-element.894, s32[]{:T(128)} %constant.126.clone.1..sunk, s32[]{:T(128)} %constant.126.clone.1..sunk, s32[]{:T(128)} %constant.126.clone.1..sunk) | dynamic-update-slice | bytes 3145732 | tf_op jit(solution)/shard_map/while/body/jit(dynamic_update_index_in_dim)/dynamic_update_slice | solution.py:155
  346.5 3.4 fusion.191
  351.5 34.5 %dynamic_update_slice.73 = f32[4,256,24,64]{1,0,3,2:T(4,128)} dynamic-update-slice(f32[4,256,24,64]{1,0,3,2:T(4,128)} %get-tuple-element.896, f32[1,256,24,64]{1,0,3,2:T(1,128)S(1)} %copy.355, s32[]{:T(128)} %get-tuple-element.894, s32[]{:T(128)} %constant.126.clone.1..sunk, s32[]{:T(128)} %constant.126.clone.1..sunk, s32[]{:T(128)} %constant.126.clone.1..sunk) | dynamic-update-slice | bytes 3145732 | tf_op jit(solution)/shard_map/while/body/jit(dynamic_update_index_in_dim)/dynamic_update_slice | solution.py:155
  391.9 3.4 fusion.191
  396.9 34.5 %dynamic_update_slice.73 = f32[4,256,24,64]{1,0,3,2:T(4,128)} dynamic-update-slice(f32[4,256,24,64]{1,0,3,2:T(4,128)} %get-tuple-element.896, f32[1,256,24,64]{1,0,3,2:T(1,128)S(1)} %copy.355, s32[]{:T(128)} %get-tuple-element.894, s32[]{:T(128)} %constant.126.clone.1..sunk, s32[]{:T(128)} %constant.126.clone.1..sunk, s32[]{:T(128)} %constant.126.clone.1..sunk) | dynamic-update-slice | bytes 3145732 | tf_op jit(solution)/shard_map/while/body/jit(dynamic_update_index_in_dim)/dynamic_update_slice | solution.py:155
  437.4 3.4 fusion.191
  442.4 34.5 %dynamic_update_slice.73 = f32[4,256,24,64]{1,0,3,2:T(4,128)} dynamic-update-slice(f32[4,256,24,64]{1,0,3,2:T(4,128)} %get-tuple-element.896, f32[1,256,24,64]{1,0,3,2:T(1,128)S(1)} %copy.355, s32[]{:T(128)} %get-tuple-element.894, s32[]{:T(128)} %constant.126.clone.1..sunk, s32[]{:T(128)} %constant.126.clone.1..sunk, s32[]{:T(128)} %constant.126.clone.1..sunk) | dynamic-update-slice | bytes 3145732 | tf_op jit(solution)/shard_map/while/body/jit(dynamic_update_index_in_dim)/dynamic_update_slice | solution.py:155
  479.5 4.3 copy.281
  483.9 8.3 multiply_reduce_fusion.9
  494.8 4.6 fusion.130
  499.4 7.8 multiply_reduce_fusion.6
  507.2 14.2 %multiply_reduce_fusion.7 = (f32[1536]{0:T(1024)}, f32[1024,1536]{0,1:T(8,128)}, bf16[1024,1536]{0,1:T(8,128)(2,1)}) fusion(f32[1024,1792]{0,1:T(8,128)} %copy-done.2, f32[1024,3352]{0,1:T(8,128)} %fusion.140, f32[1024,1536]{0,1:T(8,128)S(1)} %copy-done.8, f32[1024]{0:T(1024)S(1)} %multiply_multiply_fusion.1, f32[1024]{0:T(1024)S(1)} %fusion.127, ...), kind=kLoop, calls=%fused_computation.179 | loop fusion | flops 34601472 | bytes 40921088 | tf_op jit(solution)/shard_map/transpose(jvp())/reduce_sum | solution.py:54
  521.3 8.1 reshape.419
  529.5 4.1 broadcast.186.clone
  536.5 292.6 %while.41 = (s32[]{:T(128)}, f32[24,64,128]{2,1,0:T(8,128)S(1)}, f32[4,256,24,64]{1,0,3,2:T(4,128)}, f32[4,256,128]{2,1,0:T(8,128)}, f32[4,256,128]{2,1,0:T(8,12...) while((s32[]{:T(128)}, f32[24,64,128]{2,1,0:T(8,128)S(1)}, ...), condition=%wide.region_21.23_spmd.clone, body=%wide.region_8.22_spmd.clone.sunk | while | flops 998139968 | bytes 33770432 | solution.py:179
  539.2 4.5 constant_dynamic-slice_fusion.3
  543.7 6.0 fusion.207
  556.1 3.8 fusion.212
  562.7 34.8 %dynamic_update_slice.76 = f32[4,256,24,64]{1,0,3,2:T(4,128)} dynamic-update-slice(f32[4,256,24,64]{1,0,3,2:T(4,128)} %get-tuple-element.938, f32[1,256,24,64]{1,0,3,2:T(1,128)} %copy.368, s32[]{:T(128)S(6)} %sub.232, s32[]{:T(128)} %constant.126.clone.1..sunk.1, s32[]{:T(128)} %constant.126.clone.1..sunk.1, s32[]{:T(128)} %constant.126.clone.1..sunk.1) | dynamic-update-slice | bytes 3145732 | tf_op jit(solution)/shard_map/while/body/jit(dynamic_update_index_in_dim)/dynamic_update_slice | solution.py:155
  612.3 4.5 constant_dynamic-slice_fusion.3
  616.9 6.0 fusion.207
  629.2 3.7 fusion.212
  635.8 34.7 %dynamic_update_slice.76 = f32[4,256,24,64]{1,0,3,2:T(4,128)} dynamic-update-slice(f32[4,256,24,64]{1,0,3,2:T(4,128)} %get-tuple-element.938, f32[1,256,24,64]{1,0,3,2:T(1,128)} %copy.368, s32[]{:T(128)S(6)} %sub.232, s32[]{:T(128)} %constant.126.clone.1..sunk.1, s32[]{:T(128)} %constant.126.clone.1..sunk.1, s32[]{:T(128)} %constant.126.clone.1..sunk.1) | dynamic-update-slice | bytes 3145732 | tf_op jit(solution)/shard_map/while/body/jit(dynamic_update_index_in_dim)/dynamic_update_slice | solution.py:155
  685.4 4.5 constant_dynamic-slice_fusion.3
  689.9 6.0 fusion.207
  702.2 3.7 fusion.212
  708.9 34.7 %dynamic_update_slice.76 = f32[4,256,24,64]{1,0,3,2:T(4,128)} dynamic-update-slice(f32[4,256,24,64]{1,0,3,2:T(4,128)} %get-tuple-element.938, f32[1,256,24,64]{1,0,3,2:T(1,128)} %copy.368, s32[]{:T(128)S(6)} %sub.232, s32[]{:T(128)} %constant.126.clone.1..sunk.1, s32[]{:T(128)} %constant.126.clone.1..sunk.1, s32[]{:T(128)} %constant.126.clone.1..sunk.1) | dynamic-update-slice | bytes 3145732 | tf_op jit(solution)/shard_map/while/body/jit(dynamic_update_index_in_dim)/dynamic_update_slice | solution.py:155
  758.4 4.5 constant_dynamic-slice_fusion.3
  762.9 6.0 fusion.207
  775.2 3.7 fusion.212
  781.8 34.7 %dynamic_update_slice.76 = f32[4,256,24,64]{1,0,3,2:T(4,128)} dynamic-update-slice(f32[4,256,24,64]{1,0,3,2:T(4,128)} %get-tuple-element.938, f32[1,256,24,64]{1,0,3,2:T(1,128)} %copy.368, s32[]{:T(128)S(6)} %sub.232, s32[]{:T(128)} %constant.126.clone.1..sunk.1, s32[]{:T(128)} %constant.126.clone.1..sunk.1, s32[]{:T(128)} %constant.126.clone.1..sunk.1) | dynamic-update-slice | bytes 3145732 | tf_op jit(solution)/shard_map/while/body/jit(dynamic_update_index_in_dim)/dynamic_update_slice | solution.py:155
  831.0 7.0 copy.282
  839.6 5.3 multiply_add_fusion.1
  845.0 19.0 %multiply_reduce_fusion.4 = (f32[1792]{0:T(1024)S(1)}, f32[1792]{0:T(1024)S(1)}, f32[1792]{0:T(1024)S(1)}, f32[1792]{0:T(1024)S(1)}, f32[1792]{0:T(1024)S(1)}, /*index=5*/f32[1024,1792]{0,1:T(8,128)S(1)}) fusion(f32[1024,1792]{0,1:T(8,128)} %copy-done.3, f32[1024,3352]{0,1:T(8,128)} %fusion.140, f32[1024,1792]{0,1:T(8,128)} %get-tuple-element.668, ...), kind=kLoop, calls=%fused_computation.169 | loop fusion | flops 36691200 | bytes 36736000 | tf_op jit(solution)/shard_map/transpose(jvp())/reduce_sum | solution.py:44
  864.0 8.5 broadcast_multiply_fusion
  872.5 12.1 fusion.103
  884.6 12.9 %fusion.119 = f32[768,3352]{1,0:T(8,128)} fusion(bf16[1024,768]{1,0:T(8,128)(2,1)S(1)} %copy-done.11, bf16[1024,24]{0,1:T(8,128)(2,1)S(1)} %get-tuple-element.662, bf16[1024,1792]{0,1:T(8,128)(2,1)} %fusion.103, bf16[1024,1536]{0,1:T(8,128)(2,1)} %get-tuple-element.685), kind=kOutput, calls=%fused_computation.210 | convolution fusion | flops 5292834816 | bytes 18735104 | tf_op jit(solution)/shard_map/ti,tj->ij/dot_general | solution.py:201
  898.9 6.4 fusion.121
  905.3 4.1 copy.331
  909.9 11.5 reduce.22
  922.8 3.7 all-to-all-start.1
  926.5 10.9 fusion.114
  939.8 4.2 copy.330
  944.0 11.5 reduce.21
  956.8 19.5 %all-to-all-done.1 = bf16[16,2,24576]{2,1,0:T(2,128)(2,1)S(1)} async-done(((bf16[16,2,24576]{2,1,0:T(2,128)(2,1)}), bf16[16,2,24576]{2,1,0:T(2,128)(2,1)S(1)}, u32[]{:S(2)}, u32[]{:S(2)}) %all-to-all-start.1) | async-done | bytes 1572896 | tf_op jit(solution)/shard_map/all_to_all | solution.py:280
  976.3 28.2 %all-to-all-start.3 = ((bf16[16,2,24576]{2,1,0:T(2,128)(2,1)}), bf16[16,2,24576]{2,1,0:T(2,128)(2,1)S(1)}, u32[]{:S(2)}, u32[]{:S(2)}) async-start(bf16[16,2,24576]{2,1,0:T(2,128)(2,1)} %reshape.519), calls=%async_computation.3 | async-start | bytes 3145728 | tf_op jit(solution)/shard_map/all_to_all | solution.py:281
  1008.0 123.2 %reduce-scatter.6.cloned.1.call-done = f32[48,3352]{1,0:T(8,128)} async-done(((f32[768,3352]{1,0:T(8,128)}), f32[48,3352]{1,0:T(8,128)}) %reduce-scatter.6.cloned.1.call-update) | async-done | bytes 643600 | tf_op jit(solution)/shard_map/reduce_scatter | solution.py:298
  1131.4 40.0 %all-reduce.17 = (f32[24]{0:T(128)}, f32[24]{0:T(128)}, f32[24]{0:T(128)}) all-reduce(f32[24]{0:T(128)S(1)} %get-tuple-element.661, f32[24]{0:T(128)S(1)} %negate_multiply_fusion, f32[24]{0:T(128)S(1)} %reduce_sum.344), channel_id=1, replica_groups=mesh['rep'=2,'shard'=16] {'rep','shard'}, use_global_device_ids=true, to_apply=%region_38.40 | all-reduce | flops 72 | bytes 576 | tf_op jit(solution)/shard_map/psum | solution.py:304
  1171.4 75.7 %all-reduce.18 = (f32[768]{0:T(1024)S(1)}, f32[1792]{0:T(1024)S(1)}, f32[1536]{0:T(1024)S(1)}) all-reduce(f32[768]{0:T(1024)S(1)} %get-tuple-element.592, f32[1792]{0:T(1024)S(1)} %get-tuple-element.590, f32[1536]{0:T(1024)S(1)} %copy-done.36), channel_id=2, replica_groups=mesh['rep'=2,'shard'=16] {'shard'}, use_global_device_ids=true, to_apply=%region_25.27.clone | all-reduce | flops 4096 | bytes 32768
  1251.3 6.3 reshape.518
  1259.7 6.3 reshape.520
  1273.1 3.4 broadcast_select_fusion
  (400 shorter events, 186.9 us)
Async XLA Ops:
  7.2 1.5 copy-start
  7.2 241.2 %all-gather.4.cloned.1.call-start = ((), (), s32[]{:S(2)}) async-start(), calls=%async_computation.7 | async-start | bytes 5640192 | tf_op jit(solution)/shard_map/all_gather | solution.py:252
  12.6 73.9 %copy-start.41 = (u32[32]{0:T(128)S(1)}, u32[32]{0:T(128)}, u32[]{:S(2)}) copy-start(u32[32]{0:T(128)} %constant.162) | copy-start | bytes 388
  12.6 76.5 %copy-start.44 = (bf16[112]{0:T(256)(128)(2,1)S(1)}, bf16[112]{0:T(256)(128)(2,1)}, u32[]{:S(2)}) copy-start(bf16[112]{0:T(256)(128)(2,1)} %param.26) | copy-start | bytes 676
  12.6 76.7 %copy-start.45 = (bf16[96]{0:T(256)(128)(2,1)S(1)}, bf16[96]{0:T(256)(128)(2,1)}, u32[]{:S(2)}) copy-start(bf16[96]{0:T(256)(128)(2,1)} %param.30) | copy-start | bytes 580
  12.6 77.0 %copy-start.46 = (bf16[48]{0:T(256)(128)(2,1)S(1)}, bf16[48]{0:T(256)(128)(2,1)}, u32[]{:S(2)}) copy-start(bf16[48]{0:T(256)(128)(2,1)} %param.23) | copy-start | bytes 292
  12.6 193.1 %copy-start.42 = (bf16[112,4]{0,1:T(4,128)(2,1)S(1)}, bf16[112,4]{0,1:T(4,128)(2,1)}, u32[]{:S(2)}) copy-start(bf16[112,4]{0,1:T(4,128)(2,1)} %param.25) | copy-start | bytes 2692
  12.6 229.2 %copy-start.43 = (f32[24]{0:T(128)S(1)}, f32[24]{0:T(128)}, u32[]{:S(2)}) copy-start(f32[24]{0:T(128)} %param.29) | copy-start | bytes 292
  12.7 229.4 %copy-start.47 = (s32[1,16]{1,0:T(1,128)S(1)}, s32[1,16]{1,0:T(1,128)}, u32[]{:S(2)}) copy-start(s32[1,16]{1,0:T(1,128)} %param.21) | copy-start | bytes 196
  12.7 230.7 %copy-start.49 = (f32[24]{0:T(128)S(1)}, f32[24]{0:T(128)}, u32[]{:S(2)}) copy-start(f32[24]{0:T(128)} %param.28) | copy-start | bytes 292
  81.1 178.7 %copy-start.5 = (bf16[16,1,64,768]{3,2,1,0:T(8,128)(2,1)}, bf16[16,1,64,768]{3,2,1,0:T(8,128)(2,1)S(1)}, u32[]{:S(2)}) copy-start(bf16[16,1,64,768]{3,2,1,0:T(8,128)(2,1)S(1)} %all_to_all.42) | copy-start | bytes 4718596
  81.1 164.4 %all-to-all-start.2 = ((bf16[16,1,64,768]{3,2,1,0:T(8,128)(2,1)}), bf16[16,1,64,768]{3,2,1,0:T(8,128)(2,1)}, u32[]{:S(2)}, u32[]{:S(2)}) async-start(bf16[16,1,64,768]{3,2,1,0:T(8,128)(2,1)} %get-tuple-element.697), calls=%async_computation.2 | async-start | bytes 3145728 | tf_op jit(solution)/shard_map/all_to_all | solution.py:246
  85.6 413.7 %all-gather.6.cloned.1.call-start = ((), (), s32[]{:S(2)}) async-start(), calls=%async_computation.8 | async-start | bytes 2506752 | tf_op jit(solution)/shard_map/all_gather | solution.py:256
  86.4 921.6 %reduce-scatter.8.cloned.1.call-start = ((), (), s32[]{:S(2)}) async-start(), calls=%async_computation.10 | async-start | bytes 5013504 | tf_op jit(solution)/shard_map/reduce_scatter | solution.py:302
  205.8 54.0 %copy-start.23 = (f32[768]{0:T(1024)}, f32[768]{0:T(1024)S(1)}, u32[]{:S(2)}) copy-start(f32[768]{0:T(1024)S(1)} %convert_element_type.160) | copy-start | bytes 9220
  242.0 265.1 %copy-start.29 = (f32[1536]{0:T(1024)}, f32[1536]{0:T(1024)S(1)}, u32[]{:S(2)}) copy-start(f32[1536]{0:T(1024)S(1)} %convert_element_type.165) | copy-start | bytes 18436
  243.3 16.5 %copy-start.32 = (f32[1024]{0:T(1024)}, f32[1024]{0:T(1024)S(1)}, u32[]{:S(2)}) copy-start(f32[1024]{0:T(1024)S(1)} %fusion.126) | copy-start | bytes 12292
  243.4 20.2 %copy-start.15 = (f32[1792]{0:T(1024)}, f32[1792]{0:T(1024)S(1)}, u32[]{:S(2)}) copy-start(f32[1792]{0:T(1024)S(1)} %get-tuple-element.594) | copy-start | bytes 21508
  243.4 20.2 %copy-start.17 = (f32[1792]{0:T(1024)}, f32[1792]{0:T(1024)S(1)}, u32[]{:S(2)}) copy-start(f32[1792]{0:T(1024)S(1)} %get-tuple-element.595) | copy-start | bytes 21508
  243.4 20.2 %copy-start.19 = (f32[1792]{0:T(1024)}, f32[1792]{0:T(1024)S(1)}, u32[]{:S(2)}) copy-start(f32[1792]{0:T(1024)S(1)} %get-tuple-element.596) | copy-start | bytes 21508
  243.4 20.2 %copy-start.21 = (f32[1792]{0:T(1024)}, f32[1792]{0:T(1024)S(1)}, u32[]{:S(2)}) copy-start(f32[1792]{0:T(1024)S(1)} %get-tuple-element.597) | copy-start | bytes 21508
  243.4 47.7 %copy-start.39 = (f32[24]{0:T(128)}, f32[24]{0:T(128)S(1)}, u32[]{:S(2)}) copy-start(f32[24]{0:T(128)S(1)} %exponential_negate_fusion) | copy-start | bytes 292
  243.9 15.9 %copy-start.27 = (f32[1024]{0:T(1024)}, f32[1024]{0:T(1024)S(1)}, u32[]{:S(2)}) copy-start(f32[1024]{0:T(1024)S(1)} %add.193) | copy-start | bytes 12292
  243.9 15.9 %copy-start.25 = (f32[1024]{0:T(1024)}, f32[1024]{0:T(1024)S(1)}, u32[]{:S(2)}) copy-start(f32[1024]{0:T(1024)S(1)} %rsqrt.20) | copy-start | bytes 12292
  263.6 10.1 copy-start.3
  273.7 2.9 copy-start.2
  278.8 12.4 copy-start.37
  292.2 0.6 copy-start.13
  483.9 8.3 copy-start.4
  483.9 10.9 copy-start.12
  492.2 2.6 copy-start.7
  492.2 14.9 %copy-start.34 = (f32[1024]{0:T(1024)}, f32[1024]{0:T(1024)S(1)}, u32[]{:S(2)}) copy-start(f32[1024]{0:T(1024)S(1)} %fusion.127) | copy-start | bytes 12292
  499.4 7.8 copy-start.8
  529.4 601.7 %reduce-scatter.6.cloned.1.call-start = ((), (), s32[]{:S(2)}) async-start(), calls=%async_computation.9 | async-start | bytes 11280384 | tf_op jit(solution)/shard_map/reduce_scatter | solution.py:298
  831.0 7.1 copy-start.9
  831.0 7.3 copy-start.10
  831.0 7.5 copy-start.14
  831.0 7.5 copy-start.38
  831.0 7.5 copy-start.40
  844.9 19.0 %copy-start.16 = (f32[1792]{0:T(1024)S(1)}, f32[1792]{0:T(1024)}, u32[]{:S(2)}) copy-start(f32[1792]{0:T(1024)} %copy-done.15) | copy-start | bytes 21508
  844.9 19.0 %copy-start.18 = (f32[1792]{0:T(1024)S(1)}, f32[1792]{0:T(1024)}, u32[]{:S(2)}) copy-start(f32[1792]{0:T(1024)} %copy-done.17) | copy-start | bytes 21508
  844.9 19.0 %copy-start.20 = (f32[1792]{0:T(1024)S(1)}, f32[1792]{0:T(1024)}, u32[]{:S(2)}) copy-start(f32[1792]{0:T(1024)} %copy-done.19) | copy-start | bytes 21508
  844.9 19.0 %copy-start.22 = (f32[1792]{0:T(1024)S(1)}, f32[1792]{0:T(1024)}, u32[]{:S(2)}) copy-start(f32[1792]{0:T(1024)} %copy-done.21) | copy-start | bytes 21508
  872.5 12.1 copy-start.11
  897.5 1.4 copy-start.6
  897.5 1.4 copy-start.30
  897.5 1.4 copy-start.33
  897.5 1.4 copy-start.35
  909.4 17.0 %copy-start.24 = (f32[768]{0:T(1024)S(1)}, f32[768]{0:T(1024)}, u32[]{:S(2)}) copy-start(f32[768]{0:T(1024)} %copy-done.23) | copy-start | bytes 9220
  909.4 17.1 %copy-start.26 = (f32[1024]{0:T(1024)S(1)}, f32[1024]{0:T(1024)}, u32[]{:S(2)}) copy-start(f32[1024]{0:T(1024)} %copy-done.25) | copy-start | bytes 12292
  922.8 53.6 %all-to-all-start.1 = ((bf16[16,2,24576]{2,1,0:T(2,128)(2,1)}), bf16[16,2,24576]{2,1,0:T(2,128)(2,1)S(1)}, u32[]{:S(2)}, u32[]{:S(2)}) async-start(bf16[16,2,24576]{2,1,0:T(2,128)(2,1)} %reshape.517), calls=%async_computation.1 | async-start | bytes 3145728 | tf_op jit(solution)/shard_map/all_to_all | solution.py:280
  926.5 10.9 copy-start.28
  944.0 62.0 %copy-start.48 = (s32[1,16]{1,0:T(1,128)S(1)}, s32[1,16]{1,0:T(1,128)}, u32[]{:S(2)}) copy-start(s32[1,16]{1,0:T(1,128)} %param.22) | copy-start | bytes 196
  944.0 187.2 %copy-start.31 = (f32[1536]{0:T(1024)S(1)}, f32[1536]{0:T(1024)}, u32[]{:S(2)}) copy-start(f32[1536]{0:T(1024)} %get-tuple-element.659) | copy-start | bytes 18436
  944.0 187.4 %copy-start.50 = (f32[24]{0:T(128)S(1)}, f32[24]{0:T(128)}, u32[]{:S(2)}) copy-start(f32[24]{0:T(128)} %param.28) | copy-start | bytes 292
  944.0 227.4 %copy-start.36 = (f32[1536]{0:T(1024)S(1)}, f32[1536]{0:T(1024)}, u32[]{:S(2)}) copy-start(f32[1536]{0:T(1024)} %get-tuple-element.588) | copy-start | bytes 18436
  976.3 283.4 %all-to-all-start.3 = ((bf16[16,2,24576]{2,1,0:T(2,128)(2,1)}), bf16[16,2,24576]{2,1,0:T(2,128)(2,1)S(1)}, u32[]{:S(2)}, u32[]{:S(2)}) async-start(bf16[16,2,24576]{2,1,0:T(2,128)(2,1)} %reshape.519), calls=%async_computation.3 | async-start | bytes 3145728 | tf_op jit(solution)/shard_map/all_to_all | solution.py:281
  1004.5 242.9 %reduce-scatter.10.cloned.1.call-start = ((), (), s32[]{:S(2)}) async-start(), calls=%async_computation.11 | async-start | bytes 974848
  1005.9 270.6 %all-reduce.24.cloned.1.call-start = ((), (), s32[]{:S(2)}) async-start(), calls=%async_computation.12 | async-start | bytes 1916928 | tf_op jit(solution)/shard_map/psum | solution.py:285
  1269.2 10.9 copy-start.1
Sparse Core Ops, SparseCore 0:
  10.8 132.4 all-gather.3
  146.1 62.0 all-gather.5
  529.5 135.6 reduce-scatter.7
  897.7 233.4 reduce-scatter.5
  1133.8 76.8 reduce-scatter.9
  1213.1 16.0 all-reduce.23
where the time goes:
time: 1300 us; the launch traced here: 1290 us
  local copies, waits for them, and re-layouts  440 us (34%)
  blocking collectives  336 us (26%)
  matrix products  164 us (13%)
  other arithmetic  146 us (11%)
  waiting for transfers between devices  144 us (11%)
  starting transfers between devices  36.6 us (3%)
  between operations  19.1 us (1%)
    dynamic_update_slice x16, local copies, waits for them, and re-layouts, forward_seq(): final_state, kept = lax.scan(block_forward, start, blocks)  295 us
    unnamed x2, blocking collectives  192 us
    reduce_scatter x1, waiting for transfers between devices, on_device(): lax.psum_scatter(summed[1], 'shard', scatter_dimension=0, tiled=True)  123 us
    all_to_all x1, blocking collectives, on_device(): lax.all_to_all(sent_tokens, 'shard', split_axis=0, concat_axis=2, tiled=T...  65.5 us
    unnamed x131, local copies, waits for them, and re-layouts  55.2 us
    psum x1, blocking collectives, on_device(): lax.psum((head_terms[0], head_terms[1], head_terms[2]), ('rep', 'shard'))  40 us
    another operation x34, other arithmetic  37.7 us
    all_gather x1, blocking collectives, on_device(): lax.all_gather(conv_weight, 'shard', axis=0, tiled=True)  36 us
  transfers between devices with their start and end apart: 9, of which 2 were waited for; matrix products, arithmetic and copies ran while one was open for 55% of the time, Pallas kernels for 0%

commit v1 on v0

v1 whole, which is shorter than its diff:
```python
import functools

import jax
import jax.numpy as jnp
from jax import lax
from jax.experimental import pallas as pl
from jax.experimental.pallas import tpu as pltpu
from jax.sharding import PartitionSpec as P

HEADS = 24
HEADDIM = 64
STATE = 128
CONV = 4
SPAN = 256
DI = 1536
XBC = 1792
TILE = 128
PAIRS = DI // TILE
HALF = SPAN // 2
EDGE = 8
epsilon = 1e-05
F32 = jnp.float32
BF16 = jnp.bfloat16
FULL = lax.Precision.HIGHEST


def mul(a, b):
    return jnp.dot(a, b, preferred_element_type=F32)


def mul_nt(a, b):
    return lax.dot_general(a, b, (((1,), (1,)), ((), ())), preferred_element_type=F32)


def mul_tn(a, b):
    return lax.dot_general(a, b, (((0,), (0,)), ((), ())), preferred_element_type=F32)


def sigmoid(v):
    return 0.5 * jnp.tanh(0.5 * v) + 0.5


def softplus(v):
    return jnp.maximum(v, 0.0) + jnp.log1p(jnp.exp(-jnp.abs(v)))


def fold(v):
    return jnp.sum(v.reshape(v.shape[0] // EDGE, EDGE, v.shape[1]), axis=0)


def tile_at(j, base=0):
    return pl.ds(pl.multiple_of(base + j * TILE, TILE), TILE)


def lane_low(shape):
    return lax.broadcasted_iota(jnp.int32, shape, 1) < HEADDIM


def spread(column, h):
    return jnp.broadcast_to(column[:, h : h + 1], (column.shape[0], TILE))


def conv_argument(cin_ref, cw_ref, cb_ref, cols):
    total = cb_ref[:, cols]
    for tap in range(CONV):
        start = EDGE - CONV + 1 + tap
        total = total + cw_ref[tap : tap + 1, cols] * cin_ref[0, start : start + SPAN, cols]
    return total


def head_times(step_raw, step_bias, decay_log):
    shifted = step_raw + step_bias
    step = softplus(shifted)
    log_decay = -jnp.exp(decay_log) * step
    rows = lax.broadcasted_iota(jnp.int32, (SPAN, SPAN), 0)
    columns = lax.broadcasted_iota(jnp.int32, (SPAN, SPAN), 1)
    lower = (rows >= columns).astype(F32)
    cumul = jnp.dot(lower, log_decay, precision=FULL, preferred_element_type=F32)
    return shifted, step, cumul, cumul - jnp.log(step)


def causal_mask(flip):
    rows = lax.broadcasted_iota(jnp.int32, (HALF, HALF), 0)
    columns = lax.broadcasted_iota(jnp.int32, (HALF, HALF), 1)
    return columns >= rows if flip else rows >= columns


def forward_kernel(
    len_ref, tok_ref, w_ref, ow_ref, nw_ref, cw_ref, cb_ref, sb_ref, dl_ref, sk_ref, gn_ref,
    out_ref, cin_ref, gr_ref, mx_ref, st_ref, sr_ref, nl_ref, gl_ref,
    ws, col_t, pair_s, row_s, state, scores, gated,
):
    block = pl.program_id(0)
    offset = block * SPAN

    @pl.when(block == 0)
    def _():
        ws[...] = jnp.zeros_like(ws)
        ws[:, :HEADS] = w_ref[:, DI + XBC : DI + XBC + HEADS]
        state[...] = jnp.zeros_like(state)
        cin_ref[0, :EDGE, :] = jnp.zeros((EDGE, XBC), F32)

    @pl.when(block > 0)
    def _():
        cin_ref[0, :EDGE, :] = gated[:EDGE, :]

    for r in range(0, SPAN, 64):
        tok = tok_ref[r : r + 64, :].astype(F32)
        nrm = lax.rsqrt(jnp.mean(tok * tok, axis=-1, keepdims=True) + epsilon)
        nl_ref[r : r + 64, :] = (tok * nrm * nw_ref[...]).astype(BF16)
    low = nl_ref[...]
    sr_ref[...] = mul(low, ws[...])
    for n in range(0, XBC, 256):
        cin_ref[0, EDGE:, n : n + 256] = mul(low, w_ref[:, DI + n : DI + n + 256])
    for n in range(0, DI, 256):
        gr_ref[:, n : n + 256] = mul(low, w_ref[:, n : n + 256])

    _, _, cumul, shift = head_times(sr_ref[...], sb_ref[...], dl_ref[...])
    row_s[...] = shift.T
    low_lanes = lane_low((SPAN, TILE))
    for h in range(HEADS):
        col_t[h] = spread(cumul, h)
    for j in range(PAIRS):
        pair_s[j] = jnp.where(low_lanes, spread(shift, 2 * j), spread(shift, 2 * j + 1))

    def act(jt):
        arg = conv_argument(cin_ref, cw_ref, cb_ref, tile_at(jt))
        return arg * sigmoid(arg)

    key = act(PAIRS).astype(BF16)
    query = act(PAIRS + 1).astype(BF16)
    key_t = key.astype(F32).T.astype(BF16)
    scores[...] = mul_nt(query, key)
    st_ref[0] = state[...]
    mask = causal_mask(False)

    def pair(j, total):
        cols = tile_at(j)
        heads_in = act(j)
        heads_low = heads_in.astype(BF16)
        cum0, cum1 = col_t[2 * j], col_t[2 * j + 1]
        cum = jnp.where(low_lanes, cum0, cum1)
        last = cum[SPAN - 1 : SPAN, :]
        old = state[:, cols]
        across = mul(query, old.astype(BF16))
        weighted = (heads_low.astype(F32) * jnp.exp(last - pair_s[j])).astype(BF16)
        state[:, cols] = jnp.exp(last) * old + mul(key_t, weighted)
        zero = jnp.zeros_like(heads_low)
        parts = (jnp.where(low_lanes, heads_low, zero), jnp.where(low_lanes, zero, heads_low))
        top, bottom = [], []
        for h in range(2):
            col = (cum0, cum1)[h]
            row = row_s[pl.ds(2 * j + h, 1), :]
            first = jnp.where(mask, col[:HALF] - row[:, :HALF], -jnp.inf)
            top.append((scores[:HALF, :HALF] * jnp.exp(first)).astype(BF16))
            full = col[HALF:] - row[:, :HALF]
            bottom.append((scores[HALF:, :HALF] * jnp.exp(full)).astype(BF16))
            second = jnp.where(mask, col[HALF:] - row[:, HALF:], -jnp.inf)
            bottom.append((scores[HALF:, HALF:] * jnp.exp(second)).astype(BF16))
        tops = jnp.concatenate([p[:HALF] for p in parts], axis=0)
        within = jnp.concatenate(
            [
                mul(jnp.concatenate(top, axis=1), tops),
                mul(jnp.concatenate(bottom, axis=1), jnp.concatenate(parts, axis=0)),
            ],
            axis=0,
        )
        mixed = within + jnp.exp(cum) * across + sk_ref[:, cols] * heads_in
        mx_ref[:, cols] = mixed
        gate = gr_ref[:, cols]
        value = mixed * (gate * sigmoid(gate))
        gated[:, cols] = value
        return total + value * value

    total = lax.fori_loop(0, PAIRS, pair, jnp.zeros((SPAN, TILE), F32))
    rms = lax.rsqrt(jnp.sum(total, axis=-1, keepdims=True) * (1.0 / DI) + epsilon)

    def finish(j, carry):
        cols = tile_at(j)
        gl_ref[:, cols] = (gated[:, cols] * rms * gn_ref[:, cols]).astype(BF16)
        return carry

    lax.fori_loop(0, PAIRS, finish, 0)
    positions = offset + lax.broadcasted_iota(jnp.int32, (SPAN, 256), 0)
    valid = positions < len_ref[0]
    for n in range(0, tok_ref.shape[1], 256):
        branch = mul(gl_ref[...], ow_ref[:, n : n + 256])
        tok = tok_ref[:, n : n + 256].astype(F32)
        out_ref[:, n : n + 256] = (tok + jnp.where(valid, branch, 0.0)).astype(BF16)
    gated[:EDGE, :] = cin_ref[0, SPAN:, :]


def backward_kernel(
    len_ref, cot_ref, tok_ref, w_ref, ow_ref, nw_ref, cw_ref, cb_ref, sb_ref, dl_ref, sk_ref, gn_ref,
    cin_ref, gr_ref, mx_ref, st_ref, sr_ref,
    ig_ref, gp_ref, taps_ref, gcb_ref, ggn_ref, gsk_ref, gnw_ref, ghd_ref,
    ws, col_s, pair_t, row_t, later, scores, grad_scores, gg, sig, gpre, args, acc_q, acc_k, acc_u, acc_v, acc_l,
):
    step_id = pl.program_id(0)
    count = pl.num_programs(0)
    offset = (count - 1 - step_id) * SPAN

    @pl.when(step_id == 0)
    def _():
        ws[...] = jnp.zeros_like(ws)
        ws[:, :HEADS] = w_ref[:, DI + XBC : DI + XBC + HEADS]
        later[...] = jnp.zeros_like(later)
        gpre[SPAN:, :] = jnp.zeros((EDGE, XBC), F32)
        for ref in (taps_ref, gcb_ref, ggn_ref, gsk_ref, gnw_ref, ghd_ref):
            ref[...] = jnp.zeros_like(ref)

    width = cot_ref.shape[1]
    positions = offset + lax.broadcasted_iota(jnp.int32, (SPAN, width), 0)
    grad_branch = jnp.where(positions < len_ref[0], cot_ref[...].astype(F32), 0.0).astype(BF16)
    for n in range(0, DI, 256):
        gg[:, n : n + 256] = mul_nt(grad_branch, ow_ref[n : n + 256, :])

    shifted, step, cumul, shift = head_times(sr_ref[...], sb_ref[...], dl_ref[...])
    row_t[...] = cumul.T
    low_lanes = lane_low((SPAN, TILE))
    for h in range(HEADS):
        col_s[h] = spread(shift, h)
    for j in range(PAIRS):
        pair_t[j] = jnp.where(low_lanes, spread(cumul, 2 * j), spread(cumul, 2 * j + 1))

    def sums(j, carry):
        squares, crossed = carry
        cols = tile_at(j)
        gate = gr_ref[:, cols]
        part = sigmoid(gate)
        sig[:, cols] = part
        value = mx_ref[:, cols] * (gate * part)
        return squares + value * value, crossed + (gg[:, cols] * gn_ref[:, cols]) * value

    nothing = jnp.zeros((SPAN, TILE), F32)
    squares, crossed = lax.fori_loop(0, PAIRS, sums, (nothing, nothing))
    rms = lax.rsqrt(jnp.sum(squares, axis=-1, keepdims=True) * (1.0 / DI) + epsilon)
    coef = rms * rms * (jnp.sum(crossed, axis=-1, keepdims=True) * (1.0 / DI))
    rms = jnp.broadcast_to(rms, (SPAN, TILE))
    coef = jnp.broadcast_to(coef, (SPAN, TILE))

    def act(jt, slot):
        arg = conv_argument(cin_ref, cw_ref, cb_ref, tile_at(jt))
        args[:, slot * TILE : (slot + 1) * TILE] = arg
        return (arg * sigmoid(arg)).astype(BF16)

    key = act(PAIRS, 0)
    query = act(PAIRS + 1, 1)
    query_t = query.astype(F32).T.astype(BF16)
    scores[...] = mul_nt(key, query)
    grad_scores[...] = jnp.zeros_like(grad_scores)
    for ref in (acc_q, acc_k, acc_u, acc_v, acc_l):
        ref[...] = jnp.zeros_like(ref)
    mask = causal_mask(True)
    lane = lax.broadcasted_iota(jnp.int32, (2 * TILE, TILE), 0) % TILE
    head = lax.broadcasted_iota(jnp.int32, (2 * TILE, TILE), 1)

    def by_head(value, pick):
        high = value.astype(BF16)
        rest = (value - high.astype(F32)).astype(BF16)
        return mul(jnp.concatenate([high, rest], axis=1), pick)

    def pair(j, carry):
        cols = tile_at(j)
        arg = conv_argument(cin_ref, cw_ref, cb_ref, cols)
        part_x = sigmoid(arg)
        heads_in = arg * part_x
        heads_low = heads_in.astype(BF16)
        heads_float = heads_low.astype(F32)
        gate, mixed, part, gain, back = (
            gr_ref[:, cols], mx_ref[:, cols], sig[:, cols], gn_ref[:, cols], gg[:, cols]
        )
        silu = gate * part
        value = mixed * silu
        ggn_ref[:, cols] += fold(back * value * rms)
        grad_gated = rms * (back * gain - value * coef)
        grad_scan = grad_gated * silu
        gp_ref[:, cols] = (grad_gated * mixed * (part * (1.0 + gate * (1.0 - part)))).astype(BF16)
        gsk_ref[:, cols] += fold(grad_scan * heads_in)
        cum = pair_t[j]
        growth = jnp.exp(cum)
        last = cum[SPAN - 1 : SPAN, :]
        grad_low = grad_scan.astype(BF16)
        scaled = growth * grad_scan
        grad_across = scaled.astype(BF16)
        col0, col1 = col_s[2 * j], col_s[2 * j + 1]
        carry_weight = jnp.exp(last - jnp.where(low_lanes, col0, col1))
        weighted = (heads_float * carry_weight).astype(BF16)
        after = later[:, cols]
        after_low = after.astype(BF16)
        before = st_ref[0, :, cols]
        before_low = before.astype(BF16)
        across = mul(query, before_low)
        acc_k[...] += mul_nt(weighted, after_low)
        acc_q[...] += mul_nt(grad_across, before_low)
        grow_last = jnp.exp(last)
        carried = mul(key, after_low) * carry_weight
        last_sum = fold(carried * heads_float) + fold(after * before) * grow_last
        later[:, cols] = mul(query_t, grad_across) + grow_last * after
        zero = jnp.zeros_like(grad_low)
        parts = (jnp.where(low_lanes, grad_low, zero), jnp.where(low_lanes, zero, grad_low))
        top, bottom = [], []
        for h in range(2):
            col = (col0, col1)[h]
            row = row_t[pl.ds(2 * j + h, 1), :]
            mixed_top = mul_nt(heads_low[:HALF], parts[h])
            mixed_low = mul_nt(heads_low[HALF:], parts[h][HALF:])
            factor = jnp.exp(jnp.where(mask, row[:, :HALF] - col[:HALF], -jnp.inf))
            top.append((scores[:HALF, :HALF] * factor).astype(BF16))
            grad_scores[:HALF, :HALF] += mixed_top[:, :HALF] * factor
            factor = jnp.exp(row[:, HALF:] - col[:HALF])
            top.append((scores[:HALF, HALF:] * factor).astype(BF16))
            grad_scores[:HALF, HALF:] += mixed_top[:, HALF:] * factor
            factor = jnp.exp(jnp.where(mask, row[:, HALF:] - col[HALF:], -jnp.inf))
            bottom.append((scores[HALF:, HALF:] * factor).astype(BF16))
            grad_scores[HALF:, HALF:] += mixed_low * factor
        lows = jnp.concatenate([p[HALF:] for p in parts], axis=0)
        grad_heads = carried + jnp.concatenate(
            [
                mul(jnp.concatenate(top, axis=1), jnp.concatenate(parts, axis=0)),
                mul(jnp.concatenate(bottom, axis=1), lows),
            ],
            axis=0,
        )
        gain_skip = sk_ref[:, cols]
        spanned = growth * across
        within = mixed - gain_skip * heads_in - spanned
        pick = (head == 2 * j + lane // HEADDIM).astype(F32)
        pick_low = pick.astype(BF16)
        acc_u[...] += by_head(grad_low.astype(F32) * within + grad_scan * spanned, pick_low)
        acc_v[...] += by_head(heads_float * grad_heads, pick_low)
        acc_l[...] += jnp.dot(last_sum, pick[:TILE], precision=FULL, preferred_element_type=F32)
        grad_conv = grad_heads + gain_skip * grad_scan
        gpre[:SPAN, cols] = grad_conv * (part_x * (1.0 + arg * (1.0 - part_x)))
        return carry

    lax.fori_loop(0, PAIRS, pair, 0)

    rows = lax.broadcasted_iota(jnp.int32, (SPAN, SPAN), 0)
    columns = lax.broadcasted_iota(jnp.int32, (SPAN, SPAN), 1)
    upper = (columns >= rows).astype(F32)
    at_end = lax.broadcasted_iota(jnp.int32, (SPAN, TILE), 0) == SPAN - 1
    to_step = acc_v[...]
    ends = jnp.sum(acc_l[...], axis=0, keepdims=True)
    grad_cumul = acc_u[...] - to_step + jnp.where(at_end, ends, 0.0)
    grad_log = jnp.dot(upper, grad_cumul, precision=FULL, preferred_element_type=F32)
    rate = jnp.exp(dl_ref[...])
    safe = jnp.where(step > 0.0, step, 1.0)
    grad_step = jnp.where(step > 0.0, to_step / safe, 0.0)
    grad_raw = (grad_step - rate * grad_log) * sigmoid(shifted)
    ghd_ref[:EDGE, :] += fold(grad_raw)
    ghd_ref[EDGE:, :] -= fold(rate * step * grad_log)
    raw_low = grad_raw.astype(BF16)
    gp_ref[:, DI + XBC :] = raw_low[:, :HEADS]

    scores_low = grad_scores[...].astype(BF16)
    scores_t = grad_scores[...].T.astype(BF16)
    for slot, grad in (
        (0, acc_k[...] + mul(scores_low, query)),
        (1, acc_q[...] + mul(scores_t, key)),
    ):
        arg = args[:, slot * TILE : (slot + 1) * TILE]
        part = sigmoid(arg)
        gpre[:SPAN, DI + slot * TILE : DI + (slot + 1) * TILE] = grad * (part * (1.0 + arg * (1.0 - part)))

    def through_conv(j, carry):
        cols = tile_at(j)
        here = gpre[:SPAN, cols]
        gcb_ref[:, cols] += fold(here)
        total = jnp.zeros_like(here)
        for tap in range(CONV):
            start = EDGE - CONV + 1 + tap
            taps_ref[tap, :, cols] += fold(here * cin_ref[0, start : start + SPAN, cols])
            ahead = CONV - 1 - tap
            total = total + cw_ref[tap : tap + 1, cols] * gpre[ahead : ahead + SPAN, cols]
        gp_ref[:, tile_at(j, DI)] = total.astype(BF16)
        return carry

    lax.fori_loop(0, PAIRS + 2, through_conv, 0)
    gpre[SPAN:, :] = gpre[:EDGE, :]

    for n in range(0, width, 256):
        grad = mul_nt(gp_ref[:, : DI + XBC], w_ref[n : n + 256, : DI + XBC])
        gg[:, n : n + 256] = grad + mul_nt(raw_low, ws[n : n + 256, :])
    for r in range(0, SPAN, 64):
        tok = tok_ref[r : r + 64, :].astype(F32)
        nrm = lax.rsqrt(jnp.mean(tok * tok, axis=-1, keepdims=True) + epsilon)
        grad = gg[r : r + 64, :width]
        gnw_ref[...] += fold(grad * tok * nrm)
        value = grad * nw_ref[...]
        centre = jnp.mean(value * tok, axis=-1, keepdims=True) * (nrm * nrm)
        grad_tok = nrm * (value - tok * centre)
        ig_ref[r : r + 64, :] = (cot_ref[r : r + 64, :].astype(F32) + grad_tok).astype(BF16)


def whole(shape):
    return pl.BlockSpec(shape, lambda i: (0,) * len(shape), pipeline_mode=pl.Buffered(1))


def rows_of(width, last=None):
    if last is None:
        return pl.BlockSpec((SPAN, width), lambda i: (i, 0))
    return pl.BlockSpec((SPAN, width), lambda i: (last - i, 0))


def params_specs(width):
    proj = DI + XBC + HEADS
    return [
        whole((width, proj)), whole((DI, width)), whole((1, width)), whole((CONV, XBC)), whole((1, XBC)),
        whole((1, TILE)), whole((1, TILE)), whole((1, DI)), whole((1, DI)),
    ]


LIMIT = 60 * 2**20


def run_forward(valid, tok, params):
    length, width = tok.shape
    count = length // SPAN
    shapes = [
        ((length, width), BF16), ((count, SPAN + EDGE, XBC), F32), ((length, DI), F32), ((length, DI), F32),
        ((count, STATE, DI), F32), ((length, TILE), F32), ((length, width), BF16), ((length, DI), BF16),
    ]
    out_specs = [
        rows_of(width), pl.BlockSpec((1, SPAN + EDGE, XBC), lambda i: (i, 0, 0)), rows_of(DI), rows_of(DI),
        pl.BlockSpec((1, STATE, DI), lambda i: (i, 0, 0)), rows_of(TILE), rows_of(width), rows_of(DI),
    ]
    return pl.pallas_call(
        forward_kernel,
        grid=(count,),
        out_shape=[jax.ShapeDtypeStruct(s, d) for s, d in shapes],
        in_specs=[pl.BlockSpec(memory_space=pltpu.SMEM), rows_of(width), *params_specs(width)],
        out_specs=out_specs,
        scratch_shapes=[
            pltpu.VMEM((width, TILE), BF16), pltpu.VMEM((HEADS, SPAN, TILE), F32), pltpu.VMEM((PAIRS, SPAN, TILE), F32),
            pltpu.VMEM((TILE, SPAN), F32), pltpu.VMEM((STATE, DI), F32), pltpu.VMEM((SPAN, SPAN), F32), pltpu.VMEM((SPAN, XBC), F32),
        ],
        compiler_params=pltpu.CompilerParams(dimension_semantics=("arbitrary",), vmem_limit_bytes=LIMIT),
        cost_estimate=pl.CostEstimate(flops=20 * 10**9, bytes_accessed=60 * 10**6, transcendentals=10**7),
    )(valid, tok, *params)


def run_backward(valid, cot, tok, params, kept):
    length, width = tok.shape
    count = length // SPAN
    proj = DI + XBC + HEADS
    last = count - 1
    shapes = [
        ((length, width), BF16), ((length, proj), BF16), ((CONV, EDGE, XBC), F32), ((EDGE, XBC), F32), ((EDGE, DI), F32),
        ((EDGE, DI), F32), ((EDGE, width), F32), ((2 * EDGE, TILE), F32),
    ]
    out_specs = [rows_of(width, last), rows_of(proj, last), *(whole(s) for s, _ in shapes[2:])]
    kept_specs = [
        pl.BlockSpec((1, SPAN + EDGE, XBC), lambda i: (last - i, 0, 0)), rows_of(DI, last), rows_of(DI, last),
        pl.BlockSpec((1, STATE, DI), lambda i: (last - i, 0, 0)), rows_of(TILE, last),
    ]
    square, wide = pltpu.VMEM((SPAN, SPAN), F32), pltpu.VMEM((SPAN, DI), F32)
    narrow = pltpu.VMEM((SPAN, TILE), F32)
    return pl.pallas_call(
        backward_kernel,
        grid=(count,),
        out_shape=[jax.ShapeDtypeStruct(s, d) for s, d in shapes],
        in_specs=[pl.BlockSpec(memory_space=pltpu.SMEM), rows_of(width, last), rows_of(width, last), *params_specs(width), *kept_specs],
        out_specs=out_specs,
        scratch_shapes=[
            pltpu.VMEM((width, TILE), BF16), pltpu.VMEM((HEADS, SPAN, TILE), F32), pltpu.VMEM((PAIRS, SPAN, TILE), F32),
            pltpu.VMEM((TILE, SPAN), F32), pltpu.VMEM((STATE, DI), F32), square, square, wide, wide,
            pltpu.VMEM((SPAN + EDGE, XBC), F32), pltpu.VMEM((SPAN, 2 * TILE), F32),
            narrow, narrow, narrow, narrow, pltpu.VMEM((EDGE, TILE), F32),
        ],
        compiler_params=pltpu.CompilerParams(dimension_semantics=("arbitrary",), vmem_limit_bytes=LIMIT),
        cost_estimate=pl.CostEstimate(flops=40 * 10**9, bytes_accessed=60 * 10**6, transcendentals=2 * 10**7),
    )(valid, cot, tok, *params, *kept)


def prepare(norm_full, in_full, conv_full, shift_full, gate_full, out_full, step_bias, decay_log, skip_gain):
    pad = ((0, 0), (0, TILE - HEADS))
    return (
        in_full,
        out_full,
        norm_full.astype(F32)[None],
        conv_full.astype(F32).T,
        shift_full.astype(F32)[None],
        jnp.pad(step_bias[None], pad),
        jnp.pad(decay_log[None], pad),
        jnp.repeat(skip_gain, HEADDIM)[None],
        gate_full.astype(F32)[None],
    )


def on_device(
    tokens, cotangent, lengths, order, norm_weight, in_weight, conv_weight, conv_bias,
    step_bias, decay_log, skip_gain, gate_norm_weight, out_weight,
):
    peers = lax.axis_size("shard")
    rank = lax.axis_index("shard")
    piece, width = tokens.shape[1:]

    def gather(x):
        return lax.all_gather(x, "shard", axis=0, tiled=True)

    def to_sequences(x):
        parts = x.reshape(peers, 1, piece, width)
        return lax.all_to_all(parts, "shard", split_axis=0, concat_axis=2, tiled=True).reshape(peers * piece, width)

    def to_slots(x):
        parts = x.reshape(1, peers * piece, width)
        return lax.all_to_all(parts, "shard", split_axis=1, concat_axis=0, tiled=True)

    slots = jnp.arange(peers, dtype=jnp.int32)
    sequence = jnp.sum(jnp.where(slots == rank, order[0], 0))
    valid = jnp.sum(jnp.where(slots == sequence, lengths[0], 0))[None]
    tok = to_sequences(tokens)
    cot = to_sequences(cotangent)
    params = prepare(
        gather(norm_weight), gather(in_weight), gather(conv_weight), gather(conv_bias),
        gather(gate_norm_weight), gather(out_weight), step_bias, decay_log, skip_gain,
    )
    out, cin, gr, mx, st, sr, normed, gate_low = run_forward(valid, tok, params)
    output = to_slots(out)
    ig, gp, taps, gcb, ggn, gsk, gnw, ghd = run_backward(valid, cot, tok, params, (cin, gr, mx, st, sr))
    input_grad = to_slots(ig)
    keep = jnp.arange(peers * piece, dtype=jnp.int32)[:, None] < valid[0]
    grad_branch = jnp.where(keep, cot, jnp.zeros_like(cot))
    grad_out = mul_tn(gate_low, grad_branch)
    grad_in = mul_tn(normed, gp)

    def scatter(x):
        return lax.psum(lax.psum_scatter(x, "shard", scatter_dimension=0, tiled=True), "rep")

    heads = jnp.stack([
        jnp.sum(ghd[:EDGE], axis=0)[:HEADS], jnp.sum(ghd[EDGE:], axis=0)[:HEADS],
        jnp.sum(gsk.reshape(EDGE, HEADS, HEADDIM), axis=(0, 2)),
    ])
    heads = lax.psum(heads, ("rep", "shard"))
    return (
        output, input_grad, scatter(jnp.sum(gnw, axis=0)), scatter(grad_in), scatter(jnp.sum(taps, axis=1).T),
        scatter(jnp.sum(gcb, axis=0)), heads[0], heads[1], heads[2], scatter(jnp.sum(ggn, axis=0)), scatter(grad_out),
    )


def solution(mesh):
    placed = (
        P("rep", "shard", None), P("rep", "shard", None), P("rep", None), P("rep", None), P("shard"),
        P("shard", None), P("shard", None), P("shard"), P(), P(), P(), P("shard"), P("shard", None),
    )
    outs = (
        P("rep", "shard", None), P("rep", "shard", None), P("shard"), P("shard", None), P("shard", None),
        P("shard"), P(), P(), P(), P("shard"), P("shard", None),
    )
    return jax.shard_map(on_device, mesh=mesh, in_specs=placed, out_specs=outs, check_vma=False)
```

time: 1300 us -> 791 us (0.61)
  local copies, waits for them, and re-layouts: 440 us -> 48.6 us
  matrix products: 164 us -> 19 us
  Pallas kernels: 0 us -> 134 us
  other arithmetic: 146 us -> 26.1 us
  waiting for transfers between devices: 144 us -> 211 us
  blocking collectives: 336 us -> 307 us
  starting transfers between devices: 36.6 us -> 16.2 us
    dynamic_update_slice x32 -> x0, local copies, waits for them, and re-layouts: 308 us -> none  [the longest x16 295 us: forward_seq(): final_state, kept = lax.scan(block_forward, start, blocks)]
    dot_general x62 -> x2, matrix products: 164 us -> 19 us  [mul_tn(): lax.dot_general(a, b, (((0,), (0,)), ((), ())), preferred_element_type=F32)]
    pallas_call x0 -> x2, Pallas kernels: none -> 134 us  [the longest x1 86.8 us: run_backward(): pl.pallas_call(backward_kernel, grid=(count,), out_shape=[jax.ShapeDtypeS...]
    reduce_scatter x2, waiting for transfers between devices: 123 us -> 202 us  [scatter(): lax.psum_scatter(x, 'shard', scatter_dimension=0, tiled=True)]
    reduce_sum x15 -> x9, other arithmetic: 50.2 us -> 2.19 us  [the longest x1 1.28 us: on_device(): valid = jnp.sum(jnp.where(slots == sequence, lengths[0], 0))[None]]
    another operation x34 -> x1, other arithmetic: 37.7 us -> 0.01 us  [on_device(): jnp.stack([jnp.sum(ghd[:EDGE], axis=0)[:HEADS], jnp.sum(ghd[EDGE:], axis=...]
    all_to_all x3, starting transfers between devices: 36.4 us -> 15.5 us  [the longest x2 11.4 us: to_slots(): lax.all_to_all(parts, 'shard', split_axis=1, concat_axis=0, tiled=True)]
    unnamed x131 -> x57, local copies, waits for them, and re-layouts: 55.2 us -> 36.1 us
  transfers between devices with their start and end apart: 9 -> 9, of which waited for: 2 -> 2; matrix products, arithmetic and copies ran while one was open for 55% -> 11% of each run, Pallas kernels for 0% -> 17%
where the time goes in v1:
time: 791 us; the launch traced here: 781 us
  blocking collectives  307 us (39%)
  waiting for transfers between devices  211 us (27%)
  Pallas kernels  134 us (17%)
  local copies, waits for them, and re-layouts  48.6 us (6%)
  other arithmetic  26.1 us (3%)
  matrix products  19 us (2%)
  between operations  18.8 us (2%)
  starting transfers between devices  16.2 us (2%)
    reduce_scatter x2, waiting for transfers between devices, scatter(): lax.psum_scatter(x, 'shard', scatter_dimension=0, tiled=True)  202 us
    unnamed x2, blocking collectives  176 us
    pallas_call x1, Pallas kernels, run_backward(): pl.pallas_call(backward_kernel, grid=(count,), out_shape=[jax.ShapeDtypeS...  86.8 us
    all_to_all x1, blocking collectives, to_sequences(): lax.all_to_all(parts, 'shard', split_axis=0, concat_axis=2, tiled=True)  55.5 us
    pallas_call x1, Pallas kernels, run_forward(): pl.pallas_call(forward_kernel, grid=(count,), out_shape=[jax.ShapeDtypeSt...  46.9 us
    psum x1, blocking collectives, on_device(): heads = lax.psum(heads, ('rep', 'shard'))  36.9 us
    unnamed x57, local copies, waits for them, and re-layouts  36.1 us
    all_gather x1, blocking collectives, gather(): return lax.all_gather(x, 'shard', axis=0, tiled=True)  36 us
  transfers between devices with their start and end apart: 9, of which 2 were waited for; matrix products, arithmetic and copies ran while one was open for 11% of the time, Pallas kernels for 17%

profile of v1, /device:TPU:0, one launch (start us, length us, event | category | flops | bytes accessed | tf_op | source)
XLA Modules:
  0.0 780.7 jit_solution(3425130861500506898)
XLA Ops:
  7.2 0.0 all-gather.6.cloned.1.call-start
  7.2 0.7 all-gather.6.cloned.1.call-update
  7.9 0.0 all-gather.4.cloned.1.call-start
  8.0 0.7 all-gather.4.cloned.1.call-update
  8.7 55.5 %all_to_all.42 = bf16[16,1,64,768]{3,2,1,0:T(8,128)(2,1)} all-to-all(bf16[16,1,64,768]{3,2,1,0:T(8,128)(2,1)} %bitcast.51), channel_id=1, replica_groups=mesh['rep'=2,'shard'=16] {'shard'}, dimensions={0} | all-to-all | bytes 3145728 | tf_op jit(solution)/shard_map/all_to_all | solution.py:504
  64.3 4.0 all-to-all-start.2
  68.3 0.0 reduce-scatter.8.cloned.1.call-start
  68.4 0.6 fusion.7
  70.9 0.2 dynamic-update-slice.1
  71.2 0.2 dynamic-update-slice.2
  71.4 0.2 dynamic-update-slice
  71.7 100.2 %all-reduce.11 = (bf16[768]{0:T(1024)(128)(2,1)S(1)}, bf16[1792]{0:T(1024)(128)(2,1)S(1)}, bf16[1536]{0:T(1024)(128)(2,1)S(1)}) all-reduce(bf16[768]{0:T(1024)(128)(2,1)S(1)} %dynamic-update-slice, bf16[1792]{0:T(1024)(128)(2,1)S(1)} %dynamic-update-slice.1, ...), channel_id=1, replica_groups=mesh['rep'=2,'shard'=16] {'shard'}, use_global_device_ids=true, to_apply=%add.2 | all-reduce | flops 4096 | bytes 16384
  171.9 0.6 reshape.68.cb_ref
  172.5 0.6 reshape.69.gn_ref
  173.1 0.6 reshape.67.nw_ref
  173.6 36.0 %all-gather = bf16[16,112,4]{1,2,0:T(4,128)(2,1)S(1)} all-gather(bf16[1,112,4]{1,2,0:T(4,128)(2,1)S(1)} %bitcast.64), channel_id=1, replica_groups=mesh['rep'=2,'shard'=16] {'shard'}, dimensions={0}, use_global_device_ids=true | all-gather | bytes 15232 | tf_op jit(solution)/shard_map/all_gather | solution.py:500
  209.7 0.7 reshape.81
  210.4 0.1 broadcast_in_dim.52
  210.4 0.7 broadcast_in_dim_reshape.3.sk_ref
  211.1 0.5 pad.7.sb_ref
  211.6 0.5 pad.8.dl_ref
  212.2 0.6 fusion.4
  212.8 1.3 fusion.5
  214.1 0.6 iota_compare_fusion
  214.7 0.0 all-gather.6.cloned.1.call-done.ow_ref
  214.7 0.0 all-gather.4.cloned.1.call-done.w_ref
  214.8 46.9 %shard_map.212 = (bf16[1024,768]{1,0:T(8,128)(2,1)}, f32[4,264,1792]{2,1,0:T(8,128)}, f32[1024,1536]{1,0:T(8,128)}, f32[1024,1536]{1,0:T(8,128)}, f32[4,128,1536...) custom-call(s32[1]{0:T(128)} %bitcast.2.len_ref, ...), custom_call_target="tpu_custom_call" | custom-call | flops 20000000000 | bytes 60000000 | tf_op jit(solution)/shard_map/pallas_call | solution.py:428
  261.7 7.4 fusion
  269.1 0.0 reduce-scatter.8.cloned.1.call-update
  269.1 0.5 reduce-scatter.6.cloned.1.call-start
  269.6 86.8 %shard_map.213 = (bf16[1024,768]{1,0:T(8,128)(2,1)}, bf16[1024,3352]{1,0:T(8,128)(2,1)}, f32[4,8,1792]{2,1,0:T(8,128)}, f32[8,1792]{1,0:T(8,128)}, f32[8,1536]{1...) custom-call(s32[1]{0:T(128)} %bitcast.2.len_ref, bf16[1024,768]{1,0:T(8,128)(2,1)} %bitcast.55, ...), custom_call_target="tpu_custom_call" | custom-call | flops 40000000000 | bytes 60000000 | tf_op jit(solution)/shard_map/pallas_call | solution.py:459
  356.5 11.7 %fusion.8 = f32[768,3352]{1,0:T(8,128)} fusion(bf16[1024,768]{1,0:T(8,128)(2,1)S(1)} %copy-done.17, bf16[1024,3352]{1,0:T(8,128)(2,1)} %get-tuple-element.36), kind=kOutput, calls=%fused_computation.22 | convolution fusion | flops 5272240128 | bytes 18735104 | tf_op jit(solution)/shard_map/dot_general | solution.py:36
  368.2 3.8 copy.44
  372.0 0.5 broadcast.12
  372.5 11.6 %reduce.3 = bf16[1024,768]{1,0:T(8,128)(2,1)} reduce(bf16[1024,1,768]{2,1,0:T(2,128)(2,1)S(1)} %bitcast.47, bf16[]{:T(256)} %broadcast.12), dimensions={1}, to_apply=%bitcast.45.reduce_sub_computation | reduce | bytes 3145730
  384.1 4.6 reshape.95
  388.7 4.4 all-to-all-start.3
  393.1 3.8 copy.45
  397.0 11.6 %reduce.2 = bf16[1024,768]{1,0:T(8,128)(2,1)} reduce(bf16[1024,1,768]{2,1,0:T(2,128)(2,1)S(1)} %bitcast.48, bf16[]{:T(256)} %broadcast.12), dimensions={1}, to_apply=%bitcast.46.reduce_sub_computation | reduce | bytes 3145730
  408.6 4.6 reshape.93
  413.2 7.8 %all-to-all-done.3 = bf16[16,2,24576]{2,1,0:T(2,128)(2,1)} async-done(((bf16[16,2,24576]{2,1,0:T(2,128)(2,1)}), bf16[16,2,24576]{2,1,0:T(2,128)(2,1)}, u32[]{:S(2)}, u32[]{:S(2)}) %all-to-all-start.3) | async-done | bytes 1572896 | tf_op jit(solution)/shard_map/all_to_all | solution.py:508
  421.0 7.0 all-to-all-start.1
  428.0 0.0 reduce-scatter.10.cloned.1.call-start
  428.1 0.1 reduce_sum.91
  428.2 1.3 copy.37
  429.5 0.0 all-reduce.14.cloned.1.call-start
  429.6 0.0 reduce-scatter.8.cloned.1.call-done
  429.6 201.9 %reduce-scatter.6.cloned.1.call-done = f32[48,3352]{1,0:T(8,128)} async-done(((f32[768,3352]{1,0:T(8,128)}), f32[48,3352]{1,0:T(8,128)}) %reduce-scatter.6.cloned.1.call-update) | async-done | bytes 643600 | tf_op jit(solution)/shard_map/reduce_scatter | solution.py:529
  633.5 0.1 reduce_sum.96
  633.6 0.1 reduce_sum.97
  633.8 75.3 %all-reduce.8 = (f32[768]{0:T(1024)S(1)}, f32[1792]{0:T(1024)S(1)}, f32[1536]{0:T(1024)S(1)}) all-reduce(f32[768]{0:T(1024)S(1)} %reduce_sum.90, f32[1792]{0:T(1024)S(1)} %reduce_sum.92, f32[1536]{0:T(1024)S(1)} %reduce_sum.98), channel_id=2, replica_groups=mesh['rep'=2,'shard'=16] {'shard'}, use_global_device_ids=true, to_apply=%region_3.4.clone | all-reduce | flops 4096 | bytes 32768
  709.2 0.1 dynamic-slice.6
  709.2 0.1 dynamic-slice.8
  709.3 0.1 dynamic-slice.4
  709.4 36.9 %psum.53 = f32[3,24]{1,0:T(4,128)S(1)} all-reduce(f32[3,24]{1,0:T(4,128)S(1)} %pad_maximum_fusion), channel_id=1, replica_groups=mesh['rep'=2,'shard'=16] {'rep','shard'}, use_global_device_ids=true, to_apply=%region_17.18 | all-reduce | flops 72 | bytes 576 | tf_op jit(solution)/shard_map/psum | solution.py:535
  746.3 0.5 slice_bitcast_fusion
  746.8 0.9 copy.38
  747.7 3.0 all-reduce.9
  750.8 8.1 %reshape.96 = bf16[1024,1,768]{2,1,0:T(2,128)(2,1)S(1)} reshape(bf16[16,2,24576]{2,1,0:T(2,128)(2,1)} %all-to-all-done.3) | data formatting | bytes 3145728
  758.8 1.4 copy.40
  760.2 8.1 %reshape.94 = bf16[1024,1,768]{2,1,0:T(2,128)(2,1)S(1)} reshape(bf16[16,2,24576]{2,1,0:T(2,128)(2,1)} %all-to-all-done.1) | data formatting | bytes 3145728
  768.3 1.4 copy.39
  769.7 2.0 copy.51
  771.7 1.7 copy.52
  (54 shorter events, 0.3 us)
Async XLA Ops:
  7.2 207.6 %all-gather.6.cloned.1.call-start = ((), (), s32[]{:S(2)}) async-start(), calls=%async_computation.8 | async-start | bytes 2506752 | tf_op jit(solution)/shard_map/all_gather | solution.py:500
  7.9 206.9 %all-gather.4.cloned.1.call-start = ((), (), s32[]{:S(2)}) async-start(), calls=%async_computation.7 | async-start | bytes 5640192 | tf_op jit(solution)/shard_map/all_gather | solution.py:500
  64.2 4.2 copy-start.7
  64.2 6.7 copy-start.10
  64.2 7.0 copy-start.11
  64.2 7.3 copy-start.12
  64.2 109.4 %copy-start.8 = (bf16[112,4]{0,1:T(4,128)(2,1)S(1)}, bf16[112,4]{0,1:T(4,128)(2,1)}, u32[]{:S(2)}) copy-start(bf16[112,4]{0,1:T(4,128)(2,1)} %param.19) | copy-start | bytes 2692
  64.2 146.2 %copy-start.9 = (f32[24]{0:T(128)S(1)}, f32[24]{0:T(128)}, u32[]{:S(2)}) copy-start(f32[24]{0:T(128)} %param.23) | copy-start | bytes 292
  64.2 146.9 %copy-start.13 = (f32[24]{0:T(128)S(1)}, f32[24]{0:T(128)}, u32[]{:S(2)}) copy-start(f32[24]{0:T(128)} %param.21) | copy-start | bytes 292
  64.2 147.4 %copy-start.14 = (f32[24]{0:T(128)S(1)}, f32[24]{0:T(128)}, u32[]{:S(2)}) copy-start(f32[24]{0:T(128)} %param.22) | copy-start | bytes 292
  64.2 147.9 %copy-start.15 = (s32[1,16]{1,0:T(1,128)S(1)}, s32[1,16]{1,0:T(1,128)}, u32[]{:S(2)}) copy-start(s32[1,16]{1,0:T(1,128)} %param.16) | copy-start | bytes 196
  64.2 148.5 %copy-start.16 = (s32[1,16]{1,0:T(1,128)S(1)}, s32[1,16]{1,0:T(1,128)}, u32[]{:S(2)}) copy-start(s32[1,16]{1,0:T(1,128)} %param.15) | copy-start | bytes 196
  64.3 197.4 %all-to-all-start.2 = ((bf16[16,1,64,768]{3,2,1,0:T(8,128)(2,1)}), bf16[16,1,64,768]{3,2,1,0:T(8,128)(2,1)S(1)}, u32[]{:S(2)}, u32[]{:S(2)}) async-start(bf16[16,1,64,768]{3,2,1,0:T(8,128)(2,1)} %bitcast.13), calls=%async_computation.2 | async-start | bytes 3145728 | tf_op jit(solution)/shard_map/all_to_all | solution.py:504
  68.3 361.3 %reduce-scatter.8.cloned.1.call-start = ((), (), s32[]{:S(2)}) async-start(), calls=%async_computation.10 | async-start | bytes 5013504 | tf_op jit(solution)/shard_map/reduce_scatter | solution.py:529
  261.7 7.4 copy-start
  269.1 362.4 %reduce-scatter.6.cloned.1.call-start = ((), (), s32[]{:S(2)}) async-start(), calls=%async_computation.9 | async-start | bytes 11280384 | tf_op jit(solution)/shard_map/reduce_scatter | solution.py:529
  269.6 86.9 %copy-start.17 = (bf16[1024,768]{1,0:T(8,128)(2,1)S(1)}, bf16[1024,768]{1,0:T(8,128)(2,1)}, u32[]{:S(2)}) copy-start(bf16[1024,768]{1,0:T(8,128)(2,1)} %get-tuple-element.35) | copy-start | bytes 4718596
  388.7 32.3 %all-to-all-start.3 = ((bf16[16,2,24576]{2,1,0:T(2,128)(2,1)}), bf16[16,2,24576]{2,1,0:T(2,128)(2,1)}, u32[]{:S(2)}, u32[]{:S(2)}) async-start(bf16[16,2,24576]{2,1,0:T(2,128)(2,1)} %reshape.95), calls=%async_computation.3 | async-start | bytes 3145728 | tf_op jit(solution)/shard_map/all_to_all | solution.py:508
  413.2 14.9 %copy-start.1 = (f32[4,8,1792]{2,1,0:T(8,128)S(1)}, f32[4,8,1792]{2,1,0:T(8,128)}, u32[]{:S(2)}) copy-start(f32[4,8,1792]{2,1,0:T(8,128)} %get-tuple-element.37) | copy-start | bytes 688132
  421.0 339.2 %all-to-all-start.1 = ((bf16[16,2,24576]{2,1,0:T(2,128)(2,1)}), bf16[16,2,24576]{2,1,0:T(2,128)(2,1)}, u32[]{:S(2)}, u32[]{:S(2)}) async-start(bf16[16,2,24576]{2,1,0:T(2,128)(2,1)} %reshape.93), calls=%async_computation.1 | async-start | bytes 3145728 | tf_op jit(solution)/shard_map/all_to_all | solution.py:508
  428.0 205.5 %copy-start.4 = (f32[8,1536]{1,0:T(8,128)S(1)}, f32[8,1536]{1,0:T(8,128)}, u32[]{:S(2)}) copy-start(f32[8,1536]{1,0:T(8,128)} %get-tuple-element.40) | copy-start | bytes 147460
  428.0 318.8 %reduce-scatter.10.cloned.1.call-start = ((), (), s32[]{:S(2)}) async-start(), calls=%async_computation.11 | async-start | bytes 974848
  428.1 205.6 %copy-start.2 = (f32[8,1792]{1,0:T(8,128)S(1)}, f32[8,1792]{1,0:T(8,128)}, u32[]{:S(2)}) copy-start(f32[8,1792]{1,0:T(8,128)} %get-tuple-element.38) | copy-start | bytes 172036
  428.2 205.6 %copy-start.3 = (f32[8,1536]{1,0:T(8,128)S(1)}, f32[8,1536]{1,0:T(8,128)}, u32[]{:S(2)}) copy-start(f32[8,1536]{1,0:T(8,128)} %get-tuple-element.41) | copy-start | bytes 147460
  428.2 205.6 %copy-start.5 = (f32[8,768]{1,0:T(8,128)S(1)}, f32[8,768]{1,0:T(8,128)}, u32[]{:S(2)}) copy-start(f32[8,768]{1,0:T(8,128)} %get-tuple-element.34) | copy-start | bytes 73732
  428.2 281.2 %copy-start.6 = (f32[16,128]{1,0:T(8,128)S(1)}, f32[16,128]{1,0:T(8,128)}, u32[]{:S(2)}) copy-start(f32[16,128]{1,0:T(8,128)} %get-tuple-element.39) | copy-start | bytes 24580
  429.5 340.2 %all-reduce.14.cloned.1.call-start = ((), (), s32[]{:S(2)}) async-start(), calls=%async_computation.12 | async-start | bytes 1916928 | tf_op jit(solution)/shard_map/psum | solution.py:529
Sparse Core Ops, SparseCore 0:
  10.8 83.8 all-gather.5
  97.5 87.9 all-gather.3
  269.2 148.4 reduce-scatter.7
  424.4 207.0 reduce-scatter.5
  634.2 77.0 reduce-scatter.9
  713.7 15.8 all-reduce.13

commit v2 on v1

--- a/solution.py
+++ b/solution.py
@@ -193,7 +193,7 @@
 def backward_kernel(
     len_ref, cot_ref, tok_ref, w_ref, ow_ref, nw_ref, cw_ref, cb_ref, sb_ref, dl_ref, sk_ref, gn_ref,
     cin_ref, gr_ref, mx_ref, st_ref, sr_ref,
-    ig_ref, gp_ref, taps_ref, gcb_ref, ggn_ref, gsk_ref, gnw_ref, ghd_ref,
+    ig_ref, gp_ref, gb_ref, taps_ref, gcb_ref, ggn_ref, gsk_ref, gnw_ref, ghd_ref,
     ws, col_s, pair_t, row_t, later, scores, grad_scores, gg, sig, gpre, args, acc_q, acc_k, acc_u, acc_v, acc_l,
 ):
     step_id = pl.program_id(0)
@@ -212,6 +212,7 @@
     width = cot_ref.shape[1]
     positions = offset + lax.broadcasted_iota(jnp.int32, (SPAN, width), 0)
     grad_branch = jnp.where(positions < len_ref[0], cot_ref[...].astype(F32), 0.0).astype(BF16)
+    gb_ref[...] = grad_branch
     for n in range(0, DI, 256):
         gg[:, n : n + 256] = mul_nt(grad_branch, ow_ref[n : n + 256, :])
 
@@ -446,10 +447,10 @@
     proj = DI + XBC + HEADS
     last = count - 1
     shapes = [
-        ((length, width), BF16), ((length, proj), BF16), ((CONV, EDGE, XBC), F32), ((EDGE, XBC), F32), ((EDGE, DI), F32),
+        ((length, width), BF16), ((length, proj), BF16), ((length, width), BF16), ((CONV, EDGE, XBC), F32), ((EDGE, XBC), F32), ((EDGE, DI), F32),
         ((EDGE, DI), F32), ((EDGE, width), F32), ((2 * EDGE, TILE), F32),
     ]
-    out_specs = [rows_of(width, last), rows_of(proj, last), *(whole(s) for s, _ in shapes[2:])]
+    out_specs = [rows_of(width, last), rows_of(proj, last), rows_of(width, last), *(whole(s) for s, _ in shapes[3:])]
     kept_specs = [
         pl.BlockSpec((1, SPAN + EDGE, XBC), lambda i: (last - i, 0, 0)), rows_of(DI, last), rows_of(DI, last),
         pl.BlockSpec((1, STATE, DI), lambda i: (last - i, 0, 0)), rows_of(TILE, last),
@@ -488,6 +489,488 @@
     )
 
 
+MESH = pl.DeviceIdType.MESH
+PLANE = 4
+REP = 2
+CUTS = (1, 1, 1, 6, 11, 16)
+
+
+def gather_kernel(
+    n, tok_ref, in_ref, ow_ref, small_ref, seq_ref, inf_ref, owf_ref, smf_ref,
+    own, tok_s, tok_r, small_s, small_r, line_s, line_r, plane_s, plane_r, sib_s, sib_r,
+):
+    planes = n // PLANE
+    me = lax.axis_index("shard")
+    core = lax.axis_index("rep")
+    z, y, x = me // PLANE, (me // 2) % 2, me % 2
+    across = me + 1 - 2 * x
+    along = me + 2 - 4 * y
+    piece = tok_ref.shape[1]
+    arrays = ((in_ref, inf_ref), (ow_ref, owf_ref))
+
+    barrier = pltpu.get_barrier_semaphore()
+    for d in range(1, n):
+        pl.semaphore_signal(barrier, inc=1, device_id={"shard": lax.rem(me + d, n)}, device_id_type=MESH)
+    pl.semaphore_signal(barrier, inc=1, device_id={"rep": 1 - core}, device_id_type=MESH)
+    pl.semaphore_wait(barrier, n)
+
+    def region(a, k, part=None):
+        src, dst = arrays[a]
+        rows = src.shape[0] // REP
+        start = pl.multiple_of(k * src.shape[0] + core * rows, 8)
+        if part is None:
+            return dst.at[pl.ds(start, rows)]
+        half = src.shape[1] // 2 // TILE * TILE
+        cols = pl.ds(0, half) if part == 0 else pl.ds(half, src.shape[1] - half)
+        return dst.at[pl.ds(start, rows), cols]
+
+    def send(view, to, s, r):
+        return pltpu.make_async_remote_copy(
+            src_ref=view, dst_ref=view, send_sem=s, recv_sem=r, device_id=to, device_id_type=MESH
+        )
+
+    def line(a, origin, to):
+        return send(region(a, origin), {"shard": to}, line_s.at[a, origin // PLANE, (to > me).astype(jnp.int32)], line_r.at[a, origin // PLANE])
+
+    def hop(a, zz, kind):
+        here = zz * PLANE + 2 * y + x
+        side = zz * PLANE + 2 * y + 1 - x
+        ahead = zz * PLANE + 2 * (1 - y) + x
+        origin, part, to = (
+            (here, 0, across), (here, 1, along), (here, 0, along), (here, 1, across), (side, 0, along), (ahead, 1, across),
+        )[kind]
+        return send(region(a, origin, part), {"shard": to}, plane_s.at[a, zz, kind], plane_r.at[a, zz, kind])
+
+    def sibling(a, zz, kind):
+        origin = zz * PLANE + (2 * y + x, 2 * y + 1 - x, 2 * (1 - y) + x, 2 * (1 - y) + 1 - x)[kind]
+        return send(region(a, origin), {"rep": 1 - core}, sib_s.at[a, zz, kind], sib_r.at[a, zz, kind])
+
+    local = []
+    for a, (src, _) in enumerate(arrays):
+        rows = src.shape[0] // REP
+        start = pl.multiple_of(core * rows, 8)
+        copy = pltpu.make_async_copy(src.at[pl.ds(start, rows)], region(a, me), own.at[a])
+        copy.start()
+        local.append(copy)
+    copy = pltpu.make_async_copy(tok_ref.at[me], seq_ref.at[pl.ds(pl.multiple_of(me * piece, 8), piece)], own.at[2])
+    copy.start()
+    local.append(copy)
+    few = small_ref.shape[0]
+    mine = smf_ref.at[pl.ds(pl.multiple_of(me * few, 8), few)]
+    copy = pltpu.make_async_copy(small_ref, mine, own.at[3])
+    copy.start()
+    local.append(copy)
+    for copy in local:
+        copy.wait()
+
+    def launch(zz):
+        for a in range(2):
+            for kind in range(4):
+                hop(a, zz, kind).start()
+            sibling(a, zz, 0).start()
+
+    for a in range(2):
+        @pl.when(z + 1 < planes)
+        def _():
+            line(a, me, me + PLANE).start()
+
+        @pl.when(z > 0)
+        def _():
+            line(a, me, me - PLANE).start()
+    launch(z)
+    exchange = []
+
+    def tokens(first, last):
+        for d in range(first, last):
+            to = lax.rem(me + d, n)
+            copy = pltpu.make_async_remote_copy(
+                src_ref=tok_ref.at[to], dst_ref=seq_ref.at[pl.ds(pl.multiple_of(me * piece, 8), piece)],
+                send_sem=tok_s.at[d], recv_sem=tok_r.at[d], device_id={"shard": to}, device_id_type=MESH,
+            )
+            copy.start()
+            exchange.append(copy)
+
+    for d in range(1, n):
+        copy = send(mine, {"shard": lax.rem(me + d, n)}, small_s.at[d], small_r.at[d])
+        copy.start()
+        exchange.append(copy)
+    tokens(CUTS[0], CUTS[1])
+
+    def relay(zz):
+        for a in range(2):
+            hop(a, zz, 0).wait_recv()
+            hop(a, zz, 4).start()
+            hop(a, zz, 1).wait_recv()
+            hop(a, zz, 5).start()
+
+    def collect(zz):
+        for a in range(2):
+            hop(a, zz, 3).wait_recv()
+            sibling(a, zz, 1).start()
+            hop(a, zz, 2).wait_recv()
+            sibling(a, zz, 2).start()
+            hop(a, zz, 4).wait_recv()
+            hop(a, zz, 5).wait_recv()
+            sibling(a, zz, 3).start()
+
+    def each(d, step):
+        @pl.when(z - d >= 0)
+        def _():
+            step(z - d, me - d * PLANE, me + PLANE, z + 1 < planes)
+
+        @pl.when(z + d < planes)
+        def _():
+            step(z + d, me + d * PLANE, me - PLANE, z > 0)
+
+    def arrived(zz, origin, to, more):
+        for a in range(2):
+            line(a, origin, to).wait_recv()
+
+            @pl.when(more)
+            def _():
+                line(a, origin, to).start()
+        launch(zz)
+
+    for d in range(1, planes):
+        each(d, arrived)
+        if d == 1:
+            relay(z)
+        else:
+            each(d - 1, lambda zz, *_: relay(zz))
+        tokens(CUTS[d], CUTS[d + 1])
+    collect(z)
+    each(planes - 1, lambda zz, *_: relay(zz))
+    tokens(CUTS[4], CUTS[5])
+    for d in range(1, planes):
+        each(d, lambda zz, *_: collect(zz))
+
+    for copy in exchange:
+        copy.wait()
+    for zz in range(planes):
+        for a in range(2):
+            for kind in range(4):
+                sibling(a, zz, kind).wait()
+            for kind in range(6):
+                hop(a, zz, kind).wait_send()
+    for a in range(2):
+        def sent(zz, origin, to, more):
+            @pl.when(more)
+            def _():
+                line(a, origin, to).wait_send()
+
+        for d in range(1, planes):
+            each(d, sent)
+
+        @pl.when(z + 1 < planes)
+        def _():
+            line(a, me, me + PLANE).wait_send()
+
+        @pl.when(z > 0)
+        def _():
+            line(a, me, me - PLANE).wait_send()
+
+
+def run_gather(tokens, in_weight, out_weight, small):
+    n, piece, width = tokens.shape
+    planes = n // PLANE
+    hbm = pl.BlockSpec(memory_space=pl.ANY)
+    dma = pltpu.SemaphoreType.DMA
+    shapes = [
+        ((n * piece, width), tokens.dtype), ((n * in_weight.shape[0], in_weight.shape[1]), in_weight.dtype),
+        ((n * out_weight.shape[0], out_weight.shape[1]), out_weight.dtype), ((n * small.shape[0], TILE), small.dtype),
+    ]
+    return pl.pallas_call(
+        functools.partial(gather_kernel, n),
+        out_shape=[jax.ShapeDtypeStruct(s, d) for s, d in shapes],
+        in_specs=[hbm] * 4,
+        out_specs=[hbm] * 4,
+        scratch_shapes=[
+            dma((4,)), dma((n,)), dma((n,)), dma((n,)), dma((n,)), dma((2, planes, 2)), dma((2, planes)),
+            dma((2, planes, 6)), dma((2, planes, 6)), dma((2, planes, 4)), dma((2, planes, 4)),
+        ],
+        compiler_params=pltpu.CompilerParams(collective_id=0, has_side_effects=True),
+    )(tokens, in_weight, out_weight, small)
+
+
+PARTS = (
+    (1, 0, 384, 0), (1, 384, 384, 1), (0, 0, 768, 0), (0, 768, 768, 1), (0, 1536, 896, 0), (0, 2432, 920, 1),
+)
+SPREAD = (0, 4, 8, 12, 15)
+
+
+def scatter_kernel(n, *refs):
+    (
+        ig_ref, nl_ref, gp_ref, gl_ref, gb_ref, small_ref,
+        slot_ref, gin_ref, gout_ref, sum_ref,
+    ) = refs[:10]
+    refs = refs[10:]
+    count = len(PARTS)
+    bufs = [refs[i * 7 : (i + 1) * 7] for i in range(count)]
+    (
+        nl_t, gl_t, few, few_sib, own, ig_s, ig_r, few_s, few_r, pair_s, pair_r, s0s, s0r, s1s, s1r, s2s, s2r, s3s, s3r, s4s, s4r,
+    ) = refs[count * 7 :]
+    planes = n // PLANE
+    me = lax.axis_index("shard")
+    core = lax.axis_index("rep")
+    z, y, x = me // PLANE, (me // 2) % 2, me % 2
+    across = {"shard": me + 1 - 2 * x}
+    along = {"shard": me + 2 - 4 * y}
+    twin = {"rep": 1 - core}
+    piece = slot_ref.shape[1]
+
+    barrier = pltpu.get_barrier_semaphore()
+    for d in range(1, n):
+        pl.semaphore_signal(barrier, inc=1, device_id={"shard": lax.rem(me + d, n)}, device_id_type=MESH)
+    pl.semaphore_signal(barrier, inc=1, device_id=twin, device_id_type=MESH)
+
+    def remote(src, dst, s, r, to):
+        return pltpu.make_async_remote_copy(
+            src_ref=src, dst_ref=dst, send_sem=s, recv_sem=r, device_id=to, device_id_type=MESH
+        )
+
+    def ig_copy(d):
+        to = lax.rem(me + d, n)
+        src = ig_ref.at[pl.ds(pl.multiple_of(to * piece, 8), piece)]
+        return remote(src, slot_ref.at[me], ig_s.at[d], ig_r.at[d], {"shard": to})
+
+    def few_copy(d):
+        to = lax.rem(me + d, n)
+        return remote(small_ref.at[to], few.at[me], few_s.at[d], few_r.at[d], {"shard": to})
+
+    first = core == 0
+
+    def product(p):
+        a, start, size, _ = PARTS[p]
+        acc, s0 = bufs[p][0], bufs[p][1]
+        left, right = (nl_t, gp_ref) if a == 0 else (gl_t, gb_ref)
+        rows = acc.shape[3]
+        for c in range(0, size, 256):
+            wide = min(256, size - c)
+            total = mul(left[...], right[:, start + c : start + c + wide])
+            total = total.reshape(planes, 2, 2, 2, rows, wide)
+            acc[:, :, :, :, c : c + wide] = jnp.where(first, total[:, :, :, 0], total[:, :, :, 1])
+            s0[:, :, :, :, c : c + wide] = jnp.where(first, total[:, :, :, 1], total[:, :, :, 0]).astype(BF16)
+
+    def c0(p):
+        return remote(bufs[p][1], bufs[p][2], s0s.at[p], s0r.at[p], twin)
+
+    def c1(p):
+        sb, r1 = bufs[p][3], bufs[p][4]
+        if PARTS[p][3] == 0:
+            return remote(sb.at[:, 1 - y], r1, s1s.at[p], s1r.at[p], along)
+        return remote(sb.at[:, :, 1 - x], r1, s1s.at[p], s1r.at[p], across)
+
+    def c2(p):
+        sb, r2 = bufs[p][3], bufs[p][5]
+        if PARTS[p][3] == 0:
+            return remote(sb.at[:, y, 1 - x], r2, s2s.at[p], s2r.at[p], across)
+        return remote(sb.at[:, 1 - y, x], r2, s2s.at[p], s2r.at[p], along)
+
+    def c3(p, dest, up):
+        sb, r3 = bufs[p][3], bufs[p][6]
+        to = {"shard": me + PLANE if up else me - PLANE}
+        return remote(sb.at[dest, y, x], r3.at[int(up), dest], s3s.at[p, dest], s3r.at[p, int(up), dest], to)
+
+    def into_half(p):
+        acc, _, r0, sb = bufs[p][:4]
+        c0(p).wait_recv()
+
+        def step(i, carry):
+            zz, yy, xx = i // PLANE, (i // 2) % 2, i % 2
+            value = acc[zz, yy, xx] + r0[zz, yy, xx].astype(F32)
+            acc[zz, yy, xx] = value
+            sb[zz, yy, xx] = value.astype(BF16)
+            return carry
+
+        lax.fori_loop(0, n, step, 0)
+
+    def after_first(p):
+        acc, _, _, sb, r1 = bufs[p][:5]
+        c1(p).wait_recv()
+        c1(p).wait_send()
+
+        def step(i, carry):
+            zz, kk = i // 2, i % 2
+            at = (zz, y, kk) if PARTS[p][3] == 0 else (zz, kk, x)
+            value = acc[at] + r1[zz, kk].astype(F32)
+            acc[at] = value
+            sb[at] = value.astype(BF16)
+            return carry
+
+        lax.fori_loop(0, 2 * planes, step, 0)
+
+    def after_second(p):
+        acc, _, _, sb, _, r2 = bufs[p][:6]
+        c2(p).wait_recv()
+        c2(p).wait_send()
+        for zz in range(planes):
+            value = acc[zz, y, x] + r2[zz].astype(F32)
+            acc[zz, y, x] = value
+            sb[zz, y, x] = value.astype(BF16)
+
+    def line(p):
+        acc, sb, r3 = bufs[p][0], bufs[p][3], bufs[p][6]
+        for i in range(planes - 1):
+            for up in (True, False):
+                dest = planes - 1 - i if up else i
+                beyond = dest > z if up else dest < z
+                more = z > 0 if up else z + 1 < planes
+
+                @pl.when(beyond)
+                def _():
+                    @pl.when(more)
+                    def _():
+                        c3(p, dest, up).wait_recv()
+                        value = acc[dest, y, x] + r3[int(up), dest].astype(F32)
+                        sb[dest, y, x] = value.astype(BF16)
+
+                    c3(p, dest, up).start()
+
+    def results(p):
+        a, start, size, _ = PARTS[p]
+        acc = bufs[p][0]
+        out = gin_ref if a == 0 else gout_ref
+        rows = acc.shape[3]
+        view = out.at[pl.ds(pl.multiple_of(core * rows, 8), rows), pl.ds(start, size)]
+        return (
+            remote(acc.at[z, y, x], view, s4s.at[p], s4r.at[p], twin),
+            pltpu.make_async_copy(acc.at[z, y, x], view, own.at[p]),
+        )
+
+    def arrivals(p, up):
+        r3 = bufs[p][6]
+        return remote(bufs[p][3].at[z, y, x], r3.at[int(up), z], s3s.at[p, z], s3r.at[p, int(up), z], along)
+
+    def finish(p):
+        acc, r3 = bufs[p][0], bufs[p][6]
+        for up in (True, False):
+            @pl.when(z > 0 if up else z + 1 < planes)
+            def _():
+                arrivals(p, up).wait_recv()
+                acc[z, y, x] += r3[int(up), z].astype(F32)
+
+        for copy in results(p):
+            copy.start()
+
+    def igs(i):
+        for d in range(1 + SPREAD[i], 1 + SPREAD[i + 1]):
+            ig_copy(d).start()
+
+    units = [(0, 1), (2, 3), (4, 5)]
+    gl_t[...] = gl_ref[...].T
+    for p in units[0]:
+        product(p)
+    pl.semaphore_wait(barrier, n)
+    for p in units[0]:
+        c0(p).start()
+    for d in range(1, n):
+        few_copy(d).start()
+    igs(0)
+    own_slot = pltpu.make_async_copy(
+        ig_ref.at[pl.ds(pl.multiple_of(me * piece, 8), piece)], slot_ref.at[me], own.at[count]
+    )
+    own_slot.start()
+    nl_t[...] = nl_ref[...].T
+
+    def stage(fn, start, u):
+        for p in units[u]:
+            fn(p)
+            if start is not None:
+                start(p).start()
+
+    for p in units[1]:
+        product(p)
+        c0(p).start()
+    stage(into_half, c1, 0)
+    for p in units[2]:
+        product(p)
+        c0(p).start()
+    stage(into_half, c1, 1)
+    igs(1)
+    stage(after_first, c2, 0)
+    stage(into_half, c1, 2)
+    igs(2)
+    stage(after_second, None, 0)
+    stage(line, None, 0)
+    stage(after_first, c2, 1)
+    igs(3)
+    stage(after_second, None, 1)
+    stage(line, None, 1)
+    stage(finish, None, 0)
+    stage(after_first, c2, 2)
+    stage(finish, None, 1)
+    few[me] = small_ref[me]
+    for d in range(1, n):
+        few_copy(d).wait()
+    total = few[0]
+    for k in range(1, n):
+        total = total + few[k]
+    few_sib[0] = total
+    pair = remote(few_sib.at[0], few_sib.at[1], pair_s, pair_r, twin)
+    pair.start()
+    stage(after_second, None, 2)
+    stage(line, None, 2)
+    stage(finish, None, 2)
+    pair.wait()
+    sum_ref[...] = few_sib[0] + few_sib[1]
+    own_slot.wait()
+    for d in range(1, n):
+        ig_copy(d).wait()
+    for p in range(count):
+        c0(p).wait_send()
+        for i in range(planes - 1):
+            for up in (True, False):
+                dest = planes - 1 - i if up else i
+
+                @pl.when(dest > z if up else dest < z)
+                def _():
+                    c3(p, dest, up).wait_send()
+
+        far, near = results(p)
+        near.wait()
+        far.wait()
+
+
+def run_scatter(n, ig, normed, gp, gate_low, grad_branch, small):
+    length, width = ig.shape
+    piece = length // n
+    planes = n // PLANE
+    proj = gp.shape[1]
+    inner = gate_low.shape[1]
+    vmem = pl.BlockSpec(memory_space=pltpu.VMEM)
+    hbm = pl.BlockSpec(memory_space=pl.ANY)
+    dma = pltpu.SemaphoreType.DMA
+    scratch = []
+    for a, _, size, _ in PARTS:
+        rows = (width if a == 0 else inner) // n // REP
+        full = (planes, 2, 2, rows, size)
+        scratch += [
+            pltpu.VMEM(full, F32), pltpu.VMEM(full, BF16), pltpu.VMEM(full, BF16), pltpu.VMEM(full, BF16),
+            pltpu.VMEM((planes, 2, rows, size), BF16), pltpu.VMEM((planes, rows, size), BF16), pltpu.VMEM((2, planes, rows, size), BF16),
+        ]
+    count = len(PARTS)
+    few = small.shape[1:]
+    scratch += [
+        pltpu.VMEM((width, length), BF16), pltpu.VMEM((inner, length), BF16), pltpu.VMEM((n, *few), F32), pltpu.VMEM((2, *few), F32),
+        dma((count + 1,)), dma((n,)), dma((n,)), dma((n,)), dma((n,)), dma(()), dma(()),
+        *(dma((count,)) for _ in range(6)), dma((count, planes)), dma((count, 2, planes)), dma((count,)), dma((count,)),
+    ]
+    shapes = [
+        ((n, piece, width), BF16), ((width // n, proj), F32), ((inner // n, width), F32), (few, F32),
+    ]
+    return pl.pallas_call(
+        functools.partial(scatter_kernel, n),
+        out_shape=[jax.ShapeDtypeStruct(s, d) for s, d in shapes],
+        in_specs=[hbm, vmem, vmem, vmem, vmem, vmem],
+        out_specs=[hbm, hbm, hbm, vmem],
+        scratch_shapes=scratch,
+        compiler_params=pltpu.CompilerParams(collective_id=1, has_side_effects=True, vmem_limit_bytes=LIMIT),
+    )(ig, normed, gp, gate_low, grad_branch, small)
+
+
+FEW = EDGE * TILE
+
+
 def on_device(
     tokens, cotangent, lengths, order, norm_weight, in_weight, conv_weight, conv_bias,
     step_bias, decay_log, skip_gain, gate_norm_weight, out_weight,
@@ -504,38 +987,57 @@
         return lax.all_to_all(parts, "shard", split_axis=0, concat_axis=2, tiled=True).reshape(peers * piece, width)
 
     def to_slots(x):
-        parts = x.reshape(1, peers * piece, width)
-        return lax.all_to_all(parts, "shard", split_axis=1, concat_axis=0, tiled=True)
+        parts = x.reshape(peers, piece, width)
+        return lax.all_to_all(parts, "shard", split_axis=0, concat_axis=0, tiled=True)
 
     slots = jnp.arange(peers, dtype=jnp.int32)
     sequence = jnp.sum(jnp.where(slots == rank, order[0], 0))
     valid = jnp.sum(jnp.where(slots == sequence, lengths[0], 0))[None]
-    tok = to_sequences(tokens)
+    direct = peers == PLANE * PLANE and lax.axis_size("rep") == REP and piece % 16 == 0
+    sizes = [v.size for v in (norm_weight, conv_weight, conv_bias, gate_norm_weight)]
+    if direct:
+        few = jnp.concatenate([v.astype(F32).reshape(-1) for v in (norm_weight, conv_weight, conv_bias, gate_norm_weight)])
+        few = jnp.pad(few, (0, FEW - few.size)).reshape(EDGE, TILE)
+        tok, in_full, out_full, few = run_gather(tokens, in_weight, out_weight, few)
+        few = few.reshape(peers, FEW)
+        ends = [sum(sizes[: i + 1]) for i in range(4)]
+        norm_full, conv_full, shift_full, gate_full = (
+            few[:, e - s : e].reshape(-1) for s, e in zip(sizes, ends)
+        )
+        conv_full = conv_full.reshape(XBC, CONV)
+    else:
+        tok = to_sequences(tokens)
+        norm_full, in_full, conv_full = gather(norm_weight), gather(in_weight), gather(conv_weight)
+        shift_full, gate_full, out_full = gather(conv_bias), gather(gate_norm_weight), gather(out_weight)
     cot = to_sequences(cotangent)
-    params = prepare(
-        gather(norm_weight), gather(in_weight), gather(conv_weight), gather(conv_bias),
-        gather(gate_norm_weight), gather(out_weight), step_bias, decay_log, skip_gain,
-    )
+    params = prepare(norm_full, in_full, conv_full, shift_full, gate_full, out_full, step_bias, decay_log, skip_gain)
     out, cin, gr, mx, st, sr, normed, gate_low = run_forward(valid, tok, params)
     output = to_slots(out)
-    ig, gp, taps, gcb, ggn, gsk, gnw, ghd = run_backward(valid, cot, tok, params, (cin, gr, mx, st, sr))
-    input_grad = to_slots(ig)
-    keep = jnp.arange(peers * piece, dtype=jnp.int32)[:, None] < valid[0]
-    grad_branch = jnp.where(keep, cot, jnp.zeros_like(cot))
-    grad_out = mul_tn(gate_low, grad_branch)
-    grad_in = mul_tn(normed, gp)
-
-    def scatter(x):
-        return lax.psum(lax.psum_scatter(x, "shard", scatter_dimension=0, tiled=True), "rep")
-
+    ig, gp, gb, taps, gcb, ggn, gsk, gnw, ghd = run_backward(valid, cot, tok, params, (cin, gr, mx, st, sr))
+    few = [jnp.sum(gnw, axis=0), jnp.sum(taps, axis=1).T, jnp.sum(gcb, axis=0), jnp.sum(ggn, axis=0)]
     heads = jnp.stack([
         jnp.sum(ghd[:EDGE], axis=0)[:HEADS], jnp.sum(ghd[EDGE:], axis=0)[:HEADS],
         jnp.sum(gsk.reshape(EDGE, HEADS, HEADDIM), axis=(0, 2)),
     ])
-    heads = lax.psum(heads, ("rep", "shard"))
+    if direct:
+        rows = [v.reshape(peers, -1) for v in few] + [jnp.broadcast_to(heads.reshape(1, -1), (peers, heads.size))]
+        few = jnp.concatenate(rows, axis=1)
+        few = jnp.pad(few, ((0, 0), (0, FEW - few.shape[1]))).reshape(peers, EDGE, TILE)
+        input_grad, grad_in, grad_out, few = run_scatter(peers, ig, normed, gp, gate_low, gb, few)
+        few = few.reshape(-1)
+        few, heads = [few[e - s : e] for s, e in zip(sizes, ends)], few[ends[3] : ends[3] + heads.size].reshape(heads.shape)
+        few[1] = few[1].reshape(-1, CONV)
+    else:
+        input_grad = to_slots(ig)
+
+        def scatter(v):
+            return lax.psum(lax.psum_scatter(v, "shard", scatter_dimension=0, tiled=True), "rep")
+
+        few = [scatter(v) for v in few]
+        grad_in, grad_out = scatter(mul_tn(normed, gp)), scatter(mul_tn(gate_low, gb))
+        heads = lax.psum(heads, ("rep", "shard"))
     return (
-        output, input_grad, scatter(jnp.sum(gnw, axis=0)), scatter(grad_in), scatter(jnp.sum(taps, axis=1).T),
-        scatter(jnp.sum(gcb, axis=0)), heads[0], heads[1], heads[2], scatter(jnp.sum(ggn, axis=0)), scatter(grad_out),
+        output, input_grad, few[0], grad_in, few[1], few[2], heads[0], heads[1], heads[2], few[3], grad_out,
     )
 
 

time: 791 us -> 376 us (0.48); the launches traced: 781 us -> 375 us
  blocking collectives: 307 us -> 0 us
  waiting for transfers between devices: 211 us -> 0.01 us
  Pallas kernels: 134 us -> 327 us
  local copies, waits for them, and re-layouts: 48.6 us -> 21.1 us
  matrix products: 19 us -> 0 us
  other arithmetic: 26.1 us -> 7.65 us
  between operations: 18.8 us -> 0.91 us
    reduce_scatter x2 -> x0, waiting for transfers between devices: 202 us -> none  [scatter(): lax.psum_scatter(x, 'shard', scatter_dimension=0, tiled=True)]
    pallas_call x0 -> x2, Pallas kernels: none -> 193 us  [the longest x1 103 us: run_scatter(): pl.pallas_call(functools.partial(scatter_kernel, n), out_shape=[jax.Shape...]
    unnamed x2 -> x0, blocking collectives: 176 us -> none
    all_to_all x1 -> x0, blocking collectives: 55.5 us -> none  [to_sequences(): lax.all_to_all(parts, 'shard', split_axis=0, concat_axis=2, tiled=True)]
    psum x2 -> x0, blocking collectives: 39.9 us -> none  [the longest x1 36.9 us: on_device(): heads = lax.psum(heads, ('rep', 'shard'))]
    all_gather x1 -> x0, blocking collectives: 36 us -> none  [gather(): return lax.all_gather(x, 'shard', axis=0, tiled=True)]
    unnamed x57 -> x34, local copies, waits for them, and re-layouts: 36.1 us -> 7.72 us
    unnamed x2 -> x0, other arithmetic: 23.2 us -> none
  transfers between devices with their start and end apart: 9 -> 2, of which waited for: 2 -> 0; matrix products, arithmetic and copies ran while one was open for 11% -> 6% of each run, Pallas kernels for 17% -> 87%
where the time goes in v2:
time: 376 us; the launch traced here: 375 us
  Pallas kernels  327 us (87%)
  local copies, waits for them, and re-layouts  21.1 us (6%)
  starting transfers between devices  18.2 us (5%)
  other arithmetic  7.65 us (2%)
    pallas_call x1, Pallas kernels, run_scatter(): pl.pallas_call(functools.partial(scatter_kernel, n), out_shape=[jax.Shape...  103 us
    pallas_call x1, Pallas kernels, run_gather(): pl.pallas_call(functools.partial(gather_kernel, n), out_shape=[jax.ShapeD...  90.3 us
    pallas_call x1, Pallas kernels, run_backward(): pl.pallas_call(backward_kernel, grid=(count,), out_shape=[jax.ShapeDtypeS...  87.2 us
    pallas_call x1, Pallas kernels, run_forward(): pl.pallas_call(forward_kernel, grid=(count,), out_shape=[jax.ShapeDtypeSt...  46.9 us
    all_to_all x1, starting transfers between devices, to_slots(): lax.all_to_all(parts, 'shard', split_axis=0, concat_axis=0, tiled=True)  9.73 us
    all_to_all x1, starting transfers between devices, to_sequences(): lax.all_to_all(parts, 'shard', split_axis=0, concat_axis=2, tiled=True)  8.46 us
    unnamed x34, local copies, waits for them, and re-layouts  7.72 us
  transfers between devices with their start and end apart: 2, of which 0 were waited for; matrix products, arithmetic and copies ran while one was open for 6% of the time, Pallas kernels for 87%

profile of v2, /device:TPU:0, one launch (start us, length us, event | category | flops | bytes accessed | tf_op | source)
XLA Modules:
  0.0 375.0 jit_solution(11041489009219364484)
XLA Ops:
  0.7 8.5 %all-to-all-start.1 = ((bf16[16,1,64,768]{3,2,1,0:T(8,128)(2,1)}), bf16[16,1,64,768]{3,2,1,0:T(8,128)(2,1)S(1)}, u32[]{:S(2)}, u32[]{:S(2)}) async-start(bf16[16,1,64,768]{3,2,1,0:T(8,128)(2,1)} %bitcast.26), calls=%async_computation.1 | async-start | bytes 3145728 | tf_op jit(solution)/shard_map/all_to_all | solution.py:987
  9.1 0.0 copy-start.9
  9.2 0.0 copy-start.10
  9.2 0.0 copy-start.5
  9.2 0.0 copy-done.4
  9.2 0.1 copy.32
  9.3 0.1 reshape.79
  9.5 0.7 fusion.8.small_ref
  10.1 90.3 %shard_map.212 = (bf16[1024,768]{1,0:T(8,128)(2,1)}, bf16[768,3352]{1,0:T(8,128)(2,1)}, bf16[1536,768]{1,0:T(8,128)(2,1)}, f32[128,128]{1,0:T(8,128)}) custom-call(bf16[16,64,768]{2,1,0:T(8,128)(2,1)} %tok_ref.1, bf16[48,3352]{1,0:T(8,128)(2,1)} %in_ref.1, bf16[96,768]{1,0:T(8,128)(2,1)} %ow_ref.1, f32[8,128]{1,0:T(8,128)} %fusion.8.small_ref), custom_call_target="tpu_custom_call" | custom-call | tf_op jit(solution)/shard_map/pallas_call | solution.py:682
  100.5 0.0 copy-start.11
  100.5 0.0 copy-start.12
  100.5 0.9 reshape.82
  101.4 0.1 slice.74
  101.5 0.1 slice.73
  101.5 0.1 slice.72
  101.6 0.0 copy-done.9
  101.6 0.5 pad.17.sb_ref
  102.1 0.5 pad.18.dl_ref
  102.6 0.1 broadcast_in_dim.28
  102.7 0.7 broadcast_in_dim_reshape.14.sk_ref
  103.4 0.7 broadcast_in_dim_reshape.15.gn_ref
  104.1 0.7 broadcast_in_dim_reshape.13.cb_ref
  104.7 0.7 broadcast_in_dim_reshape.12.nw_ref
  105.4 0.5 reshape_reshape.3
  105.9 0.9 copy.33
  106.8 0.0 copy-done.11
  106.8 0.6 fusion.9
  107.4 1.3 fusion.10
  108.7 46.9 %shard_map.213 = (bf16[1024,768]{1,0:T(8,128)(2,1)}, f32[4,264,1792]{2,1,0:T(8,128)}, f32[1024,1536]{1,0:T(8,128)}, f32[1024,1536]{1,0:T(8,128)}, f32[4,128,1536...) custom-call(s32[1]{0:T(128)} %bitcast.2.len_ref, ...), custom_call_target="tpu_custom_call" | custom-call | flops 20000000000 | bytes 60000000 | tf_op jit(solution)/shard_map/pallas_call | solution.py:429
  155.6 0.0 all-to-all-done.1
  155.6 0.0 copy-start
  155.6 1.2 copy-done
  156.8 9.7 %all-to-all-start = ((bf16[16,64,768]{2,1,0:T(8,128)(2,1)}), bf16[16,64,768]{2,1,0:T(8,128)(2,1)S(1)}, u32[]{:S(2)}, u32[]{:S(2)}) async-start(bf16[16,64,768]{2,1,0:T(8,128)(2,1)} %bitcast.27), calls=%async_computation | async-start | bytes 3145728 | tf_op jit(solution)/shard_map/all_to_all | solution.py:991
  166.5 87.2 %shard_map.214 = (bf16[1024,768]{1,0:T(8,128)(2,1)}, bf16[1024,3352]{1,0:T(8,128)(2,1)}, bf16[1024,768]{1,0:T(8,128)(2,1)}, f32[4,8,1792]{2,1,0:T(8,128)}, f32[8...) custom-call(s32[1]{0:T(128)} %bitcast.2.len_ref, ...), custom_call_target="tpu_custom_call" | custom-call | flops 40000000000 | bytes 60000000 | tf_op jit(solution)/shard_map/pallas_call | solution.py:460
  253.7 0.8 reduce_sum.90
  254.5 0.1 reshape.86
  254.6 0.8 reduce_sum.92
  255.4 0.1 reshape.88
  255.5 0.8 reduce_sum.93
  256.3 0.1 reshape.89
  256.4 0.8 reduce_sum.96
  257.2 0.1 reduce_sum.97
  257.3 0.1 reduce_sum.98
  257.4 1.0 reduce_sum.91
  258.4 0.7 slice_reduce_fusion.1
  259.1 0.1 broadcast_in_dim.29
  259.2 0.3 copy.34
  259.5 0.4 reshape.87
  259.9 0.1 concatenate.8
  260.1 0.6 copy.36
  260.7 102.6 %shard_map.215 = (bf16[16,64,768]{2,1,0:T(8,128)(2,1)}, f32[48,3352]{1,0:T(8,128)}, f32[96,768]{1,0:T(8,128)}, f32[8,128]{1,0:T(8,128)}) custom-call(bf16[1024,768]{1,0:T(8,128)(2,1)} %get-tuple-element.46.refs_0_, bf16[1024,768]{1,0:T(8,128)(2,1)} %get-tuple-element.47.refs_1_, bf16[1024,3352]{1,0:T(8,128)(2,1)} %get-tuple-element.48.refs_2_, ...), custom_call_target="tpu_custom_call" | custom-call | tf_op jit(solution)/shard_map/pallas_call | solution.py:961
  363.3 1.3 slice.70
  364.6 1.3 slice.66
  365.8 1.2 slice.63
  367.0 0.8 slice.64
  367.9 0.7 copy.35
  368.5 1.4 fusion.11
  369.9 0.0 all-to-all-done
  369.9 1.1 copy.41
  371.0 0.8 copy-done.1
  371.9 1.1 copy.42
  373.0 0.4 copy-done.2
  373.4 0.8 copy.43
  374.2 0.7 copy.44
  (20 shorter events, 0.1 us)
Async XLA Ops:
  0.6 8.5 %copy-start.4 = (bf16[112,4]{0,1:T(4,128)(2,1)S(1)}, bf16[112,4]{0,1:T(4,128)(2,1)}, u32[]{:S(2)}) copy-start(bf16[112,4]{0,1:T(4,128)(2,1)} %param.19) | copy-start | bytes 2692
  0.7 8.8 %copy-start.6 = (bf16[96]{0:T(256)(128)(2,1)S(1)}, bf16[96]{0:T(256)(128)(2,1)}, u32[]{:S(2)}) copy-start(bf16[96]{0:T(256)(128)(2,1)} %param.24) | copy-start | bytes 580
  0.7 8.8 %copy-start.7 = (bf16[112]{0:T(256)(128)(2,1)S(1)}, bf16[112]{0:T(256)(128)(2,1)}, u32[]{:S(2)}) copy-start(bf16[112]{0:T(256)(128)(2,1)} %param.20) | copy-start | bytes 676
  0.7 8.8 %copy-start.8 = (bf16[48]{0:T(256)(128)(2,1)S(1)}, bf16[48]{0:T(256)(128)(2,1)}, u32[]{:S(2)}) copy-start(bf16[48]{0:T(256)(128)(2,1)} %param.17) | copy-start | bytes 292
  0.7 154.9 %all-to-all-start.1 = ((bf16[16,1,64,768]{3,2,1,0:T(8,128)(2,1)}), bf16[16,1,64,768]{3,2,1,0:T(8,128)(2,1)S(1)}, u32[]{:S(2)}, u32[]{:S(2)}) async-start(bf16[16,1,64,768]{3,2,1,0:T(8,128)(2,1)} %bitcast.26), calls=%async_computation.1 | async-start | bytes 3145728 | tf_op jit(solution)/shard_map/all_to_all | solution.py:987
  9.1 92.5 %copy-start.9 = (f32[24]{0:T(128)S(1)}, f32[24]{0:T(128)}, u32[]{:S(2)}) copy-start(f32[24]{0:T(128)} %param.21) | copy-start | bytes 292
  9.2 93.0 %copy-start.10 = (f32[24]{0:T(128)S(1)}, f32[24]{0:T(128)}, u32[]{:S(2)}) copy-start(f32[24]{0:T(128)} %param.22) | copy-start | bytes 292
  9.2 93.5 %copy-start.5 = (f32[24]{0:T(128)S(1)}, f32[24]{0:T(128)}, u32[]{:S(2)}) copy-start(f32[24]{0:T(128)} %param.23) | copy-start | bytes 292
  100.5 6.3 %copy-start.11 = (s32[1,16]{1,0:T(1,128)S(1)}, s32[1,16]{1,0:T(1,128)}, u32[]{:S(2)}) copy-start(s32[1,16]{1,0:T(1,128)} %param.16) | copy-start | bytes 196
  100.5 6.9 %copy-start.12 = (s32[1,16]{1,0:T(1,128)S(1)}, s32[1,16]{1,0:T(1,128)}, u32[]{:S(2)}) copy-start(s32[1,16]{1,0:T(1,128)} %param.15) | copy-start | bytes 196
  155.6 1.2 copy-start
  156.8 213.1 %all-to-all-start = ((bf16[16,64,768]{2,1,0:T(8,128)(2,1)}), bf16[16,64,768]{2,1,0:T(8,128)(2,1)S(1)}, u32[]{:S(2)}, u32[]{:S(2)}) async-start(bf16[16,64,768]{2,1,0:T(8,128)(2,1)} %bitcast.27), calls=%async_computation | async-start | bytes 3145728 | tf_op jit(solution)/shard_map/all_to_all | solution.py:991
  369.9 2.0 copy-start.1
  371.9 1.5 copy-start.2
  371.9 2.4 copy-start.3

commit v3 on v2

--- a/solution.py
+++ b/solution.py
@@ -85,20 +85,19 @@
     return columns >= rows if flip else rows >= columns
 
 
-def forward_kernel(
-    len_ref, tok_ref, w_ref, ow_ref, nw_ref, cw_ref, cb_ref, sb_ref, dl_ref, sk_ref, gn_ref,
+def forward_start(w_ref, ws, state, cin_ref):
+    ws[...] = jnp.zeros_like(ws)
+    ws[:, :HEADS] = w_ref[:, DI + XBC : DI + XBC + HEADS]
+    state[...] = jnp.zeros_like(state)
+    cin_ref[0, :EDGE, :] = jnp.zeros((EDGE, XBC), F32)
+
+
+def forward_step(
+    block, len_ref, tok_ref, w_ref, ow_ref, nw_ref, cw_ref, cb_ref, sb_ref, dl_ref, sk_ref, gn_ref,
     out_ref, cin_ref, gr_ref, mx_ref, st_ref, sr_ref, nl_ref, gl_ref,
-    ws, col_t, pair_s, row_s, state, scores, gated,
+    ws, col_t, pair_s, row_s, state, scores, gated, hook=None,
 ):
-    block = pl.program_id(0)
     offset = block * SPAN
-
-    @pl.when(block == 0)
-    def _():
-        ws[...] = jnp.zeros_like(ws)
-        ws[:, :HEADS] = w_ref[:, DI + XBC : DI + XBC + HEADS]
-        state[...] = jnp.zeros_like(state)
-        cin_ref[0, :EDGE, :] = jnp.zeros((EDGE, XBC), F32)
 
     @pl.when(block > 0)
     def _():
@@ -136,6 +135,8 @@
 
     def pair(j, total):
         cols = tile_at(j)
+        if hook is not None:
+            hook(j)
         heads_in = act(j)
         heads_low = heads_in.astype(BF16)
         cum0, cum1 = col_t[2 * j], col_t[2 * j + 1]
@@ -188,6 +189,24 @@
         tok = tok_ref[:, n : n + 256].astype(F32)
         out_ref[:, n : n + 256] = (tok + jnp.where(valid, branch, 0.0)).astype(BF16)
     gated[:EDGE, :] = cin_ref[0, SPAN:, :]
+
+
+def forward_kernel(
+    len_ref, tok_ref, w_ref, ow_ref, nw_ref, cw_ref, cb_ref, sb_ref, dl_ref, sk_ref, gn_ref,
+    out_ref, cin_ref, gr_ref, mx_ref, st_ref, sr_ref, nl_ref, gl_ref,
+    ws, col_t, pair_s, row_s, state, scores, gated,
+):
+    block = pl.program_id(0)
+
+    @pl.when(block == 0)
+    def _():
+        forward_start(w_ref, ws, state, cin_ref)
+
+    forward_step(
+        block, len_ref, tok_ref, w_ref, ow_ref, nw_ref, cw_ref, cb_ref, sb_ref, dl_ref, sk_ref, gn_ref,
+        out_ref, cin_ref, gr_ref, mx_ref, st_ref, sr_ref, nl_ref, gl_ref,
+        ws, col_t, pair_s, row_s, state, scores, gated,
+    )
 
 
 def backward_kernel(
@@ -404,8 +423,7 @@
     return pl.BlockSpec((SPAN, width), lambda i: (last - i, 0))
 
 
-def params_specs(width):
-    proj = DI + XBC + HEADS
+def params_specs(width, proj):
     return [
         whole((width, proj)), whole((DI, width)), whole((1, width)), whole((CONV, XBC)), whole((1, XBC)),
         whole((1, TILE)), whole((1, TILE)), whole((1, DI)), whole((1, DI)),
@@ -415,8 +433,7 @@
 LIMIT = 60 * 2**20
 
 
-def run_forward(valid, tok, params):
-    length, width = tok.shape
+def forward_results(length, width):
     count = length // SPAN
     shapes = [
         ((length, width), BF16), ((count, SPAN + EDGE, XBC), F32), ((length, DI), F32), ((length, DI), F32),
@@ -426,16 +443,23 @@
         rows_of(width), pl.BlockSpec((1, SPAN + EDGE, XBC), lambda i: (i, 0, 0)), rows_of(DI), rows_of(DI),
         pl.BlockSpec((1, STATE, DI), lambda i: (i, 0, 0)), rows_of(TILE), rows_of(width), rows_of(DI),
     ]
+    scratch = [
+        pltpu.VMEM((width, TILE), BF16), pltpu.VMEM((HEADS, SPAN, TILE), F32), pltpu.VMEM((PAIRS, SPAN, TILE), F32),
+        pltpu.VMEM((TILE, SPAN), F32), pltpu.VMEM((STATE, DI), F32), pltpu.VMEM((SPAN, SPAN), F32), pltpu.VMEM((SPAN, XBC), F32),
+    ]
+    return [jax.ShapeDtypeStruct(s, d) for s, d in shapes], out_specs, scratch
+
+
+def run_forward(valid, tok, params):
+    length, width = tok.shape
+    shapes, out_specs, scratch = forward_results(length, width)
     return pl.pallas_call(
         forward_kernel,
-        grid=(count,),
-        out_shape=[jax.ShapeDtypeStruct(s, d) for s, d in shapes],
-        in_specs=[pl.BlockSpec(memory_space=pltpu.SMEM), rows_of(width), *params_specs(width)],
+        grid=(length // SPAN,),
+        out_shape=shapes,
+        in_specs=[pl.BlockSpec(memory_space=pltpu.SMEM), rows_of(width), *params_specs(width, params[0].shape[1])],
         out_specs=out_specs,
-        scratch_shapes=[
-            pltpu.VMEM((width, TILE), BF16), pltpu.VMEM((HEADS, SPAN, TILE), F32), pltpu.VMEM((PAIRS, SPAN, TILE), F32),
-            pltpu.VMEM((TILE, SPAN), F32), pltpu.VMEM((STATE, DI), F32), pltpu.VMEM((SPAN, SPAN), F32), pltpu.VMEM((SPAN, XBC), F32),
-        ],
+        scratch_shapes=scratch,
         compiler_params=pltpu.CompilerParams(dimension_semantics=("arbitrary",), vmem_limit_bytes=LIMIT),
         cost_estimate=pl.CostEstimate(flops=20 * 10**9, bytes_accessed=60 * 10**6, transcendentals=10**7),
     )(valid, tok, *params)
@@ -461,7 +485,7 @@
         backward_kernel,
         grid=(count,),
         out_shape=[jax.ShapeDtypeStruct(s, d) for s, d in shapes],
-        in_specs=[pl.BlockSpec(memory_space=pltpu.SMEM), rows_of(width, last), rows_of(width, last), *params_specs(width), *kept_specs],
+        in_specs=[pl.BlockSpec(memory_space=pltpu.SMEM), rows_of(width, last), rows_of(width, last), *params_specs(width, params[0].shape[1]), *kept_specs],
         out_specs=out_specs,
         scratch_shapes=[
             pltpu.VMEM((width, TILE), BF16), pltpu.VMEM((HEADS, SPAN, TILE), F32), pltpu.VMEM((PAIRS, SPAN, TILE), F32),
@@ -492,37 +516,42 @@
 MESH = pl.DeviceIdType.MESH
 PLANE = 4
 REP = 2
-CUTS = (1, 1, 1, 6, 11, 16)
-
-
-def gather_kernel(
-    n, tok_ref, in_ref, ow_ref, small_ref, seq_ref, inf_ref, owf_ref, smf_ref,
-    own, tok_s, tok_r, small_s, small_r, line_s, line_r, plane_s, plane_r, sib_s, sib_r,
-):
+COT_AT = 1
+
+
+def lay_out(few, n, nw_ref, cw_ref, cb_ref, gn_ref):
+    for ref, row in ((nw_ref, 0), (cw_ref, 1), (cb_ref, 1 + CONV), (gn_ref, 2 + CONV)):
+        size = ref.shape[1] // n
+        for k in range(n):
+            ref[:, k * size : (k + 1) * size] = few[k, row : row + ref.shape[0], :size]
+
+
+def gather_forward_kernel(n, *refs):
+    len_ref, tok_ref, cot_ref, in_ref, ow_ref, small_ref, head_ref = refs[:7]
+    blocks = refs[7:15]
+    seq_ref, cots_ref, inf_ref, owf_ref, nw_ref, cw_ref, cb_ref, sk_ref, gn_ref = refs[15:24]
+    own_scratch = refs[24:31]
+    (
+        tok_v, w_v, ow_v, few, tok_stage, cot_stage, own,
+        tok_s, tok_r, tok_fs, tok_fr, tok_l, cot_s, cot_r, cot_fs, cot_fr, cot_l, small_s, small_r, line_s, line_r, plane_s, plane_r, sib_s, sib_r, keep_s,
+    ) = refs[31:]
     planes = n // PLANE
+    block = pl.program_id(0)
     me = lax.axis_index("shard")
     core = lax.axis_index("rep")
     z, y, x = me // PLANE, (me // 2) % 2, me % 2
     across = me + 1 - 2 * x
     along = me + 2 - 4 * y
     piece = tok_ref.shape[1]
-    arrays = ((in_ref, inf_ref), (ow_ref, owf_ref))
-
-    barrier = pltpu.get_barrier_semaphore()
-    for d in range(1, n):
-        pl.semaphore_signal(barrier, inc=1, device_id={"shard": lax.rem(me + d, n)}, device_id_type=MESH)
-    pl.semaphore_signal(barrier, inc=1, device_id={"rep": 1 - core}, device_id_type=MESH)
-    pl.semaphore_wait(barrier, n)
+    arrays = ((in_ref, w_v), (ow_ref, ow_v))
 
     def region(a, k, part=None):
         src, dst = arrays[a]
-        rows = src.shape[0] // REP
-        start = pl.multiple_of(k * src.shape[0] + core * rows, 8)
-        if part is None:
-            return dst.at[pl.ds(start, rows)]
-        half = src.shape[1] // 2 // TILE * TILE
-        cols = pl.ds(0, half) if part == 0 else pl.ds(half, src.shape[1] - half)
-        return dst.at[pl.ds(start, rows), cols]
+        half = src.shape[1] // REP
+        first = pl.cdiv(half // TILE, 2) * TILE
+        rows = pl.ds(pl.multiple_of(k * src.shape[0], src.shape[0]), src.shape[0])
+        start, size = ((0, first), (first, half - first), (0, half))[2 if part is None else part]
+        return dst.at[rows, pl.ds(pl.multiple_of(core * half + start, TILE), size)]
 
     def send(view, to, s, r):
         return pltpu.make_async_remote_copy(
@@ -545,73 +574,117 @@
         origin = zz * PLANE + (2 * y + x, 2 * y + 1 - x, 2 * (1 - y) + x, 2 * (1 - y) + 1 - x)[kind]
         return send(region(a, origin), {"rep": 1 - core}, sib_s.at[a, zz, kind], sib_r.at[a, zz, kind])
 
-    local = []
-    for a, (src, _) in enumerate(arrays):
-        rows = src.shape[0] // REP
-        start = pl.multiple_of(core * rows, 8)
-        copy = pltpu.make_async_copy(src.at[pl.ds(start, rows)], region(a, me), own.at[a])
-        copy.start()
-        local.append(copy)
-    copy = pltpu.make_async_copy(tok_ref.at[me], seq_ref.at[pl.ds(pl.multiple_of(me * piece, 8), piece)], own.at[2])
-    copy.start()
-    local.append(copy)
-    few = small_ref.shape[0]
-    mine = smf_ref.at[pl.ds(pl.multiple_of(me * few, 8), few)]
-    copy = pltpu.make_async_copy(small_ref, mine, own.at[3])
-    copy.start()
-    local.append(copy)
-    for copy in local:
-        copy.wait()
-
-    def launch(zz):
-        for a in range(2):
-            for kind in range(4):
-                hop(a, zz, kind).start()
-            sibling(a, zz, 0).start()
-
-    for a in range(2):
-        @pl.when(z + 1 < planes)
+    def rows(k):
+        return pl.ds(pl.multiple_of(k * piece, piece), piece)
+
+    quad = me % PLANE
+    moves = (
+        (tok_ref, tok_stage, tok_v, tok_s, tok_r, tok_fs, tok_fr, tok_l),
+        (cot_ref, cot_stage, cots_ref, cot_s, cot_r, cot_fs, cot_fr, cot_l),
+    )
+
+    def stage_copy(m, to, source):
+        src, stage, _, ss, sr = moves[m][:5]
+        return pltpu.make_async_remote_copy(
+            src_ref=src.at[pl.ds(pl.multiple_of(to * PLANE, PLANE), PLANE)], dst_ref=stage.at[source],
+            send_sem=ss.at[to], recv_sem=sr.at[source],
+            device_id={"shard": to * PLANE + quad}, device_id_type=MESH,
+        )
+
+    def own_stage(m):
+        src, stage = moves[m][:2]
+        return pltpu.make_async_copy(src.at[pl.ds(pl.multiple_of(z * PLANE, PLANE), PLANE)], stage.at[z], moves[m][7].at[planes])
+
+    def pass_copy(m, zz, j, source):
+        _, stage, dst, _, _, ss, sr, _ = moves[m]
+        return pltpu.make_async_remote_copy(
+            src_ref=stage.at[zz, j], dst_ref=dst.at[rows(zz * PLANE + source)],
+            send_sem=ss.at[zz, j], recv_sem=sr.at[zz, source],
+            device_id={"shard": z * PLANE + j}, device_id_type=MESH,
+        )
+
+    def keep_copy(m, zz):
+        _, stage, dst = moves[m][:3]
+        return pltpu.make_async_copy(stage.at[zz, quad], dst.at[rows(zz * PLANE + quad)], moves[m][7].at[zz])
+
+    def start_stage(m):
+        for p in range(planes):
+            @pl.when(p != z)
+            def _():
+                stage_copy(m, p, z).start()
+
+    def pass_on(m, zz):
+        @pl.when(zz != z)
         def _():
-            line(a, me, me + PLANE).start()
-
-        @pl.when(z > 0)
-        def _():
-            line(a, me, me - PLANE).start()
-    launch(z)
-    exchange = []
-
-    def tokens(first, last):
-        for d in range(first, last):
-            to = lax.rem(me + d, n)
-            copy = pltpu.make_async_remote_copy(
-                src_ref=tok_ref.at[to], dst_ref=seq_ref.at[pl.ds(pl.multiple_of(me * piece, 8), piece)],
-                send_sem=tok_s.at[d], recv_sem=tok_r.at[d], device_id={"shard": to}, device_id_type=MESH,
-            )
-            copy.start()
-            exchange.append(copy)
-
-    for d in range(1, n):
-        copy = send(mine, {"shard": lax.rem(me + d, n)}, small_s.at[d], small_r.at[d])
-        copy.start()
-        exchange.append(copy)
-    tokens(CUTS[0], CUTS[1])
-
-    def relay(zz):
-        for a in range(2):
-            hop(a, zz, 0).wait_recv()
-            hop(a, zz, 4).start()
-            hop(a, zz, 1).wait_recv()
-            hop(a, zz, 5).start()
-
-    def collect(zz):
-        for a in range(2):
-            hop(a, zz, 3).wait_recv()
-            sibling(a, zz, 1).start()
-            hop(a, zz, 2).wait_recv()
-            sibling(a, zz, 2).start()
-            hop(a, zz, 4).wait_recv()
-            hop(a, zz, 5).wait_recv()
-            sibling(a, zz, 3).start()
+            stage_copy(m, zz, zz).wait_recv()
+
+        for j in range(PLANE):
+            @pl.when(j != quad)
+            def _():
+                pass_copy(m, zz, j, quad).start()
+
+        keep_copy(m, zz).start()
+
+    def landed(m, zz):
+        for j in range(PLANE):
+            @pl.when(j != quad)
+            def _():
+                pass_copy(m, zz, j, j).wait_recv()
+
+        keep_copy(m, zz).wait()
+
+    def gone(m):
+        for zz in range(planes):
+            @pl.when(zz != z)
+            def _():
+                stage_copy(m, zz, z).wait_send()
+
+            for j in range(PLANE):
+                @pl.when(j != quad)
+                def _():
+                    pass_copy(m, zz, j, quad).wait_send()
+
+    def small_copy(to, source):
+        return pltpu.make_async_remote_copy(
+            src_ref=small_ref, dst_ref=few.at[source], send_sem=small_s.at[to], recv_sem=small_r.at[source],
+            device_id={"shard": to}, device_id_type=MESH,
+        )
+
+    def local_copies():
+        both = [
+            pltpu.make_async_copy(src, dst.at[pl.ds(pl.multiple_of(me * src.shape[0], 8), src.shape[0])], own.at[a])
+            for a, (src, dst) in enumerate(arrays)
+        ]
+        return both + [
+            pltpu.make_async_copy(small_ref, few.at[me], own.at[2]),
+            own_stage(0),
+            own_stage(1),
+        ]
+
+    def saves():
+        return [
+            pltpu.make_async_copy(w_v, inf_ref, keep_s.at[0]),
+            pltpu.make_async_copy(ow_v, owf_ref, keep_s.at[1]),
+        ]
+
+    def launch(a, zz):
+        for kind in range(4):
+            hop(a, zz, kind).start()
+
+    def relay(a, zz):
+        hop(a, zz, 0).wait_recv()
+        hop(a, zz, 4).start()
+        hop(a, zz, 1).wait_recv()
+        hop(a, zz, 5).start()
+
+    def collect(a, zz):
+        hop(a, zz, 3).wait_recv()
+        sibling(a, zz, 1).start()
+        hop(a, zz, 2).wait_recv()
+        sibling(a, zz, 2).start()
+        hop(a, zz, 4).wait_recv()
+        hop(a, zz, 5).wait_recv()
+        sibling(a, zz, 3).start()
 
     def each(d, step):
         @pl.when(z - d >= 0)
@@ -622,74 +695,185 @@
         def _():
             step(z + d, me + d * PLANE, me - PLANE, z > 0)
 
-    def arrived(zz, origin, to, more):
-        for a in range(2):
+    def start_line(a):
+        @pl.when(z + 1 < planes)
+        def _():
+            line(a, me, me + PLANE).start()
+
+        @pl.when(z > 0)
+        def _():
+            line(a, me, me - PLANE).start()
+
+    def arrived(a):
+        def step(zz, origin, to, more):
             line(a, origin, to).wait_recv()
 
             @pl.when(more)
             def _():
                 line(a, origin, to).start()
-        launch(zz)
-
-    for d in range(1, planes):
-        each(d, arrived)
-        if d == 1:
-            relay(z)
-        else:
-            each(d - 1, lambda zz, *_: relay(zz))
-        tokens(CUTS[d], CUTS[d + 1])
-    collect(z)
-    each(planes - 1, lambda zz, *_: relay(zz))
-    tokens(CUTS[4], CUTS[5])
-    for d in range(1, planes):
-        each(d, lambda zz, *_: collect(zz))
-
-    for copy in exchange:
-        copy.wait()
-    for zz in range(planes):
+
+            sibling(a, zz, 0).start()
+            launch(a, zz)
+
+        return step
+
+    def send_pieces(copy, first, last):
+        for d in range(first, last):
+            copy(lax.rem(me + d, n), me).start()
+
+    @pl.when(block == 0)
+    def _():
+        barrier = pltpu.get_barrier_semaphore()
+        for d in range(1, n):
+            pl.semaphore_signal(barrier, inc=1, device_id={"shard": lax.rem(me + d, n)}, device_id_type=MESH)
+        pl.semaphore_signal(barrier, inc=1, device_id={"rep": 1 - core}, device_id_type=MESH)
+        local = local_copies()
+        for copy in local:
+            copy.start()
+        for copy in local[:2]:
+            copy.wait()
+        pl.semaphore_wait(barrier, n)
         for a in range(2):
-            for kind in range(4):
-                sibling(a, zz, kind).wait()
-            for kind in range(6):
-                hop(a, zz, kind).wait_send()
-    for a in range(2):
-        def sent(zz, origin, to, more):
-            @pl.when(more)
-            def _():
-                line(a, origin, to).wait_send()
-
+            start_line(a)
+        for a in range(2):
+            launch(a, z)
+
+        @pl.when(z == 0)
+        def _():
+            start_stage(0)
+
+        send_pieces(small_copy, 1, n)
         for d in range(1, planes):
-            each(d, sent)
-
-        @pl.when(z + 1 < planes)
-        def _():
-            line(a, me, me + PLANE).wait_send()
+            for a in range(2):
+                each(d, arrived(a))
+                if d == 1:
+                    relay(a, z)
+                else:
+                    each(d - 1, lambda zz, *_: relay(a, zz))
 
         @pl.when(z > 0)
         def _():
-            line(a, me, me - PLANE).wait_send()
-
-
-def run_gather(tokens, in_weight, out_weight, small):
+            start_stage(0)
+
+        for a in range(2):
+            collect(a, z)
+            each(planes - 1, lambda zz, *_: relay(a, zz))
+        for a in range(2):
+            for d in range(1, planes):
+                each(d, lambda zz, *_: collect(a, zz))
+        for copy in local[2:]:
+            copy.wait()
+        for k in range(n):
+            @pl.when(me != k)
+            def _():
+                small_copy(k, k).wait_recv()
+        lay_out(few, n, nw_ref, cw_ref, cb_ref, gn_ref)
+        for h in range(HEADS):
+            sk_ref[:, h * HEADDIM : (h + 1) * HEADDIM] = jnp.broadcast_to(head_ref[2:3, h : h + 1], (1, HEADDIM))
+        for a in range(2):
+            for d in range(planes):
+                for kind in range(4):
+                    if kind > 0:
+                        sibling(a, d, kind).wait_recv()
+                    else:
+                        @pl.when(z != d)
+                        def _():
+                            sibling(a, d, kind).wait_recv()
+        for copy in saves():
+            copy.start()
+        pass_on(0, 0)
+        forward_start(w_v, own_scratch[0], own_scratch[4], blocks[1])
+
+    @pl.when(block + 1 < planes)
+    def _():
+        pass_on(0, block + 1)
+
+    landed(0, block)
+
+    @pl.when(block == COT_AT)
+    def _():
+        start_stage(1)
+
+    forward_step(
+        block, len_ref, tok_v.at[pl.ds(pl.multiple_of(block * SPAN, SPAN), SPAN)], w_v, ow_v,
+        nw_ref, cw_ref, cb_ref, head_ref.at[0:1], head_ref.at[1:2], sk_ref, gn_ref, *blocks, *own_scratch,
+    )
+
+    @pl.when(block == pl.num_programs(0) - 1)
+    def _():
+        keep = pltpu.make_async_copy(tok_v, seq_ref, keep_s.at[2])
+        keep.start()
+        for copy in saves():
+            copy.wait()
+        for zz in range(planes):
+            pass_on(1, zz)
+        for m in range(2):
+            gone(m)
+        for zz in range(planes):
+            landed(1, zz)
+        for k in range(n):
+            @pl.when(me != k)
+            def _():
+                small_copy(k, k).wait_send()
+        for a in range(2):
+            def sent(zz, origin, to, more):
+                @pl.when(more)
+                def _():
+                    line(a, origin, to).wait_send()
+
+            for d in range(1, planes):
+                each(d, sent)
+
+            @pl.when(z + 1 < planes)
+            def _():
+                line(a, me, me + PLANE).wait_send()
+
+            @pl.when(z > 0)
+            def _():
+                line(a, me, me - PLANE).wait_send()
+
+            for zz in range(planes):
+                for kind in range(6):
+                    hop(a, zz, kind).wait_send()
+                for kind in range(4):
+                    if kind > 0:
+                        sibling(a, zz, kind).wait_send()
+                    else:
+                        @pl.when(z != zz)
+                        def _():
+                            sibling(a, zz, kind).wait_send()
+        keep.wait()
+
+
+def run_gather_forward(valid, tokens, cotangent, in_weight, out_weight, small, heads):
     n, piece, width = tokens.shape
+    length = n * piece
     planes = n // PLANE
+    proj = in_weight.shape[1]
+    inner = n * out_weight.shape[0]
     hbm = pl.BlockSpec(memory_space=pl.ANY)
+    vmem = pl.BlockSpec(memory_space=pltpu.VMEM)
     dma = pltpu.SemaphoreType.DMA
-    shapes = [
-        ((n * piece, width), tokens.dtype), ((n * in_weight.shape[0], in_weight.shape[1]), in_weight.dtype),
-        ((n * out_weight.shape[0], out_weight.shape[1]), out_weight.dtype), ((n * small.shape[0], TILE), small.dtype),
-    ]
-    return pl.pallas_call(
-        functools.partial(gather_kernel, n),
-        out_shape=[jax.ShapeDtypeStruct(s, d) for s, d in shapes],
-        in_specs=[hbm] * 4,
-        out_specs=[hbm] * 4,
-        scratch_shapes=[
-            dma((4,)), dma((n,)), dma((n,)), dma((n,)), dma((n,)), dma((2, planes, 2)), dma((2, planes)),
-            dma((2, planes, 6)), dma((2, planes, 6)), dma((2, planes, 4)), dma((2, planes, 4)),
+    shapes, out_specs, scratch = forward_results(length, width)
+    rows = [(1, width), (CONV, XBC), (1, XBC), (1, DI), (1, DI)]
+    more = [((length, width), BF16)] * 2 + [((width, proj), BF16), ((inner, width), BF16)] + [(r, F32) for r in rows]
+    results = pl.pallas_call(
+        functools.partial(gather_forward_kernel, n),
+        grid=(length // SPAN,),
+        out_shape=shapes + [jax.ShapeDtypeStruct(s, d) for s, d in more],
+        in_specs=[pl.BlockSpec(memory_space=pltpu.SMEM), hbm, hbm, hbm, hbm, vmem, vmem],
+        out_specs=out_specs + [hbm] * 4 + [whole(r) for r in rows],
+        scratch_shapes=scratch + [
+            pltpu.VMEM((length, width), BF16), pltpu.VMEM((width, proj), BF16), pltpu.VMEM((inner, width), BF16),
+            pltpu.VMEM((n, EDGE, TILE), F32), *(pltpu.VMEM((planes, PLANE, piece, width), BF16) for _ in range(2)), dma((3,)),
+            *(dma(d) for _ in range(2) for d in ((planes,), (planes,), (planes, PLANE), (planes, PLANE), (planes + 1,))), dma((n,)), dma((n,)), dma((2, planes, 2)), dma((2, planes)),
+            dma((2, planes, 6)), dma((2, planes, 6)), dma((2, planes, 4)), dma((2, planes, 4)), dma((3,)),
         ],
-        compiler_params=pltpu.CompilerParams(collective_id=0, has_side_effects=True),
-    )(tokens, in_weight, out_weight, small)
+        compiler_params=pltpu.CompilerParams(
+            dimension_semantics=("arbitrary",), collective_id=0, has_side_effects=True, vmem_limit_bytes=LIMIT
+        ),
+    )(valid, tokens, cotangent, in_weight, out_weight, small, heads)
+    return results[:8], results[8:]
 
 
 PARTS = (
@@ -766,10 +950,10 @@
             return remote(sb.at[:, y, 1 - x], r2, s2s.at[p], s2r.at[p], across)
         return remote(sb.at[:, 1 - y, x], r2, s2s.at[p], s2r.at[p], along)
 
-    def c3(p, dest, up):
+    def c3(p, dest, source):
         sb, r3 = bufs[p][3], bufs[p][6]
-        to = {"shard": me + PLANE if up else me - PLANE}
-        return remote(sb.at[dest, y, x], r3.at[int(up), dest], s3s.at[p, dest], s3r.at[p, int(up), dest], to)
+        to = {"shard": dest * PLANE + 2 * y + x}
+        return remote(sb.at[dest, y, x], r3.at[source], s3s.at[p, dest], s3r.at[p, source], to)
 
     def into_half(p):
         acc, _, r0, sb = bufs[p][:4]
@@ -808,23 +992,11 @@
             acc[zz, y, x] = value
             sb[zz, y, x] = value.astype(BF16)
 
-    def line(p):
-        acc, sb, r3 = bufs[p][0], bufs[p][3], bufs[p][6]
-        for i in range(planes - 1):
-            for up in (True, False):
-                dest = planes - 1 - i if up else i
-                beyond = dest > z if up else dest < z
-                more = z > 0 if up else z + 1 < planes
-
-                @pl.when(beyond)
-                def _():
-                    @pl.when(more)
-                    def _():
-                        c3(p, dest, up).wait_recv()
-                        value = acc[dest, y, x] + r3[int(up), dest].astype(F32)
-                        sb[dest, y, x] = value.astype(BF16)
-
-                    c3(p, dest, up).start()
+    def to_planes(p):
+        for dest in range(planes):
+            @pl.when(dest != z)
+            def _():
+                c3(p, dest, z).start()
 
     def results(p):
         a, start, size, _ = PARTS[p]
@@ -837,17 +1009,13 @@
             pltpu.make_async_copy(acc.at[z, y, x], view, own.at[p]),
         )
 
-    def arrivals(p, up):
-        r3 = bufs[p][6]
-        return remote(bufs[p][3].at[z, y, x], r3.at[int(up), z], s3s.at[p, z], s3r.at[p, int(up), z], along)
-
     def finish(p):
         acc, r3 = bufs[p][0], bufs[p][6]
-        for up in (True, False):
-            @pl.when(z > 0 if up else z + 1 < planes)
+        for source in range(planes):
+            @pl.when(source != z)
             def _():
-                arrivals(p, up).wait_recv()
-                acc[z, y, x] += r3[int(up), z].astype(F32)
+                c3(p, source, source).wait_recv()
+                acc[z, y, x] += r3[source].astype(F32)
 
         for copy in results(p):
             copy.start()
@@ -891,11 +1059,11 @@
     stage(into_half, c1, 2)
     igs(2)
     stage(after_second, None, 0)
-    stage(line, None, 0)
+    stage(to_planes, None, 0)
     stage(after_first, c2, 1)
     igs(3)
     stage(after_second, None, 1)
-    stage(line, None, 1)
+    stage(to_planes, None, 1)
     stage(finish, None, 0)
     stage(after_first, c2, 2)
     stage(finish, None, 1)
@@ -909,7 +1077,7 @@
     pair = remote(few_sib.at[0], few_sib.at[1], pair_s, pair_r, twin)
     pair.start()
     stage(after_second, None, 2)
-    stage(line, None, 2)
+    stage(to_planes, None, 2)
     stage(finish, None, 2)
     pair.wait()
     sum_ref[...] = few_sib[0] + few_sib[1]
@@ -918,13 +1086,10 @@
         ig_copy(d).wait()
     for p in range(count):
         c0(p).wait_send()
-        for i in range(planes - 1):
-            for up in (True, False):
-                dest = planes - 1 - i if up else i
-
-                @pl.when(dest > z if up else dest < z)
-                def _():
-                    c3(p, dest, up).wait_send()
+        for dest in range(planes):
+            @pl.when(dest != z)
+            def _():
+                c3(p, dest, z).wait_send()
 
         far, near = results(p)
         near.wait()
@@ -946,14 +1111,14 @@
         full = (planes, 2, 2, rows, size)
         scratch += [
             pltpu.VMEM(full, F32), pltpu.VMEM(full, BF16), pltpu.VMEM(full, BF16), pltpu.VMEM(full, BF16),
-            pltpu.VMEM((planes, 2, rows, size), BF16), pltpu.VMEM((planes, rows, size), BF16), pltpu.VMEM((2, planes, rows, size), BF16),
+            pltpu.VMEM((planes, 2, rows, size), BF16), pltpu.VMEM((planes, rows, size), BF16), pltpu.VMEM((planes, rows, size), BF16),
         ]
     count = len(PARTS)
     few = small.shape[1:]
     scratch += [
         pltpu.VMEM((width, length), BF16), pltpu.VMEM((inner, length), BF16), pltpu.VMEM((n, *few), F32), pltpu.VMEM((2, *few), F32),
         dma((count + 1,)), dma((n,)), dma((n,)), dma((n,)), dma((n,)), dma(()), dma(()),
-        *(dma((count,)) for _ in range(6)), dma((count, planes)), dma((count, 2, planes)), dma((count,)), dma((count,)),
+        *(dma((count,)) for _ in range(6)), dma((count, planes)), dma((count, planes)), dma((count,)), dma((count,)),
     ]
     shapes = [
         ((n, piece, width), BF16), ((width // n, proj), F32), ((inner // n, width), F32), (few, F32),
@@ -968,9 +1133,6 @@
     )(ig, normed, gp, gate_low, grad_branch, small)
 
 
-FEW = EDGE * TILE
-
-
 def on_device(
     tokens, cotangent, lengths, order, norm_weight, in_weight, conv_weight, conv_bias,
     step_bias, decay_log, skip_gain, gate_norm_weight, out_weight,
@@ -994,45 +1156,49 @@
     sequence = jnp.sum(jnp.where(slots == rank, order[0], 0))
     valid = jnp.sum(jnp.where(slots == sequence, lengths[0], 0))[None]
     direct = peers == PLANE * PLANE and lax.axis_size("rep") == REP and piece % 16 == 0
-    sizes = [v.size for v in (norm_weight, conv_weight, conv_bias, gate_norm_weight)]
     if direct:
-        few = jnp.concatenate([v.astype(F32).reshape(-1) for v in (norm_weight, conv_weight, conv_bias, gate_norm_weight)])
-        few = jnp.pad(few, (0, FEW - few.size)).reshape(EDGE, TILE)
-        tok, in_full, out_full, few = run_gather(tokens, in_weight, out_weight, few)
-        few = few.reshape(peers, FEW)
-        ends = [sum(sizes[: i + 1]) for i in range(4)]
-        norm_full, conv_full, shift_full, gate_full = (
-            few[:, e - s : e].reshape(-1) for s, e in zip(sizes, ends)
+        def row(v):
+            return jnp.pad(v.astype(F32).reshape(-1, v.shape[-1]), ((0, 0), (0, TILE - v.shape[-1])))
+
+        blank = jnp.zeros((EDGE - CONV - 3, TILE), F32)
+        small = jnp.concatenate([row(norm_weight), row(conv_weight.T), row(conv_bias), row(gate_norm_weight), blank])
+        heads = jnp.concatenate([row(step_bias), row(decay_log), row(skip_gain), jnp.zeros((EDGE - 3, TILE), F32)])
+        wide = jnp.pad(in_weight, ((0, 0), (0, -in_weight.shape[1] % (2 * REP * TILE))))
+        forward, gathered = run_gather_forward(valid, tokens, cotangent, wide, out_weight, small, heads)
+        out, cin, gr, mx, st, sr, normed, gate_low = forward
+        tok, cot, in_full, out_full, norm_row, taps_rows, shift_row, skip_row, gate_row = gathered
+        params = (in_full, out_full, norm_row, taps_rows, shift_row, heads[0:1], heads[1:2], skip_row, gate_row)
+    else:
+        tok, cot = to_sequences(tokens), to_sequences(cotangent)
+        params = prepare(
+            gather(norm_weight), gather(in_weight), gather(conv_weight), gather(conv_bias),
+            gather(gate_norm_weight), gather(out_weight), step_bias, decay_log, skip_gain,
         )
-        conv_full = conv_full.reshape(XBC, CONV)
-    else:
-        tok = to_sequences(tokens)
-        norm_full, in_full, conv_full = gather(norm_weight), gather(in_weight), gather(conv_weight)
-        shift_full, gate_full, out_full = gather(conv_bias), gather(gate_norm_weight), gather(out_weight)
-    cot = to_sequences(cotangent)
-    params = prepare(norm_full, in_full, conv_full, shift_full, gate_full, out_full, step_bias, decay_log, skip_gain)
-    out, cin, gr, mx, st, sr, normed, gate_low = run_forward(valid, tok, params)
+        out, cin, gr, mx, st, sr, normed, gate_low = run_forward(valid, tok, params)
     output = to_slots(out)
     ig, gp, gb, taps, gcb, ggn, gsk, gnw, ghd = run_backward(valid, cot, tok, params, (cin, gr, mx, st, sr))
-    few = [jnp.sum(gnw, axis=0), jnp.sum(taps, axis=1).T, jnp.sum(gcb, axis=0), jnp.sum(ggn, axis=0)]
+    few = [jnp.sum(gnw, axis=0), jnp.sum(taps, axis=1), jnp.sum(gcb, axis=0), jnp.sum(ggn, axis=0)]
     heads = jnp.stack([
         jnp.sum(ghd[:EDGE], axis=0)[:HEADS], jnp.sum(ghd[EDGE:], axis=0)[:HEADS],
         jnp.sum(gsk.reshape(EDGE, HEADS, HEADDIM), axis=(0, 2)),
     ])
     if direct:
-        rows = [v.reshape(peers, -1) for v in few] + [jnp.broadcast_to(heads.reshape(1, -1), (peers, heads.size))]
-        few = jnp.concatenate(rows, axis=1)
-        few = jnp.pad(few, ((0, 0), (0, FEW - few.shape[1]))).reshape(peers, EDGE, TILE)
+        parts = [jnp.moveaxis(v.reshape(-1, peers, v.shape[-1] // peers), 1, 0) for v in few]
+        parts.append(jnp.broadcast_to(heads.reshape(1, 1, -1), (peers, 1, heads.size)))
+        few = jnp.concatenate([jnp.pad(v, ((0, 0), (0, 0), (0, TILE - v.shape[2]))) for v in parts], axis=1)
         input_grad, grad_in, grad_out, few = run_scatter(peers, ig, normed, gp, gate_low, gb, few)
-        few = few.reshape(-1)
-        few, heads = [few[e - s : e] for s, e in zip(sizes, ends)], few[ends[3] : ends[3] + heads.size].reshape(heads.shape)
-        few[1] = few[1].reshape(-1, CONV)
+        heads = few[EDGE - 1, : heads.size].reshape(heads.shape)
+        few = [
+            few[0, : norm_weight.size], few[1 : 1 + CONV, : conv_bias.size].T,
+            few[1 + CONV, : conv_bias.size], few[2 + CONV, : gate_norm_weight.size],
+        ]
     else:
         input_grad = to_slots(ig)
 
         def scatter(v):
             return lax.psum(lax.psum_scatter(v, "shard", scatter_dimension=0, tiled=True), "rep")
 
+        few[1] = few[1].T
         few = [scatter(v) for v in few]
         grad_in, grad_out = scatter(mul_tn(normed, gp)), scatter(mul_tn(gate_low, gb))
         heads = lax.psum(heads, ("rep", "shard"))

time: 376 us -> 322 us (0.86)
  Pallas kernels: 327 us -> 279 us
  local copies, waits for them, and re-layouts: 21.1 us -> 16.3 us
  starting transfers between devices: 18.2 us -> 13.5 us
  other arithmetic: 7.65 us -> 11.6 us
    pallas_call x1, Pallas kernels: 103 us -> 75.4 us  [run_scatter(): pl.pallas_call(functools.partial(scatter_kernel, n), out_shape=[jax.Shape...]
    pallas_call x2 -> x1, Pallas kernels: 137 us -> 116 us  [run_gather_forward(): pl.pallas_call(functools.partial(gather_forward_kernel, n), grid=(length...]
    all_to_all x1 -> x0, starting transfers between devices: 8.46 us -> none  [to_sequences(): lax.all_to_all(parts, 'shard', split_axis=0, concat_axis=2, tiled=True)]
    slice x10 -> x0, local copies, waits for them, and re-layouts: 6.1 us -> none  [the longest x5 4.5 us: on_device(): few[e - s:e]]
    squeeze x0 -> x4, local copies, waits for them, and re-layouts: none -> 4.93 us  [the longest x1 1.37 us: on_device(): heads[2]]
    another operation x6 -> x3, local copies, waits for them, and re-layouts: 4.05 us -> 0.25 us  [on_device(): jnp.moveaxis(v.reshape(-1, peers, v.shape[-1] // peers), 1, 0)]
    unnamed x34 -> x14, local copies, waits for them, and re-layouts: 7.72 us -> 5.08 us
  transfers between devices with their start and end apart: 2 -> 1, of which waited for: 0 -> 0; matrix products, arithmetic and copies ran while one was open for 6% -> 4% of each run, Pallas kernels for 87% -> 51%
where the time goes in v3:
time: 322 us; the launch traced here: 321 us
  Pallas kernels  279 us (87%)
  local copies, waits for them, and re-layouts  16.3 us (5%)
  starting transfers between devices  13.5 us (4%)
  other arithmetic  11.6 us (4%)
    pallas_call x1, Pallas kernels, run_gather_forward(): pl.pallas_call(functools.partial(gather_forward_kernel, n), grid=(length...  116 us
    pallas_call x1, Pallas kernels, run_backward(): pl.pallas_call(backward_kernel, grid=(count,), out_shape=[jax.ShapeDtypeS...  87.3 us
    pallas_call x1, Pallas kernels, run_scatter(): pl.pallas_call(functools.partial(scatter_kernel, n), out_shape=[jax.Shape...  75.4 us
    all_to_all x1, starting transfers between devices, to_slots(): lax.all_to_all(parts, 'shard', split_axis=0, concat_axis=0, tiled=True)  13.5 us
  transfers between devices with their start and end apart: 1, of which 0 were waited for; matrix products, arithmetic and copies ran while one was open for 4% of the time, Pallas kernels for 51%

profile of v3, /device:TPU:0, one launch (start us, length us, event | category | flops | bytes accessed | tf_op | source)
XLA Modules:
  0.0 321.0 jit_solution(1849419860538601742)
XLA Ops:
  0.6 0.7 pad.73.sb_ref
  1.3 0.0 copy-start.3
  1.3 0.7 pad.74.dl_ref
  2.0 0.0 copy-start.4
  2.0 0.7 pad_convert_fusion.3
  2.6 0.7 pad_convert_fusion
  3.3 1.3 fusion.2
  4.6 1.9 fusion.3
  6.6 0.1 pad.88.clone
  6.6 0.7 pad_convert_fusion.1
  7.3 1.7 pad.64.refs_3_
  9.0 1.3 fusion.refs_6_
  10.4 0.6 concatenate.9.refs_5_
  11.0 116.2 %shard_map.212 = (bf16[1024,768]{1,0:T(8,128)(2,1)}, f32[4,264,1792]{2,1,0:T(8,128)}, f32[1024,1536]{1,0:T(8,128)}, f32[1024,1536]{1,0:T(8,128)}, f32[4,128,1536...) custom-call(s32[1]{0:T(128)} %bitcast.2.refs_0_.len_ref, ...), custom_call_target="tpu_custom_call" | custom-call | tf_op jit(solution)/shard_map/pallas_call | solution.py:860
  127.2 0.0 copy-done.3
  127.2 0.0 copy-done.4
  127.2 13.5 %all-to-all-start = ((bf16[16,64,768]{2,1,0:T(8,128)(2,1)}), bf16[16,64,768]{2,1,0:T(8,128)(2,1)S(1)}, u32[]{:S(2)}, u32[]{:S(2)}) async-start(bf16[16,64,768]{2,1,0:T(8,128)(2,1)} %bitcast.35), calls=%async_computation | async-start | bytes 3145728 | tf_op jit(solution)/shard_map/all_to_all | solution.py:1153
  140.7 87.3 %shard_map.213 = (bf16[1024,768]{1,0:T(8,128)(2,1)}, bf16[1024,3352]{1,0:T(8,128)(2,1)}, bf16[1024,768]{1,0:T(8,128)(2,1)}, f32[4,8,1792]{2,1,0:T(8,128)}, f32[8...) custom-call(s32[1]{0:T(128)} %bitcast.2.refs_0_.len_ref, ...), custom_call_target="tpu_custom_call" | custom-call | flops 40000000000 | bytes 60000000 | tf_op jit(solution)/shard_map/pallas_call | solution.py:484
  227.9 0.8 reduce_sum.90
  228.7 0.1 transpose_reshape.9
  228.8 0.8 reduce_sum.92
  229.6 0.1 transpose_reshape.10
  229.7 0.8 reduce_sum.93
  230.6 0.1 transpose_reshape.11
  230.7 0.8 reduce_sum.96
  231.5 0.1 reduce_sum.97
  231.6 0.1 reduce_sum.98
  231.7 0.7 slice_reduce_fusion.1
  232.4 0.1 broadcast_in_dim.23
  232.5 1.0 reduce_sum.91
  233.5 0.1 reshape.68
  233.6 0.7 concatenate.11.refs_5_
  234.3 75.4 %shard_map.214 = (bf16[16,64,768]{2,1,0:T(8,128)(2,1)}, f32[48,3352]{1,0:T(8,128)}, f32[96,768]{1,0:T(8,128)}, f32[8,128]{1,0:T(8,128)}) custom-call(bf16[1024,768]{1,0:T(8,128)(2,1)} %get-tuple-element.56.refs_0_, bf16[1024,768]{1,0:T(8,128)(2,1)} %get-tuple-element.57.refs_1_, bf16[1024,3352]{1,0:T(8,128)(2,1)} %get-tuple-element.58.refs_2_, ...), custom_call_target="tpu_custom_call" | custom-call | tf_op jit(solution)/shard_map/pallas_call | solution.py:1126
  309.7 1.2 slice_bitcast_fusion.1
  310.9 1.2 slice_bitcast_fusion.5
  312.1 1.2 slice_bitcast_fusion.6
  313.3 1.4 slice_bitcast_fusion.2
  314.7 1.3 slice_bitcast_fusion
  315.9 0.0 all-to-all-done
  315.9 0.0 copy-start
  315.9 1.1 copy.32
  317.1 0.8 copy-done
  317.9 0.0 copy-start.1
  317.9 0.0 copy-start.2
  317.9 1.1 copy.33
  319.0 0.4 copy-done.1
  319.4 0.8 copy.34
  320.3 0.0 copy-done.2
  320.3 0.7 copy.35
  (12 shorter events, 0.1 us)
Async XLA Ops:
  1.3 125.9 %copy-start.3 = (f32[1,128]{1,0:T(1,128)}, f32[1,128]{1,0:T(1,128)S(1)}, u32[]{:S(2)}) copy-start(f32[1,128]{1,0:T(1,128)S(1)} %pad.73.sb_ref) | copy-start | bytes 1540
  2.0 125.2 %copy-start.4 = (f32[1,128]{1,0:T(1,128)}, f32[1,128]{1,0:T(1,128)S(1)}, u32[]{:S(2)}) copy-start(f32[1,128]{1,0:T(1,128)S(1)} %pad.74.dl_ref) | copy-start | bytes 1540
  127.2 188.7 %all-to-all-start = ((bf16[16,64,768]{2,1,0:T(8,128)(2,1)}), bf16[16,64,768]{2,1,0:T(8,128)(2,1)S(1)}, u32[]{:S(2)}, u32[]{:S(2)}) async-start(bf16[16,64,768]{2,1,0:T(8,128)(2,1)} %bitcast.35), calls=%async_computation | async-start | bytes 3145728 | tf_op jit(solution)/shard_map/all_to_all | solution.py:1153
  315.9 2.0 copy-start
  317.9 1.5 copy-start.1
  317.9 2.4 copy-start.2

commit v4 on v3

--- a/solution.py
+++ b/solution.py
@@ -79,6 +79,10 @@
     return shifted, step, cumul, cumul - jnp.log(step)
 
 
+def own_length(len_ref, ord_ref):
+    return len_ref[0, ord_ref[0, lax.axis_index("shard")]]
+
+
 def causal_mask(flip):
     rows = lax.broadcasted_iota(jnp.int32, (HALF, HALF), 0)
     columns = lax.broadcasted_iota(jnp.int32, (HALF, HALF), 1)
@@ -93,8 +97,8 @@
 
 
 def forward_step(
-    block, len_ref, tok_ref, w_ref, ow_ref, nw_ref, cw_ref, cb_ref, sb_ref, dl_ref, sk_ref, gn_ref,
-    out_ref, cin_ref, gr_ref, mx_ref, st_ref, sr_ref, nl_ref, gl_ref,
+    block, length, tok_ref, w_ref, ow_ref, nw_ref, cw_ref, cb_ref, sb_ref, dl_ref, sk_ref, gn_ref,
+    out_ref, cin_ref, gr_ref, mx_ref, st_ref, sr_ref, nl_ref, gl_ref, ar_ref,
     ws, col_t, pair_s, row_s, state, scores, gated, hook=None,
 ):
     offset = block * SPAN
@@ -123,7 +127,9 @@
         pair_s[j] = jnp.where(low_lanes, spread(shift, 2 * j), spread(shift, 2 * j + 1))
 
     def act(jt):
-        arg = conv_argument(cin_ref, cw_ref, cb_ref, tile_at(jt))
+        cols = tile_at(jt)
+        arg = conv_argument(cin_ref, cw_ref, cb_ref, cols)
+        ar_ref[:, cols] = arg
         return arg * sigmoid(arg)
 
     key = act(PAIRS).astype(BF16)
@@ -173,7 +179,7 @@
         gated[:, cols] = value
         return total + value * value
 
-    total = lax.fori_loop(0, PAIRS, pair, jnp.zeros((SPAN, TILE), F32))
+    total = lax.fori_loop(0, PAIRS, pair, jnp.zeros((SPAN, TILE), F32), unroll=3)
     rms = lax.rsqrt(jnp.sum(total, axis=-1, keepdims=True) * (1.0 / DI) + epsilon)
 
     def finish(j, carry):
@@ -183,7 +189,7 @@
 
     lax.fori_loop(0, PAIRS, finish, 0)
     positions = offset + lax.broadcasted_iota(jnp.int32, (SPAN, 256), 0)
-    valid = positions < len_ref[0]
+    valid = positions < length
     for n in range(0, tok_ref.shape[1], 256):
         branch = mul(gl_ref[...], ow_ref[:, n : n + 256])
         tok = tok_ref[:, n : n + 256].astype(F32)
@@ -192,8 +198,8 @@
 
 
 def forward_kernel(
-    len_ref, tok_ref, w_ref, ow_ref, nw_ref, cw_ref, cb_ref, sb_ref, dl_ref, sk_ref, gn_ref,
-    out_ref, cin_ref, gr_ref, mx_ref, st_ref, sr_ref, nl_ref, gl_ref,
+    len_ref, ord_ref, tok_ref, w_ref, ow_ref, nw_ref, cw_ref, cb_ref, sb_ref, dl_ref, sk_ref, gn_ref,
+    out_ref, cin_ref, gr_ref, mx_ref, st_ref, sr_ref, nl_ref, gl_ref, ar_ref,
     ws, col_t, pair_s, row_s, state, scores, gated,
 ):
     block = pl.program_id(0)
@@ -203,17 +209,18 @@
         forward_start(w_ref, ws, state, cin_ref)
 
     forward_step(
-        block, len_ref, tok_ref, w_ref, ow_ref, nw_ref, cw_ref, cb_ref, sb_ref, dl_ref, sk_ref, gn_ref,
-        out_ref, cin_ref, gr_ref, mx_ref, st_ref, sr_ref, nl_ref, gl_ref,
+        block, own_length(len_ref, ord_ref), tok_ref, w_ref, ow_ref, nw_ref, cw_ref, cb_ref, sb_ref, dl_ref, sk_ref, gn_ref,
+        out_ref, cin_ref, gr_ref, mx_ref, st_ref, sr_ref, nl_ref, gl_ref, ar_ref,
         ws, col_t, pair_s, row_s, state, scores, gated,
     )
 
 
 def backward_kernel(
-    len_ref, cot_ref, tok_ref, w_ref, ow_ref, nw_ref, cw_ref, cb_ref, sb_ref, dl_ref, sk_ref, gn_ref,
-    cin_ref, gr_ref, mx_ref, st_ref, sr_ref,
-    ig_ref, gp_ref, gb_ref, taps_ref, gcb_ref, ggn_ref, gsk_ref, gnw_ref, ghd_ref,
-    ws, col_s, pair_t, row_t, later, scores, grad_scores, gg, sig, gpre, args, acc_q, acc_k, acc_u, acc_v, acc_l,
+    peers, len_ref, ord_ref, cot_ref, tok_ref, w_ref, ow_ref, nw_ref, cw_ref, cb_ref, sb_ref, dl_ref, sk_ref, gn_ref,
+    cin_ref, gr_ref, mx_ref, st_ref, sr_ref, ar_ref,
+    ig_ref, gp_ref, gb_ref, few_ref,
+    taps_ref, gcb_ref, ggn_ref, gsk_ref, gnw_ref, ghd_ref,
+    ws, col_s, pair_t, row_t, later, scores, grad_scores, gg, sig, gpre, acc_q, acc_k, acc_u, acc_v, acc_l,
 ):
     step_id = pl.program_id(0)
     count = pl.num_programs(0)
@@ -230,7 +237,7 @@
 
     width = cot_ref.shape[1]
     positions = offset + lax.broadcasted_iota(jnp.int32, (SPAN, width), 0)
-    grad_branch = jnp.where(positions < len_ref[0], cot_ref[...].astype(F32), 0.0).astype(BF16)
+    grad_branch = jnp.where(positions < own_length(len_ref, ord_ref), cot_ref[...].astype(F32), 0.0).astype(BF16)
     gb_ref[...] = grad_branch
     for n in range(0, DI, 256):
         gg[:, n : n + 256] = mul_nt(grad_branch, ow_ref[n : n + 256, :])
@@ -259,13 +266,12 @@
     rms = jnp.broadcast_to(rms, (SPAN, TILE))
     coef = jnp.broadcast_to(coef, (SPAN, TILE))
 
-    def act(jt, slot):
-        arg = conv_argument(cin_ref, cw_ref, cb_ref, tile_at(jt))
-        args[:, slot * TILE : (slot + 1) * TILE] = arg
+    def act(jt):
+        arg = ar_ref[:, jt * TILE : (jt + 1) * TILE]
         return (arg * sigmoid(arg)).astype(BF16)
 
-    key = act(PAIRS, 0)
-    query = act(PAIRS + 1, 1)
+    key = act(PAIRS)
+    query = act(PAIRS + 1)
     query_t = query.astype(F32).T.astype(BF16)
     scores[...] = mul_nt(key, query)
     grad_scores[...] = jnp.zeros_like(grad_scores)
@@ -282,7 +288,7 @@
 
     def pair(j, carry):
         cols = tile_at(j)
-        arg = conv_argument(cin_ref, cw_ref, cb_ref, cols)
+        arg = ar_ref[:, cols]
         part_x = sigmoid(arg)
         heads_in = arg * part_x
         heads_low = heads_in.astype(BF16)
@@ -354,7 +360,7 @@
         gpre[:SPAN, cols] = grad_conv * (part_x * (1.0 + arg * (1.0 - part_x)))
         return carry
 
-    lax.fori_loop(0, PAIRS, pair, 0)
+    lax.fori_loop(0, PAIRS, pair, 0, unroll=3)
 
     rows = lax.broadcasted_iota(jnp.int32, (SPAN, SPAN), 0)
     columns = lax.broadcasted_iota(jnp.int32, (SPAN, SPAN), 1)
@@ -379,7 +385,7 @@
         (0, acc_k[...] + mul(scores_low, query)),
         (1, acc_q[...] + mul(scores_t, key)),
     ):
-        arg = args[:, slot * TILE : (slot + 1) * TILE]
+        arg = ar_ref[:, DI + slot * TILE : DI + (slot + 1) * TILE]
         part = sigmoid(arg)
         gpre[:SPAN, DI + slot * TILE : DI + (slot + 1) * TILE] = grad * (part * (1.0 + arg * (1.0 - part)))
 
@@ -388,11 +394,12 @@
         here = gpre[:SPAN, cols]
         gcb_ref[:, cols] += fold(here)
         total = jnp.zeros_like(here)
+        given = cin_ref[0, EDGE:, cols]
         for tap in range(CONV):
-            start = EDGE - CONV + 1 + tap
-            taps_ref[tap, :, cols] += fold(here * cin_ref[0, start : start + SPAN, cols])
             ahead = CONV - 1 - tap
-            total = total + cw_ref[tap : tap + 1, cols] * gpre[ahead : ahead + SPAN, cols]
+            later_grad = gpre[ahead : ahead + SPAN, cols]
+            taps_ref[tap, :, cols] += fold(given * later_grad)
+            total = total + cw_ref[tap : tap + 1, cols] * later_grad
         gp_ref[:, tile_at(j, DI)] = total.astype(BF16)
         return carry
 
@@ -412,6 +419,37 @@
         grad_tok = nrm * (value - tok * centre)
         ig_ref[r : r + 64, :] = (cot_ref[r : r + 64, :].astype(F32) + grad_tok).astype(BF16)
 
+    @pl.when(step_id == count - 1)
+    def _():
+        rows = lax.broadcasted_iota(jnp.int32, (DI, TILE), 0) // HEADDIM
+        pick = (lax.broadcasted_iota(jnp.int32, (DI, TILE), 1) == rows + 2 * HEADS).astype(F32)
+        skips = jnp.dot(gsk_ref[...], pick, precision=FULL, preferred_element_type=F32)
+        heads = ghd_ref[:EDGE, :] + pltpu.roll(ghd_ref[EDGE:, :], HEADS, 1) + skips
+        heads = jnp.sum(heads, axis=0, keepdims=True)
+        few_ref[...] = jnp.zeros_like(few_ref)
+        grads = [jnp.sum(gnw_ref[...], axis=0, keepdims=True)]
+        grads += [jnp.sum(taps_ref[tap], axis=0, keepdims=True) for tap in range(CONV)]
+        grads += [jnp.sum(ref[...], axis=0, keepdims=True) for ref in (gcb_ref, ggn_ref)]
+        for r, grad in enumerate(grads):
+            size = grad.shape[1] // peers
+            for k in range(peers):
+                few_ref[k, r : r + 1, :size] = grad[:, k * size : (k + 1) * size]
+        for k in range(peers):
+            few_ref[k, EDGE - 1 : EDGE, :] = heads
+
+
+def split_kernel(sum_ref, *outs):
+    rows = [0, 1, 1 + CONV, 2 + CONV] + [EDGE - 1] * 3
+    for i, (ref, r) in enumerate(zip(outs, rows)):
+        start = max(i - 4, 0) * HEADS
+        ref[...] = sum_ref[r : r + ref.shape[0], start : start + ref.shape[1]]
+
+
+def run_split(total, norm, taps, gate):
+    shapes = [(1, norm), (CONV, taps), (1, taps), (1, gate)] + [(1, HEADS)] * 3
+    outs = pl.pallas_call(split_kernel, out_shape=[jax.ShapeDtypeStruct(s, F32) for s in shapes])(total)
+    return [outs[0][0], outs[1].T, outs[2][0], outs[3][0]], [o[0] for o in outs[4:]]
+
 
 def whole(shape):
     return pl.BlockSpec(shape, lambda i: (0,) * len(shape), pipeline_mode=pl.Buffered(1))
@@ -431,17 +469,18 @@
 
 
 LIMIT = 60 * 2**20
+SCALARS = pl.BlockSpec(memory_space=pltpu.SMEM)
 
 
 def forward_results(length, width):
     count = length // SPAN
     shapes = [
         ((length, width), BF16), ((count, SPAN + EDGE, XBC), F32), ((length, DI), F32), ((length, DI), F32),
-        ((count, STATE, DI), F32), ((length, TILE), F32), ((length, width), BF16), ((length, DI), BF16),
+        ((count, STATE, DI), F32), ((length, TILE), F32), ((length, width), BF16), ((length, DI), BF16), ((length, XBC), F32),
     ]
     out_specs = [
         rows_of(width), pl.BlockSpec((1, SPAN + EDGE, XBC), lambda i: (i, 0, 0)), rows_of(DI), rows_of(DI),
-        pl.BlockSpec((1, STATE, DI), lambda i: (i, 0, 0)), rows_of(TILE), rows_of(width), rows_of(DI),
+        pl.BlockSpec((1, STATE, DI), lambda i: (i, 0, 0)), rows_of(TILE), rows_of(width), rows_of(DI), rows_of(XBC),
     ]
     scratch = [
         pltpu.VMEM((width, TILE), BF16), pltpu.VMEM((HEADS, SPAN, TILE), F32), pltpu.VMEM((PAIRS, SPAN, TILE), F32),
@@ -450,52 +489,50 @@
     return [jax.ShapeDtypeStruct(s, d) for s, d in shapes], out_specs, scratch
 
 
-def run_forward(valid, tok, params):
+def run_forward(lengths, order, tok, params):
     length, width = tok.shape
     shapes, out_specs, scratch = forward_results(length, width)
     return pl.pallas_call(
         forward_kernel,
         grid=(length // SPAN,),
         out_shape=shapes,
-        in_specs=[pl.BlockSpec(memory_space=pltpu.SMEM), rows_of(width), *params_specs(width, params[0].shape[1])],
+        in_specs=[SCALARS, SCALARS, rows_of(width), *params_specs(width, params[0].shape[1])],
         out_specs=out_specs,
         scratch_shapes=scratch,
         compiler_params=pltpu.CompilerParams(dimension_semantics=("arbitrary",), vmem_limit_bytes=LIMIT),
         cost_estimate=pl.CostEstimate(flops=20 * 10**9, bytes_accessed=60 * 10**6, transcendentals=10**7),
-    )(valid, tok, *params)
-
-
-def run_backward(valid, cot, tok, params, kept):
+    )(lengths, order, tok, *params)
+
+
+def run_backward(peers, lengths, order, cot, tok, params, kept):
     length, width = tok.shape
     count = length // SPAN
     proj = DI + XBC + HEADS
     last = count - 1
-    shapes = [
-        ((length, width), BF16), ((length, proj), BF16), ((length, width), BF16), ((CONV, EDGE, XBC), F32), ((EDGE, XBC), F32), ((EDGE, DI), F32),
-        ((EDGE, DI), F32), ((EDGE, width), F32), ((2 * EDGE, TILE), F32),
-    ]
-    out_specs = [rows_of(width, last), rows_of(proj, last), rows_of(width, last), *(whole(s) for s, _ in shapes[3:])]
+    shapes = [((length, width), BF16), ((length, proj), BF16), ((length, width), BF16), ((peers, EDGE, TILE), F32)]
+    out_specs = [rows_of(width, last), rows_of(proj, last), rows_of(width, last), whole(shapes[3][0])]
     kept_specs = [
         pl.BlockSpec((1, SPAN + EDGE, XBC), lambda i: (last - i, 0, 0)), rows_of(DI, last), rows_of(DI, last),
-        pl.BlockSpec((1, STATE, DI), lambda i: (last - i, 0, 0)), rows_of(TILE, last),
+        pl.BlockSpec((1, STATE, DI), lambda i: (last - i, 0, 0)), rows_of(TILE, last), rows_of(XBC, last),
     ]
     square, wide = pltpu.VMEM((SPAN, SPAN), F32), pltpu.VMEM((SPAN, DI), F32)
     narrow = pltpu.VMEM((SPAN, TILE), F32)
     return pl.pallas_call(
-        backward_kernel,
+        functools.partial(backward_kernel, peers),
         grid=(count,),
         out_shape=[jax.ShapeDtypeStruct(s, d) for s, d in shapes],
-        in_specs=[pl.BlockSpec(memory_space=pltpu.SMEM), rows_of(width, last), rows_of(width, last), *params_specs(width, params[0].shape[1]), *kept_specs],
+        in_specs=[SCALARS, SCALARS, rows_of(width, last), rows_of(width, last), *params_specs(width, params[0].shape[1]), *kept_specs],
         out_specs=out_specs,
         scratch_shapes=[
+            *(pltpu.VMEM(s, F32) for s in ((CONV, EDGE, XBC), (EDGE, XBC), (EDGE, DI), (EDGE, DI), (EDGE, width), (2 * EDGE, TILE))),
             pltpu.VMEM((width, TILE), BF16), pltpu.VMEM((HEADS, SPAN, TILE), F32), pltpu.VMEM((PAIRS, SPAN, TILE), F32),
             pltpu.VMEM((TILE, SPAN), F32), pltpu.VMEM((STATE, DI), F32), square, square, wide, wide,
-            pltpu.VMEM((SPAN + EDGE, XBC), F32), pltpu.VMEM((SPAN, 2 * TILE), F32),
+            pltpu.VMEM((SPAN + EDGE, XBC), F32),
             narrow, narrow, narrow, narrow, pltpu.VMEM((EDGE, TILE), F32),
         ],
         compiler_params=pltpu.CompilerParams(dimension_semantics=("arbitrary",), vmem_limit_bytes=LIMIT),
         cost_estimate=pl.CostEstimate(flops=40 * 10**9, bytes_accessed=60 * 10**6, transcendentals=2 * 10**7),
-    )(valid, cot, tok, *params, *kept)
+    )(lengths, order, cot, tok, *params, *kept)
 
 
 def prepare(norm_full, in_full, conv_full, shift_full, gate_full, out_full, step_bias, decay_log, skip_gain):
@@ -527,14 +564,15 @@
 
 
 def gather_forward_kernel(n, *refs):
-    len_ref, tok_ref, cot_ref, in_ref, ow_ref, small_ref, head_ref = refs[:7]
-    blocks = refs[7:15]
-    seq_ref, cots_ref, inf_ref, owf_ref, nw_ref, cw_ref, cb_ref, sk_ref, gn_ref = refs[15:24]
-    own_scratch = refs[24:31]
+    len_ref, ord_ref, tok_ref, cot_ref, in_ref, ow_ref = refs[:6]
+    pieces, (sb_in, dl_in, sk_in) = refs[6:10], refs[10:13]
+    blocks = refs[13:22]
+    seq_ref, cots_ref, inf_ref, owf_ref, nw_ref, cw_ref, cb_ref, sb_ref, dl_ref, sk_ref, gn_ref = refs[22:33]
+    own_scratch = refs[33:40]
     (
-        tok_v, w_v, ow_v, few, tok_stage, cot_stage, own,
+        tok_v, w_v, ow_v, small_ref, few, tok_stage, cot_stage, own,
         tok_s, tok_r, tok_fs, tok_fr, tok_l, cot_s, cot_r, cot_fs, cot_fr, cot_l, small_s, small_r, line_s, line_r, plane_s, plane_r, sib_s, sib_r, keep_s,
-    ) = refs[31:]
+    ) = refs[40:]
     planes = n // PLANE
     block = pl.program_id(0)
     me = lax.axis_index("shard")
@@ -547,7 +585,7 @@
 
     def region(a, k, part=None):
         src, dst = arrays[a]
-        half = src.shape[1] // REP
+        half = dst.shape[1] // REP
         first = pl.cdiv(half // TILE, 2) * TILE
         rows = pl.ds(pl.multiple_of(k * src.shape[0], src.shape[0]), src.shape[0])
         start, size = ((0, first), (first, half - first), (0, half))[2 if part is None else part]
@@ -651,11 +689,9 @@
         )
 
     def local_copies():
-        both = [
-            pltpu.make_async_copy(src, dst.at[pl.ds(pl.multiple_of(me * src.shape[0], 8), src.shape[0])], own.at[a])
-            for a, (src, dst) in enumerate(arrays)
-        ]
-        return both + [
+        src, dst = arrays[1]
+        return [
+            pltpu.make_async_copy(src, dst.at[pl.ds(pl.multiple_of(me * src.shape[0], 8), src.shape[0])], own.at[1]),
             pltpu.make_async_copy(small_ref, few.at[me], own.at[2]),
             own_stage(0),
             own_stage(1),
@@ -727,10 +763,22 @@
         for d in range(1, n):
             pl.semaphore_signal(barrier, inc=1, device_id={"shard": lax.rem(me + d, n)}, device_id_type=MESH)
         pl.semaphore_signal(barrier, inc=1, device_id={"rep": 1 - core}, device_id_type=MESH)
+        small_ref[...] = jnp.zeros_like(small_ref)
+        for row, ref in zip((0, 1, 1 + CONV, 2 + CONV), pieces):
+            small_ref[row : row + ref.shape[0], : ref.shape[1]] = ref[...].astype(F32)
+        for ref, given in ((sb_ref, sb_in), (dl_ref, dl_in)):
+            ref[...] = jnp.zeros_like(ref)
+            ref[:, :HEADS] = given[...]
+        for h in range(HEADS):
+            sk_ref[:, h * HEADDIM : (h + 1) * HEADDIM] = jnp.broadcast_to(sk_in[:, h : h + 1], (1, HEADDIM))
         local = local_copies()
         for copy in local:
             copy.start()
-        for copy in local[:2]:
+        width = in_ref.shape[1]
+        mine = pl.ds(pl.multiple_of(me * in_ref.shape[0], in_ref.shape[0]), in_ref.shape[0])
+        w_v[mine, width // TILE * TILE :] = jnp.zeros((in_ref.shape[0], w_v.shape[1] - width // TILE * TILE), BF16)
+        w_v[mine, :width] = in_ref[...]
+        for copy in local[:1]:
             copy.wait()
         pl.semaphore_wait(barrier, n)
         for a in range(2):
@@ -761,15 +809,13 @@
         for a in range(2):
             for d in range(1, planes):
                 each(d, lambda zz, *_: collect(a, zz))
-        for copy in local[2:]:
+        for copy in local[1:]:
             copy.wait()
         for k in range(n):
             @pl.when(me != k)
             def _():
                 small_copy(k, k).wait_recv()
         lay_out(few, n, nw_ref, cw_ref, cb_ref, gn_ref)
-        for h in range(HEADS):
-            sk_ref[:, h * HEADDIM : (h + 1) * HEADDIM] = jnp.broadcast_to(head_ref[2:3, h : h + 1], (1, HEADDIM))
         for a in range(2):
             for d in range(planes):
                 for kind in range(4):
@@ -795,8 +841,8 @@
         start_stage(1)
 
     forward_step(
-        block, len_ref, tok_v.at[pl.ds(pl.multiple_of(block * SPAN, SPAN), SPAN)], w_v, ow_v,
-        nw_ref, cw_ref, cb_ref, head_ref.at[0:1], head_ref.at[1:2], sk_ref, gn_ref, *blocks, *own_scratch,
+        block, own_length(len_ref, ord_ref), tok_v.at[pl.ds(pl.multiple_of(block * SPAN, SPAN), SPAN)], w_v, ow_v,
+        nw_ref, cw_ref, cb_ref, sb_ref, dl_ref, sk_ref, gn_ref, *blocks, *own_scratch,
     )
 
     @pl.when(block == pl.num_programs(0) - 1)
@@ -845,35 +891,35 @@
         keep.wait()
 
 
-def run_gather_forward(valid, tokens, cotangent, in_weight, out_weight, small, heads):
+def run_gather_forward(lengths, order, tokens, cotangent, in_weight, out_weight, pieces, heads):
     n, piece, width = tokens.shape
     length = n * piece
     planes = n // PLANE
-    proj = in_weight.shape[1]
+    proj = pl.cdiv(in_weight.shape[1], 2 * REP * TILE) * 2 * REP * TILE
     inner = n * out_weight.shape[0]
     hbm = pl.BlockSpec(memory_space=pl.ANY)
     vmem = pl.BlockSpec(memory_space=pltpu.VMEM)
     dma = pltpu.SemaphoreType.DMA
     shapes, out_specs, scratch = forward_results(length, width)
-    rows = [(1, width), (CONV, XBC), (1, XBC), (1, DI), (1, DI)]
+    rows = [(1, width), (CONV, XBC), (1, XBC), (1, TILE), (1, TILE), (1, DI), (1, DI)]
     more = [((length, width), BF16)] * 2 + [((width, proj), BF16), ((inner, width), BF16)] + [(r, F32) for r in rows]
     results = pl.pallas_call(
         functools.partial(gather_forward_kernel, n),
         grid=(length // SPAN,),
         out_shape=shapes + [jax.ShapeDtypeStruct(s, d) for s, d in more],
-        in_specs=[pl.BlockSpec(memory_space=pltpu.SMEM), hbm, hbm, hbm, hbm, vmem, vmem],
+        in_specs=[SCALARS, SCALARS, hbm, hbm, vmem, hbm] + [vmem] * 7,
         out_specs=out_specs + [hbm] * 4 + [whole(r) for r in rows],
         scratch_shapes=scratch + [
             pltpu.VMEM((length, width), BF16), pltpu.VMEM((width, proj), BF16), pltpu.VMEM((inner, width), BF16),
-            pltpu.VMEM((n, EDGE, TILE), F32), *(pltpu.VMEM((planes, PLANE, piece, width), BF16) for _ in range(2)), dma((3,)),
+            pltpu.VMEM((EDGE, TILE), F32), pltpu.VMEM((n, EDGE, TILE), F32), *(pltpu.VMEM((planes, PLANE, piece, width), BF16) for _ in range(2)), dma((3,)),
             *(dma(d) for _ in range(2) for d in ((planes,), (planes,), (planes, PLANE), (planes, PLANE), (planes + 1,))), dma((n,)), dma((n,)), dma((2, planes, 2)), dma((2, planes)),
             dma((2, planes, 6)), dma((2, planes, 6)), dma((2, planes, 4)), dma((2, planes, 4)), dma((3,)),
         ],
         compiler_params=pltpu.CompilerParams(
             dimension_semantics=("arbitrary",), collective_id=0, has_side_effects=True, vmem_limit_bytes=LIMIT
         ),
-    )(valid, tokens, cotangent, in_weight, out_weight, small, heads)
-    return results[:8], results[8:]
+    )(lengths, order, tokens, cotangent, in_weight, out_weight, *pieces, *heads)
+    return results[:9], results[9:]
 
 
 PARTS = (
@@ -1152,56 +1198,34 @@
         parts = x.reshape(peers, piece, width)
         return lax.all_to_all(parts, "shard", split_axis=0, concat_axis=0, tiled=True)
 
-    slots = jnp.arange(peers, dtype=jnp.int32)
-    sequence = jnp.sum(jnp.where(slots == rank, order[0], 0))
-    valid = jnp.sum(jnp.where(slots == sequence, lengths[0], 0))[None]
     direct = peers == PLANE * PLANE and lax.axis_size("rep") == REP and piece % 16 == 0
     if direct:
-        def row(v):
-            return jnp.pad(v.astype(F32).reshape(-1, v.shape[-1]), ((0, 0), (0, TILE - v.shape[-1])))
-
-        blank = jnp.zeros((EDGE - CONV - 3, TILE), F32)
-        small = jnp.concatenate([row(norm_weight), row(conv_weight.T), row(conv_bias), row(gate_norm_weight), blank])
-        heads = jnp.concatenate([row(step_bias), row(decay_log), row(skip_gain), jnp.zeros((EDGE - 3, TILE), F32)])
-        wide = jnp.pad(in_weight, ((0, 0), (0, -in_weight.shape[1] % (2 * REP * TILE))))
-        forward, gathered = run_gather_forward(valid, tokens, cotangent, wide, out_weight, small, heads)
-        out, cin, gr, mx, st, sr, normed, gate_low = forward
-        tok, cot, in_full, out_full, norm_row, taps_rows, shift_row, skip_row, gate_row = gathered
-        params = (in_full, out_full, norm_row, taps_rows, shift_row, heads[0:1], heads[1:2], skip_row, gate_row)
+        pieces = (norm_weight[None], conv_weight.T, conv_bias[None], gate_norm_weight[None])
+        heads = (step_bias[None], decay_log[None], skip_gain[None])
+        forward, gathered = run_gather_forward(lengths, order, tokens, cotangent, in_weight, out_weight, pieces, heads)
+        out, cin, gr, mx, st, sr, normed, gate_low, ar = forward
+        tok, cot, params = gathered[0], gathered[1], gathered[2:]
     else:
         tok, cot = to_sequences(tokens), to_sequences(cotangent)
         params = prepare(
             gather(norm_weight), gather(in_weight), gather(conv_weight), gather(conv_bias),
             gather(gate_norm_weight), gather(out_weight), step_bias, decay_log, skip_gain,
         )
-        out, cin, gr, mx, st, sr, normed, gate_low = run_forward(valid, tok, params)
+        out, cin, gr, mx, st, sr, normed, gate_low, ar = run_forward(lengths, order, tok, params)
     output = to_slots(out)
-    ig, gp, gb, taps, gcb, ggn, gsk, gnw, ghd = run_backward(valid, cot, tok, params, (cin, gr, mx, st, sr))
-    few = [jnp.sum(gnw, axis=0), jnp.sum(taps, axis=1), jnp.sum(gcb, axis=0), jnp.sum(ggn, axis=0)]
-    heads = jnp.stack([
-        jnp.sum(ghd[:EDGE], axis=0)[:HEADS], jnp.sum(ghd[EDGE:], axis=0)[:HEADS],
-        jnp.sum(gsk.reshape(EDGE, HEADS, HEADDIM), axis=(0, 2)),
-    ])
+    ig, gp, gb, few = run_backward(peers, lengths, order, cot, tok, params, (cin, gr, mx, st, sr, ar))
     if direct:
-        parts = [jnp.moveaxis(v.reshape(-1, peers, v.shape[-1] // peers), 1, 0) for v in few]
-        parts.append(jnp.broadcast_to(heads.reshape(1, 1, -1), (peers, 1, heads.size)))
-        few = jnp.concatenate([jnp.pad(v, ((0, 0), (0, 0), (0, TILE - v.shape[2]))) for v in parts], axis=1)
         input_grad, grad_in, grad_out, few = run_scatter(peers, ig, normed, gp, gate_low, gb, few)
-        heads = few[EDGE - 1, : heads.size].reshape(heads.shape)
-        few = [
-            few[0, : norm_weight.size], few[1 : 1 + CONV, : conv_bias.size].T,
-            few[1 + CONV, : conv_bias.size], few[2 + CONV, : gate_norm_weight.size],
-        ]
     else:
         input_grad = to_slots(ig)
 
         def scatter(v):
             return lax.psum(lax.psum_scatter(v, "shard", scatter_dimension=0, tiled=True), "rep")
 
-        few[1] = few[1].T
-        few = [scatter(v) for v in few]
         grad_in, grad_out = scatter(mul_tn(normed, gp)), scatter(mul_tn(gate_low, gb))
-        heads = lax.psum(heads, ("rep", "shard"))
+        parts = scatter(few[:, : EDGE - 1])
+        few = jnp.concatenate([parts[0], lax.psum(few[0, EDGE - 1 :], ("rep", "shard"))])
+    few, heads = run_split(few, norm_weight.size, conv_bias.size, gate_norm_weight.size)
     return (
         output, input_grad, few[0], grad_in, few[1], few[2], heads[0], heads[1], heads[2], few[3], grad_out,
     )

time: 322 us -> 288 us (0.89)
  other arithmetic: 11.6 us -> 0 us
  local copies, waits for them, and re-layouts: 16.3 us -> 5.07 us
  Pallas kernels: 279 us -> 269 us
    pallas_call x1 -> x2, Pallas kernels: 87.3 us -> 77.5 us  [the longest x1 76.2 us: run_backward(): pl.pallas_call(functools.partial(backward_kernel, peers), grid=(count,),...]
    reduce_sum x9 -> x0, other arithmetic: 8.28 us -> none  [the longest x1 1.94 us: on_device(): valid = jnp.sum(jnp.where(slots == sequence, lengths[0], 0))[None]]
    squeeze x4 -> x0, local copies, waits for them, and re-layouts: 4.93 us -> none  [the longest x1 1.37 us: on_device(): heads[2]]
  transfers between devices with their start and end apart: 1 -> 1, of which waited for: 0 -> 0; matrix products, arithmetic and copies ran while one was open for 4% -> 0% of each run, Pallas kernels for 51% -> 53%
where the time goes in v4:
time: 288 us
  Pallas kernels  269 us (93%)
  starting transfers between devices  13.5 us (5%)
  local copies, waits for them, and re-layouts  5.07 us (2%)
    pallas_call x1, Pallas kernels, run_gather_forward(): pl.pallas_call(functools.partial(gather_forward_kernel, n), grid=(length...  116 us
    pallas_call x1, Pallas kernels, run_backward(): pl.pallas_call(functools.partial(backward_kernel, peers), grid=(count,),...  76.2 us
    pallas_call x1, Pallas kernels, run_scatter(): pl.pallas_call(functools.partial(scatter_kernel, n), out_shape=[jax.Shape...  75.4 us
    all_to_all x1, starting transfers between devices, to_slots(): lax.all_to_all(parts, 'shard', split_axis=0, concat_axis=0, tiled=True)  13.5 us
  transfers between devices with their start and end apart: 1, of which 0 were waited for; matrix products, arithmetic and copies ran while one was open for 0% of the time, Pallas kernels for 53%

profile of v4, /device:TPU:0, one launch (start us, length us, event | category | flops | bytes accessed | tf_op | source)
XLA Modules:
  0.0 287.8 jit_solution(17421437343508074341)
XLA Ops:
  0.6 115.7 %shard_map.212 = (bf16[1024,768]{1,0:T(8,128)(2,1)}, f32[4,264,1792]{2,1,0:T(8,128)}, f32[1024,1536]{1,0:T(8,128)}, f32[1024,1536]{1,0:T(8,128)}, f32[4,128,1536...) custom-call(s32[1,16]{1,0:T(1,128)} %len_ref.1, ...), custom_call_target="tpu_custom_call" | custom-call | tf_op jit(solution)/shard_map/pallas_call | solution.py:906
  116.4 13.5 %all-to-all-start = ((bf16[16,64,768]{2,1,0:T(8,128)(2,1)}), bf16[16,64,768]{2,1,0:T(8,128)(2,1)S(1)}, u32[]{:S(2)}, u32[]{:S(2)}) async-start(bf16[16,64,768]{2,1,0:T(8,128)(2,1)} %bitcast.15), calls=%async_computation | async-start | bytes 3145728 | tf_op jit(solution)/shard_map/all_to_all | solution.py:1199
  129.9 76.2 %shard_map.213 = (bf16[1024,768]{1,0:T(8,128)(2,1)}, bf16[1024,3352]{1,0:T(8,128)(2,1)}, bf16[1024,768]{1,0:T(8,128)(2,1)}, f32[16,8,128]{2,1,0:T(8,128)}) custom-call(s32[1,16]{1,0:T(1,128)} %len_ref.1, s32[1,16]{1,0:T(1,128)} %ord_ref.1, bf16[1024,768]{1,0:T(8,128)(2,1)} %get-tuple-element.47.cot_ref, bf16[1024,768]{1,0:T(8,128)(2,1)} %get-tuple-element.48.tok_ref, ...), custom_call_target="tpu_custom_call" | custom-call | flops 40000000000 | bytes 60000000 | tf_op jit(solution)/shard_map/pallas_call | solution.py:520
  206.1 75.4 %shard_map.214 = (bf16[16,64,768]{2,1,0:T(8,128)(2,1)}, f32[48,3352]{1,0:T(8,128)}, f32[96,768]{1,0:T(8,128)}, f32[8,128]{1,0:T(8,128)}) custom-call(bf16[1024,768]{1,0:T(8,128)(2,1)} %get-tuple-element.64.refs_0_, bf16[1024,768]{1,0:T(8,128)(2,1)} %get-tuple-element.65.refs_1_, bf16[1024,3352]{1,0:T(8,128)(2,1)} %get-tuple-element.66.refs_2_, ...), custom_call_target="tpu_custom_call" | custom-call | tf_op jit(solution)/shard_map/pallas_call | solution.py:1172
  281.5 1.3 shard_map.215
  282.8 0.0 all-to-all-done
  282.8 0.0 copy-start
  282.8 1.1 copy.28
  283.9 0.8 copy-done
  284.7 0.0 copy-start.1
  284.7 0.0 copy-start.2
  284.7 1.1 copy.29
  285.9 0.4 copy-done.1
  286.3 0.8 copy.30
  287.1 0.0 copy-done.2
  287.1 0.7 copy.31
Async XLA Ops:
  116.4 166.4 %all-to-all-start = ((bf16[16,64,768]{2,1,0:T(8,128)(2,1)}), bf16[16,64,768]{2,1,0:T(8,128)(2,1)S(1)}, u32[]{:S(2)}, u32[]{:S(2)}) async-start(bf16[16,64,768]{2,1,0:T(8,128)(2,1)} %bitcast.15), calls=%async_computation | async-start | bytes 3145728 | tf_op jit(solution)/shard_map/all_to_all | solution.py:1199
  282.8 2.0 copy-start
  284.7 1.5 copy-start.1
  284.7 2.4 copy-start.2

commit v5 on v4

--- a/solution.py
+++ b/solution.py
@@ -98,8 +98,8 @@
 
 def forward_step(
     block, length, tok_ref, w_ref, ow_ref, nw_ref, cw_ref, cb_ref, sb_ref, dl_ref, sk_ref, gn_ref,
-    out_ref, cin_ref, gr_ref, mx_ref, st_ref, sr_ref, nl_ref, gl_ref, ar_ref,
-    ws, col_t, pair_s, row_s, state, scores, gated, hook=None,
+    out_ref, cin_ref, gr_ref, mx_ref, st_ref, sr_ref, nl_ref, gt_ref, ar_ref,
+    ws, col_t, pair_s, row_s, state, scores, gated, gl_ref, hook=None,
 ):
     offset = block * SPAN
 
@@ -188,6 +188,7 @@
         return carry
 
     lax.fori_loop(0, PAIRS, finish, 0)
+    gt_ref[...] = gl_ref[...].T
     positions = offset + lax.broadcasted_iota(jnp.int32, (SPAN, 256), 0)
     valid = positions < length
     for n in range(0, tok_ref.shape[1], 256):
@@ -199,8 +200,8 @@
 
 def forward_kernel(
     len_ref, ord_ref, tok_ref, w_ref, ow_ref, nw_ref, cw_ref, cb_ref, sb_ref, dl_ref, sk_ref, gn_ref,
-    out_ref, cin_ref, gr_ref, mx_ref, st_ref, sr_ref, nl_ref, gl_ref, ar_ref,
-    ws, col_t, pair_s, row_s, state, scores, gated,
+    out_ref, cin_ref, gr_ref, mx_ref, st_ref, sr_ref, nl_ref, gt_ref, ar_ref,
+    ws, col_t, pair_s, row_s, state, scores, gated, gl_ref,
 ):
     block = pl.program_id(0)
 
@@ -210,8 +211,8 @@
 
     forward_step(
         block, own_length(len_ref, ord_ref), tok_ref, w_ref, ow_ref, nw_ref, cw_ref, cb_ref, sb_ref, dl_ref, sk_ref, gn_ref,
-        out_ref, cin_ref, gr_ref, mx_ref, st_ref, sr_ref, nl_ref, gl_ref, ar_ref,
-        ws, col_t, pair_s, row_s, state, scores, gated,
+        out_ref, cin_ref, gr_ref, mx_ref, st_ref, sr_ref, nl_ref, gt_ref, ar_ref,
+        ws, col_t, pair_s, row_s, state, scores, gated, gl_ref,
     )
 
 
@@ -476,15 +477,15 @@
     count = length // SPAN
     shapes = [
         ((length, width), BF16), ((count, SPAN + EDGE, XBC), F32), ((length, DI), F32), ((length, DI), F32),
-        ((count, STATE, DI), F32), ((length, TILE), F32), ((length, width), BF16), ((length, DI), BF16), ((length, XBC), F32),
+        ((count, STATE, DI), F32), ((length, TILE), F32), ((length, width), BF16), ((DI, length), BF16), ((length, XBC), F32),
     ]
     out_specs = [
         rows_of(width), pl.BlockSpec((1, SPAN + EDGE, XBC), lambda i: (i, 0, 0)), rows_of(DI), rows_of(DI),
-        pl.BlockSpec((1, STATE, DI), lambda i: (i, 0, 0)), rows_of(TILE), rows_of(width), rows_of(DI), rows_of(XBC),
+        pl.BlockSpec((1, STATE, DI), lambda i: (i, 0, 0)), rows_of(TILE), rows_of(width), pl.BlockSpec((DI, SPAN), lambda i: (0, i)), rows_of(XBC),
     ]
     scratch = [
         pltpu.VMEM((width, TILE), BF16), pltpu.VMEM((HEADS, SPAN, TILE), F32), pltpu.VMEM((PAIRS, SPAN, TILE), F32),
-        pltpu.VMEM((TILE, SPAN), F32), pltpu.VMEM((STATE, DI), F32), pltpu.VMEM((SPAN, SPAN), F32), pltpu.VMEM((SPAN, XBC), F32),
+        pltpu.VMEM((TILE, SPAN), F32), pltpu.VMEM((STATE, DI), F32), pltpu.VMEM((SPAN, SPAN), F32), pltpu.VMEM((SPAN, XBC), F32), pltpu.VMEM((SPAN, DI), BF16),
     ]
     return [jax.ShapeDtypeStruct(s, d) for s, d in shapes], out_specs, scratch
 
@@ -504,6 +505,25 @@
     )(lengths, order, tok, *params)
 
 
+def backward_scratch(width):
+    square, wide = pltpu.VMEM((SPAN, SPAN), F32), pltpu.VMEM((SPAN, DI), F32)
+    narrow = pltpu.VMEM((SPAN, TILE), F32)
+    return [
+        *(pltpu.VMEM(s, F32) for s in ((CONV, EDGE, XBC), (EDGE, XBC), (EDGE, DI), (EDGE, DI), (EDGE, width), (2 * EDGE, TILE))),
+        pltpu.VMEM((width, TILE), BF16), pltpu.VMEM((HEADS, SPAN, TILE), F32), pltpu.VMEM((PAIRS, SPAN, TILE), F32),
+        pltpu.VMEM((TILE, SPAN), F32), pltpu.VMEM((STATE, DI), F32), square, square, wide, wide,
+        pltpu.VMEM((SPAN + EDGE, XBC), F32),
+        narrow, narrow, narrow, narrow, pltpu.VMEM((EDGE, TILE), F32),
+    ]
+
+
+def kept_blocks(last):
+    return [
+        pl.BlockSpec((1, SPAN + EDGE, XBC), lambda i: (last - i, 0, 0)), rows_of(DI, last), rows_of(DI, last),
+        pl.BlockSpec((1, STATE, DI), lambda i: (last - i, 0, 0)), rows_of(TILE, last), rows_of(XBC, last),
+    ]
+
+
 def run_backward(peers, lengths, order, cot, tok, params, kept):
     length, width = tok.shape
     count = length // SPAN
@@ -511,25 +531,14 @@
     last = count - 1
     shapes = [((length, width), BF16), ((length, proj), BF16), ((length, width), BF16), ((peers, EDGE, TILE), F32)]
     out_specs = [rows_of(width, last), rows_of(proj, last), rows_of(width, last), whole(shapes[3][0])]
-    kept_specs = [
-        pl.BlockSpec((1, SPAN + EDGE, XBC), lambda i: (last - i, 0, 0)), rows_of(DI, last), rows_of(DI, last),
-        pl.BlockSpec((1, STATE, DI), lambda i: (last - i, 0, 0)), rows_of(TILE, last), rows_of(XBC, last),
-    ]
-    square, wide = pltpu.VMEM((SPAN, SPAN), F32), pltpu.VMEM((SPAN, DI), F32)
-    narrow = pltpu.VMEM((SPAN, TILE), F32)
+    kept_specs = kept_blocks(last)
     return pl.pallas_call(
         functools.partial(backward_kernel, peers),
         grid=(count,),
         out_shape=[jax.ShapeDtypeStruct(s, d) for s, d in shapes],
         in_specs=[SCALARS, SCALARS, rows_of(width, last), rows_of(width, last), *params_specs(width, params[0].shape[1]), *kept_specs],
         out_specs=out_specs,
-        scratch_shapes=[
-            *(pltpu.VMEM(s, F32) for s in ((CONV, EDGE, XBC), (EDGE, XBC), (EDGE, DI), (EDGE, DI), (EDGE, width), (2 * EDGE, TILE))),
-            pltpu.VMEM((width, TILE), BF16), pltpu.VMEM((HEADS, SPAN, TILE), F32), pltpu.VMEM((PAIRS, SPAN, TILE), F32),
-            pltpu.VMEM((TILE, SPAN), F32), pltpu.VMEM((STATE, DI), F32), square, square, wide, wide,
-            pltpu.VMEM((SPAN + EDGE, XBC), F32),
-            narrow, narrow, narrow, narrow, pltpu.VMEM((EDGE, TILE), F32),
-        ],
+        scratch_shapes=backward_scratch(width),
         compiler_params=pltpu.CompilerParams(dimension_semantics=("arbitrary",), vmem_limit_bytes=LIMIT),
         cost_estimate=pl.CostEstimate(flops=40 * 10**9, bytes_accessed=60 * 10**6, transcendentals=2 * 10**7),
     )(lengths, order, cot, tok, *params, *kept)
@@ -568,11 +577,11 @@
     pieces, (sb_in, dl_in, sk_in) = refs[6:10], refs[10:13]
     blocks = refs[13:22]
     seq_ref, cots_ref, inf_ref, owf_ref, nw_ref, cw_ref, cb_ref, sb_ref, dl_ref, sk_ref, gn_ref = refs[22:33]
-    own_scratch = refs[33:40]
+    own_scratch = refs[33:41]
     (
-        tok_v, w_v, ow_v, small_ref, few, tok_stage, cot_stage, own,
-        tok_s, tok_r, tok_fs, tok_fr, tok_l, cot_s, cot_r, cot_fs, cot_fr, cot_l, small_s, small_r, line_s, line_r, plane_s, plane_r, sib_s, sib_r, keep_s,
-    ) = refs[40:]
+        tok_v, w_v, ow_v, small_ref, few, tok_stage, own,
+        tok_s, tok_r, tok_fs, tok_fr, tok_l, cot_s, cot_r, small_s, small_r, line_s, line_r, plane_s, plane_r, sib_s, sib_r, keep_s,
+    ) = refs[41:]
     planes = n // PLANE
     block = pl.program_id(0)
     me = lax.axis_index("shard")
@@ -618,7 +627,6 @@
     quad = me % PLANE
     moves = (
         (tok_ref, tok_stage, tok_v, tok_s, tok_r, tok_fs, tok_fr, tok_l),
-        (cot_ref, cot_stage, cots_ref, cot_s, cot_r, cot_fs, cot_fr, cot_l),
     )
 
     def stage_copy(m, to, source):
@@ -682,6 +690,12 @@
                 def _():
                     pass_copy(m, zz, j, quad).wait_send()
 
+    def cot_copy(to, source):
+        return pltpu.make_async_remote_copy(
+            src_ref=cot_ref.at[to], dst_ref=cots_ref.at[rows(source)], send_sem=cot_s.at[to], recv_sem=cot_r.at[source],
+            device_id={"shard": to}, device_id_type=MESH,
+        )
+
     def small_copy(to, source):
         return pltpu.make_async_remote_copy(
             src_ref=small_ref, dst_ref=few.at[source], send_sem=small_s.at[to], recv_sem=small_r.at[source],
@@ -694,7 +708,7 @@
             pltpu.make_async_copy(src, dst.at[pl.ds(pl.multiple_of(me * src.shape[0], 8), src.shape[0])], own.at[1]),
             pltpu.make_async_copy(small_ref, few.at[me], own.at[2]),
             own_stage(0),
-            own_stage(1),
+            pltpu.make_async_copy(cot_ref.at[me], cots_ref.at[rows(me)], own.at[0]),
         ]
 
     def saves():
@@ -838,7 +852,7 @@
 
     @pl.when(block == COT_AT)
     def _():
-        start_stage(1)
+        send_pieces(cot_copy, 1, n)
 
     forward_step(
         block, own_length(len_ref, ord_ref), tok_v.at[pl.ds(pl.multiple_of(block * SPAN, SPAN), SPAN)], w_v, ow_v,
@@ -851,16 +865,12 @@
         keep.start()
         for copy in saves():
             copy.wait()
-        for zz in range(planes):
-            pass_on(1, zz)
-        for m in range(2):
-            gone(m)
-        for zz in range(planes):
-            landed(1, zz)
+        gone(0)
         for k in range(n):
             @pl.when(me != k)
             def _():
                 small_copy(k, k).wait_send()
+                cot_copy(k, k).wait()
         for a in range(2):
             def sent(zz, origin, to, more):
                 @pl.when(more)
@@ -911,8 +921,8 @@
         out_specs=out_specs + [hbm] * 4 + [whole(r) for r in rows],
         scratch_shapes=scratch + [
             pltpu.VMEM((length, width), BF16), pltpu.VMEM((width, proj), BF16), pltpu.VMEM((inner, width), BF16),
-            pltpu.VMEM((EDGE, TILE), F32), pltpu.VMEM((n, EDGE, TILE), F32), *(pltpu.VMEM((planes, PLANE, piece, width), BF16) for _ in range(2)), dma((3,)),
-            *(dma(d) for _ in range(2) for d in ((planes,), (planes,), (planes, PLANE), (planes, PLANE), (planes + 1,))), dma((n,)), dma((n,)), dma((2, planes, 2)), dma((2, planes)),
+            pltpu.VMEM((EDGE, TILE), F32), pltpu.VMEM((n, EDGE, TILE), F32), pltpu.VMEM((planes, PLANE, piece, width), BF16), dma((3,)),
+            *(dma(d) for d in ((planes,), (planes,), (planes, PLANE), (planes, PLANE), (planes + 1,))), *(dma((n,)) for _ in range(4)), dma((2, planes, 2)), dma((2, planes)),
             dma((2, planes, 6)), dma((2, planes, 6)), dma((2, planes, 4)), dma((2, planes, 4)), dma((3,)),
         ],
         compiler_params=pltpu.CompilerParams(
@@ -922,197 +932,365 @@
     return results[:9], results[9:]
 
 
-PARTS = (
-    (1, 0, 384, 0), (1, 384, 384, 1), (0, 0, 768, 0), (0, 768, 768, 1), (0, 1536, 896, 0), (0, 2432, 920, 1),
-)
-SPREAD = (0, 4, 8, 12, 15)
-
-
-def scatter_kernel(n, *refs):
-    (
-        ig_ref, nl_ref, gp_ref, gl_ref, gb_ref, small_ref,
-        slot_ref, gin_ref, gout_ref, sum_ref,
-    ) = refs[:10]
-    refs = refs[10:]
-    count = len(PARTS)
-    bufs = [refs[i * 7 : (i + 1) * 7] for i in range(count)]
-    (
-        nl_t, gl_t, few, few_sib, own, ig_s, ig_r, few_s, few_r, pair_s, pair_r, s0s, s0r, s1s, s1r, s2s, s2r, s3s, s3r, s4s, s4r,
-    ) = refs[count * 7 :]
-    planes = n // PLANE
-    me = lax.axis_index("shard")
-    core = lax.axis_index("rep")
-    z, y, x = me // PLANE, (me // 2) % 2, me % 2
-    across = {"shard": me + 1 - 2 * x}
-    along = {"shard": me + 2 - 4 * y}
-    twin = {"rep": 1 - core}
-    piece = slot_ref.shape[1]
-
-    barrier = pltpu.get_barrier_semaphore()
-    for d in range(1, n):
-        pl.semaphore_signal(barrier, inc=1, device_id={"shard": lax.rem(me + d, n)}, device_id_type=MESH)
-    pl.semaphore_signal(barrier, inc=1, device_id=twin, device_id_type=MESH)
-
-    def remote(src, dst, s, r, to):
-        return pltpu.make_async_remote_copy(
-            src_ref=src, dst_ref=dst, send_sem=s, recv_sem=r, device_id=to, device_id_type=MESH
-        )
-
-    def ig_copy(d):
-        to = lax.rem(me + d, n)
-        src = ig_ref.at[pl.ds(pl.multiple_of(to * piece, 8), piece)]
-        return remote(src, slot_ref.at[me], ig_s.at[d], ig_r.at[d], {"shard": to})
-
-    def few_copy(d):
-        to = lax.rem(me + d, n)
-        return remote(small_ref.at[to], few.at[me], few_s.at[d], few_r.at[d], {"shard": to})
-
-    first = core == 0
-
-    def product(p):
-        a, start, size, _ = PARTS[p]
-        acc, s0 = bufs[p][0], bufs[p][1]
-        left, right = (nl_t, gp_ref) if a == 0 else (gl_t, gb_ref)
+OUT_PARTS = ((1, 0, 384, 0), (1, 384, 384, 1))
+IN_PARTS = ((0, 0, 768, 0), (0, 768, 768, 1), (0, 1536, 896, 0), (0, 2432, 920, 1))
+
+
+SPREAD = (1, 6, 11, 16, 16)
+
+
+def remote(src, dst, s, r, to):
+    return pltpu.make_async_remote_copy(src_ref=src, dst_ref=dst, send_sem=s, recv_sem=r, device_id=to, device_id_type=MESH)
+
+
+class Reduction:
+    def __init__(self, n, parts, out, refs):
+        self.n, self.parts, self.out = n, parts, out
+        count = len(parts)
+        self.bufs = [refs[i * 7 : (i + 1) * 7] for i in range(count)]
+        self.sems = refs[count * 7 :]
+        self.planes = n // PLANE
+        me = lax.axis_index("shard")
+        self.core = lax.axis_index("rep")
+        self.z, self.y, self.x = me // PLANE, (me // 2) % 2, me % 2
+        self.across = {"shard": me + 1 - 2 * self.x}
+        self.along = {"shard": me + 2 - 4 * self.y}
+        self.twin = {"rep": 1 - self.core}
+
+    @staticmethod
+    def scratch(n, parts, rows):
+        planes, count, dma = n // PLANE, len(parts), pltpu.SemaphoreType.DMA
+        out = []
+        for _, _, size, _ in parts:
+            full = (planes, 2, 2, rows, size)
+            out += [
+                pltpu.VMEM(full, F32), pltpu.VMEM(full, BF16), pltpu.VMEM(full, BF16), pltpu.VMEM(full, BF16),
+                pltpu.VMEM((planes, 2, rows, size), BF16), pltpu.VMEM((planes, rows, size), BF16), pltpu.VMEM((planes, rows, size), BF16),
+            ]
+        return out + [dma((count,))] * 7 + [dma((count, planes))] * 2 + [dma((count,))] * 2
+
+    def product(self, p, left, right):
+        _, start, size, _ = self.parts[p]
+        acc, s0 = self.bufs[p][0], self.bufs[p][1]
+        first = self.core == 0
         rows = acc.shape[3]
         for c in range(0, size, 256):
             wide = min(256, size - c)
             total = mul(left[...], right[:, start + c : start + c + wide])
-            total = total.reshape(planes, 2, 2, 2, rows, wide)
+            total = total.reshape(self.planes, 2, 2, 2, rows, wide)
             acc[:, :, :, :, c : c + wide] = jnp.where(first, total[:, :, :, 0], total[:, :, :, 1])
             s0[:, :, :, :, c : c + wide] = jnp.where(first, total[:, :, :, 1], total[:, :, :, 0]).astype(BF16)
 
-    def c0(p):
-        return remote(bufs[p][1], bufs[p][2], s0s.at[p], s0r.at[p], twin)
-
-    def c1(p):
-        sb, r1 = bufs[p][3], bufs[p][4]
-        if PARTS[p][3] == 0:
-            return remote(sb.at[:, 1 - y], r1, s1s.at[p], s1r.at[p], along)
-        return remote(sb.at[:, :, 1 - x], r1, s1s.at[p], s1r.at[p], across)
-
-    def c2(p):
-        sb, r2 = bufs[p][3], bufs[p][5]
-        if PARTS[p][3] == 0:
-            return remote(sb.at[:, y, 1 - x], r2, s2s.at[p], s2r.at[p], across)
-        return remote(sb.at[:, 1 - y, x], r2, s2s.at[p], s2r.at[p], along)
-
-    def c3(p, dest, source):
-        sb, r3 = bufs[p][3], bufs[p][6]
-        to = {"shard": dest * PLANE + 2 * y + x}
-        return remote(sb.at[dest, y, x], r3.at[source], s3s.at[p, dest], s3r.at[p, source], to)
-
-    def into_half(p):
-        acc, _, r0, sb = bufs[p][:4]
-        c0(p).wait_recv()
+    def c0(self, p):
+        own, s0s, s0r = self.sems[:3]
+        return remote(self.bufs[p][1], self.bufs[p][2], s0s.at[p], s0r.at[p], self.twin)
+
+    def c1(self, p):
+        s1s, s1r = self.sems[3:5]
+        sb, r1 = self.bufs[p][3], self.bufs[p][4]
+        if self.parts[p][3] == 0:
+            return remote(sb.at[:, 1 - self.y], r1, s1s.at[p], s1r.at[p], self.along)
+        return remote(sb.at[:, :, 1 - self.x], r1, s1s.at[p], s1r.at[p], self.across)
+
+    def c2(self, p):
+        s2s, s2r = self.sems[5:7]
+        sb, r2 = self.bufs[p][3], self.bufs[p][5]
+        if self.parts[p][3] == 0:
+            return remote(sb.at[:, self.y, 1 - self.x], r2, s2s.at[p], s2r.at[p], self.across)
+        return remote(sb.at[:, 1 - self.y, self.x], r2, s2s.at[p], s2r.at[p], self.along)
+
+    def c3(self, p, dest, source):
+        s3s, s3r = self.sems[7:9]
+        sb, r3 = self.bufs[p][3], self.bufs[p][6]
+        to = {"shard": dest * PLANE + 2 * self.y + self.x}
+        return remote(sb.at[dest, self.y, self.x], r3.at[source], s3s.at[p, dest], s3r.at[p, source], to)
+
+    def into_half(self, p):
+        acc, _, r0, sb = self.bufs[p][:4]
+        self.c0(p).wait_recv()
 
         def step(i, carry):
-            zz, yy, xx = i // PLANE, (i // 2) % 2, i % 2
-            value = acc[zz, yy, xx] + r0[zz, yy, xx].astype(F32)
-            acc[zz, yy, xx] = value
-            sb[zz, yy, xx] = value.astype(BF16)
+            at = (i // PLANE, (i // 2) % 2, i % 2)
+            value = acc[at] + r0[at].astype(F32)
+            acc[at] = value
+            sb[at] = value.astype(BF16)
             return carry
 
-        lax.fori_loop(0, n, step, 0)
-
-    def after_first(p):
-        acc, _, _, sb, r1 = bufs[p][:5]
-        c1(p).wait_recv()
-        c1(p).wait_send()
+        lax.fori_loop(0, self.n, step, 0)
+        self.c1(p).start()
+
+    def after_first(self, p):
+        acc, _, _, sb, r1 = self.bufs[p][:5]
+        self.c1(p).wait_recv()
+        self.c1(p).wait_send()
 
         def step(i, carry):
             zz, kk = i // 2, i % 2
-            at = (zz, y, kk) if PARTS[p][3] == 0 else (zz, kk, x)
+            at = (zz, self.y, kk) if self.parts[p][3] == 0 else (zz, kk, self.x)
             value = acc[at] + r1[zz, kk].astype(F32)
             acc[at] = value
             sb[at] = value.astype(BF16)
             return carry
 
-        lax.fori_loop(0, 2 * planes, step, 0)
-
-    def after_second(p):
-        acc, _, _, sb, _, r2 = bufs[p][:6]
-        c2(p).wait_recv()
-        c2(p).wait_send()
-        for zz in range(planes):
+        lax.fori_loop(0, 2 * self.planes, step, 0)
+        self.c2(p).start()
+
+    def after_second(self, p):
+        acc, _, _, sb, _, r2 = self.bufs[p][:6]
+        z, y, x = self.z, self.y, self.x
+        self.c2(p).wait_recv()
+        self.c2(p).wait_send()
+        for zz in range(self.planes):
             value = acc[zz, y, x] + r2[zz].astype(F32)
             acc[zz, y, x] = value
             sb[zz, y, x] = value.astype(BF16)
-
-    def to_planes(p):
-        for dest in range(planes):
+        for dest in range(self.planes):
             @pl.when(dest != z)
             def _():
-                c3(p, dest, z).start()
-
-    def results(p):
-        a, start, size, _ = PARTS[p]
-        acc = bufs[p][0]
-        out = gin_ref if a == 0 else gout_ref
+                self.c3(p, dest, z).start()
+
+    def results(self, p):
+        own, s4s, s4r = self.sems[0], *self.sems[9:11]
+        _, start, size, _ = self.parts[p]
+        acc = self.bufs[p][0]
         rows = acc.shape[3]
-        view = out.at[pl.ds(pl.multiple_of(core * rows, 8), rows), pl.ds(start, size)]
-        return (
-            remote(acc.at[z, y, x], view, s4s.at[p], s4r.at[p], twin),
-            pltpu.make_async_copy(acc.at[z, y, x], view, own.at[p]),
+        view = self.out.at[pl.ds(pl.multiple_of(self.core * rows, 8), rows), pl.ds(start, size)]
+        mine = acc.at[self.z, self.y, self.x]
+        return remote(mine, view, s4s.at[p], s4r.at[p], self.twin), pltpu.make_async_copy(mine, view, own.at[p])
+
+    def finish(self, p):
+        acc, r3 = self.bufs[p][0], self.bufs[p][6]
+        for source in range(self.planes):
+            @pl.when(source != self.z)
+            def _():
+                self.c3(p, source, source).wait_recv()
+                acc[self.z, self.y, self.x] += r3[source].astype(F32)
+
+        for copy in self.results(p):
+            copy.start()
+
+    def close(self, p):
+        self.c0(p).wait_send()
+        for dest in range(self.planes):
+            @pl.when(dest != self.z)
+            def _():
+                self.c3(p, dest, self.z).wait_send()
+
+        far, near = self.results(p)
+        near.wait()
+        far.wait()
+
+
+def backward_exchange_kernel(n, *refs):
+    len_ref, ord_ref, out_ref, glt_ref, cot_ref = refs[:5]
+    blocks = refs[5:21]
+    ig_ref, gp_ref, few_ref, slot_ref, gout_ref, out_stage = refs[21:27]
+    scratch = refs[27:48]
+    gb_v, out_s, out_r, out_fs, out_fr, out_l = refs[48:54]
+    red = Reduction(n, OUT_PARTS, gout_ref, refs[54:])
+    planes = n // PLANE
+    step = pl.program_id(0)
+    me = lax.axis_index("shard")
+    z, quad = me // PLANE, me % PLANE
+    piece = slot_ref.shape[1]
+    width = cot_ref.shape[1]
+    moves = ((out_stage, slot_ref, out_fs, out_fr, out_l),)
+
+    def span(c):
+        return pl.ds(pl.multiple_of(c * SPAN, SPAN), SPAN)
+
+    def out_copy(to, source):
+        return remote(
+            out_ref.at[span(to)], out_stage.at[source], out_s.at[to], out_r.at[source], {"shard": to * PLANE + quad}
         )
 
-    def finish(p):
-        acc, r3 = bufs[p][0], bufs[p][6]
-        for source in range(planes):
-            @pl.when(source != z)
-            def _():
-                c3(p, source, source).wait_recv()
-                acc[z, y, x] += r3[source].astype(F32)
-
-        for copy in results(p):
-            copy.start()
-
-    def igs(i):
-        for d in range(1 + SPREAD[i], 1 + SPREAD[i + 1]):
+    def own_out():
+        return pltpu.make_async_copy(out_ref.at[span(z)], out_stage.at[z], out_l.at[planes])
+
+    def pass_copy(m, zz, j, source):
+        stage, dst, ss, sr, _ = moves[m]
+        return remote(
+            stage.at[zz, pl.ds(j * piece, piece)], dst.at[zz * PLANE + source], ss.at[zz, j], sr.at[zz, source],
+            {"shard": z * PLANE + j},
+        )
+
+    def keep_copy(m, zz):
+        stage, dst, _, _, sem = moves[m]
+        rows = pl.ds(pl.multiple_of(quad * piece, piece), piece)
+        return pltpu.make_async_copy(stage.at[zz, rows], dst.at[zz * PLANE + quad], sem.at[zz])
+
+    def pass_on(m):
+        for zz in range(planes):
+            for j in range(PLANE):
+                @pl.when(j != quad)
+                def _():
+                    pass_copy(m, zz, j, quad).start()
+
+            keep_copy(m, zz).start()
+
+    def landed(m):
+        for zz in range(planes):
+            for j in range(PLANE):
+                @pl.when(j != quad)
+                def _():
+                    pass_copy(m, zz, j, quad).wait_send()
+                    pass_copy(m, zz, j, j).wait_recv()
+
+            keep_copy(m, zz).wait()
+
+    @pl.when(step == 0)
+    def _():
+        barrier = pltpu.get_barrier_semaphore()
+        for d in range(1, PLANE):
+            near = z * PLANE + lax.rem(quad + d, PLANE)
+            pl.semaphore_signal(barrier, inc=1, device_id={"shard": near}, device_id_type=MESH)
+        for d in range(1, planes):
+            far = lax.rem(z + d, planes) * PLANE + quad
+            pl.semaphore_signal(barrier, inc=1, device_id={"shard": far}, device_id_type=MESH)
+        pl.semaphore_signal(barrier, inc=1, device_id=red.twin, device_id_type=MESH)
+        own_out().start()
+        length = own_length(len_ref, ord_ref)
+        for c in range(planes):
+            positions = c * SPAN + lax.broadcasted_iota(jnp.int32, (SPAN, width), 0)
+            rows = slice(c * SPAN, (c + 1) * SPAN)
+            gb_v[rows, :] = jnp.where(positions < length, cot_ref[rows, :].astype(F32), 0.0).astype(BF16)
+        pl.semaphore_wait(barrier, PLANE + planes - 1)
+        for c in range(planes):
+            @pl.when(c != z)
+            def _():
+                out_copy(c, z).start()
+
+        for p in range(len(OUT_PARTS)):
+            red.product(p, glt_ref, gb_v)
+            red.c0(p).start()
+
+    @pl.when(step == 1)
+    def _():
+        for p in range(len(OUT_PARTS)):
+            red.into_half(p)
+
+    @pl.when(step == 2)
+    def _():
+        for p in range(len(OUT_PARTS)):
+            red.after_first(p)
+        own_out().wait()
+        for zz in range(planes):
+            @pl.when(zz != z)
+            def _():
+                out_copy(zz, zz).wait_recv()
+
+        pass_on(0)
+
+    @pl.when(step == 3)
+    def _():
+        for p in range(len(OUT_PARTS)):
+            red.after_second(p)
+
+    rows = span(planes - 1 - step)
+    backward_kernel(
+        n, len_ref, ord_ref, cot_ref.at[rows], *blocks, ig_ref, gp_ref, gb_v.at[rows], few_ref, *scratch
+    )
+
+    @pl.when(step == planes - 1)
+    def _():
+        for p in range(len(OUT_PARTS)):
+            red.finish(p)
+        for c in range(planes):
+            @pl.when(c != z)
+            def _():
+                out_copy(c, z).wait_send()
+
+        landed(0)
+        for p in range(len(OUT_PARTS)):
+            red.close(p)
+
+
+def run_backward_exchange(n, lengths, order, out, cot, tok, params, kept, glt):
+    length, width = tok.shape
+    count, piece, planes = length // SPAN, length // n, n // PLANE
+    proj = DI + XBC + HEADS
+    last = count - 1
+    hbm = pl.BlockSpec(memory_space=pl.ANY)
+    dma = pltpu.SemaphoreType.DMA
+    shapes = [
+        ((length, width), BF16), ((length, proj), BF16), ((n, EDGE, TILE), F32), ((n, piece, width), BF16),
+        ((DI // n, width), F32), ((planes, SPAN, width), BF16),
+    ]
+    passes = [dma((planes,)), dma((planes,)), dma((planes, PLANE)), dma((planes, PLANE)), dma((planes + 1,))]
+    return pl.pallas_call(
+        functools.partial(backward_exchange_kernel, n),
+        grid=(count,),
+        out_shape=[jax.ShapeDtypeStruct(s, d) for s, d in shapes],
+        in_specs=[
+            SCALARS, SCALARS, hbm, whole((DI, length)), whole((length, width)), rows_of(width, last),
+            *params_specs(width, params[0].shape[1]), *kept_blocks(last),
+        ],
+        out_specs=[rows_of(width, last), rows_of(proj, last), whole(shapes[2][0])] + [hbm] * 3,
+        scratch_shapes=backward_scratch(width) + [
+            pltpu.VMEM((length, width), BF16), *passes,
+        ] + Reduction.scratch(n, OUT_PARTS, DI // n // REP),
+        compiler_params=pltpu.CompilerParams(
+            dimension_semantics=("arbitrary",), collective_id=2, has_side_effects=True, vmem_limit_bytes=LIMIT
+        ),
+    )(lengths, order, out, glt, cot, tok, *params, *kept)
+
+
+def scatter_kernel(n, *refs):
+    ig_ref, nl_ref, gp_ref, small_ref, slot_ref, gin_ref, sum_ref = refs[:7]
+    nl_t, few, few_sib, ig_s, ig_r, few_s, few_r, pair_s, pair_r, own = refs[7:17]
+    red = Reduction(n, IN_PARTS, gin_ref, refs[17:])
+    me = lax.axis_index("shard")
+    z = me // PLANE
+    piece = slot_ref.shape[1]
+
+    barrier = pltpu.get_barrier_semaphore()
+    for d in range(1, n):
+        pl.semaphore_signal(barrier, inc=1, device_id={"shard": lax.rem(me + d, n)}, device_id_type=MESH)
+    pl.semaphore_signal(barrier, inc=1, device_id=red.twin, device_id_type=MESH)
+
+    def ig_copy(d):
+        to = lax.rem(me + d, n)
+        src = ig_ref.at[pl.ds(pl.multiple_of(to * piece, piece), piece)]
+        return remote(src, slot_ref.at[me], ig_s.at[d], ig_r.at[d], {"shard": to})
+
+    def igs(first, last):
+        for d in range(first, last):
             ig_copy(d).start()
 
-    units = [(0, 1), (2, 3), (4, 5)]
-    gl_t[...] = gl_ref[...].T
-    for p in units[0]:
-        product(p)
+    own_slot = pltpu.make_async_copy(ig_ref.at[pl.ds(pl.multiple_of(me * piece, piece), piece)], slot_ref.at[me], own)
+
+    def few_copy(d):
+        to = lax.rem(me + d, n)
+        return remote(small_ref.at[to], few.at[me], few_s.at[d], few_r.at[d], {"shard": to})
+
+    nl_t[...] = nl_ref[...].T
+    for p in (0, 1):
+        red.product(p, nl_t, gp_ref)
     pl.semaphore_wait(barrier, n)
-    for p in units[0]:
-        c0(p).start()
+    for p in (0, 1):
+        red.c0(p).start()
+    own_slot.start()
+    igs(*SPREAD[0:2])
     for d in range(1, n):
         few_copy(d).start()
-    igs(0)
-    own_slot = pltpu.make_async_copy(
-        ig_ref.at[pl.ds(pl.multiple_of(me * piece, 8), piece)], slot_ref.at[me], own.at[count]
-    )
-    own_slot.start()
-    nl_t[...] = nl_ref[...].T
-
-    def stage(fn, start, u):
-        for p in units[u]:
-            fn(p)
-            if start is not None:
-                start(p).start()
-
-    for p in units[1]:
-        product(p)
-        c0(p).start()
-    stage(into_half, c1, 0)
-    for p in units[2]:
-        product(p)
-        c0(p).start()
-    stage(into_half, c1, 1)
-    igs(1)
-    stage(after_first, c2, 0)
-    stage(into_half, c1, 2)
-    igs(2)
-    stage(after_second, None, 0)
-    stage(to_planes, None, 0)
-    stage(after_first, c2, 1)
-    igs(3)
-    stage(after_second, None, 1)
-    stage(to_planes, None, 1)
-    stage(finish, None, 0)
-    stage(after_first, c2, 2)
-    stage(finish, None, 1)
+    for p in (2, 3):
+        red.product(p, nl_t, gp_ref)
+        red.c0(p).start()
+    for p in (0, 1):
+        red.into_half(p)
+    igs(*SPREAD[1:3])
+    for p in (2, 3):
+        red.into_half(p)
+    igs(*SPREAD[2:4])
+    for p in (0, 1):
+        red.after_first(p)
+    igs(*SPREAD[3:5])
+    for p in (0, 1):
+        red.after_second(p)
+    for p in (2, 3):
+        red.after_first(p)
+    for p in (0, 1):
+        red.finish(p)
     few[me] = small_ref[me]
     for d in range(1, n):
         few_copy(d).wait()
@@ -1120,63 +1298,39 @@
     for k in range(1, n):
         total = total + few[k]
     few_sib[0] = total
-    pair = remote(few_sib.at[0], few_sib.at[1], pair_s, pair_r, twin)
+    pair = remote(few_sib.at[0], few_sib.at[1], pair_s, pair_r, red.twin)
     pair.start()
-    stage(after_second, None, 2)
-    stage(to_planes, None, 2)
-    stage(finish, None, 2)
+    for p in (2, 3):
+        red.after_second(p)
+    for p in (2, 3):
+        red.finish(p)
     pair.wait()
     sum_ref[...] = few_sib[0] + few_sib[1]
     own_slot.wait()
     for d in range(1, n):
         ig_copy(d).wait()
-    for p in range(count):
-        c0(p).wait_send()
-        for dest in range(planes):
-            @pl.when(dest != z)
-            def _():
-                c3(p, dest, z).wait_send()
-
-        far, near = results(p)
-        near.wait()
-        far.wait()
-
-
-def run_scatter(n, ig, normed, gp, gate_low, grad_branch, small):
-    length, width = ig.shape
+    for p in range(len(IN_PARTS)):
+        red.close(p)
+
+
+def run_scatter(n, ig, normed, gp, small):
+    length, width = normed.shape
     piece = length // n
-    planes = n // PLANE
-    proj = gp.shape[1]
-    inner = gate_low.shape[1]
-    vmem = pl.BlockSpec(memory_space=pltpu.VMEM)
-    hbm = pl.BlockSpec(memory_space=pl.ANY)
+    few = small.shape[1:]
+    vmem, hbm = pl.BlockSpec(memory_space=pltpu.VMEM), pl.BlockSpec(memory_space=pl.ANY)
     dma = pltpu.SemaphoreType.DMA
-    scratch = []
-    for a, _, size, _ in PARTS:
-        rows = (width if a == 0 else inner) // n // REP
-        full = (planes, 2, 2, rows, size)
-        scratch += [
-            pltpu.VMEM(full, F32), pltpu.VMEM(full, BF16), pltpu.VMEM(full, BF16), pltpu.VMEM(full, BF16),
-            pltpu.VMEM((planes, 2, rows, size), BF16), pltpu.VMEM((planes, rows, size), BF16), pltpu.VMEM((planes, rows, size), BF16),
-        ]
-    count = len(PARTS)
-    few = small.shape[1:]
-    scratch += [
-        pltpu.VMEM((width, length), BF16), pltpu.VMEM((inner, length), BF16), pltpu.VMEM((n, *few), F32), pltpu.VMEM((2, *few), F32),
-        dma((count + 1,)), dma((n,)), dma((n,)), dma((n,)), dma((n,)), dma(()), dma(()),
-        *(dma((count,)) for _ in range(6)), dma((count, planes)), dma((count, planes)), dma((count,)), dma((count,)),
-    ]
-    shapes = [
-        ((n, piece, width), BF16), ((width // n, proj), F32), ((inner // n, width), F32), (few, F32),
-    ]
+    shapes = [((n, piece, width), BF16), ((width // n, gp.shape[1]), F32), (few, F32)]
     return pl.pallas_call(
         functools.partial(scatter_kernel, n),
         out_shape=[jax.ShapeDtypeStruct(s, d) for s, d in shapes],
-        in_specs=[hbm, vmem, vmem, vmem, vmem, vmem],
-        out_specs=[hbm, hbm, hbm, vmem],
-        scratch_shapes=scratch,
+        in_specs=[hbm, vmem, vmem, vmem],
+        out_specs=[hbm, hbm, vmem],
+        scratch_shapes=[
+            pltpu.VMEM((width, length), BF16), pltpu.VMEM((n, *few), F32), pltpu.VMEM((2, *few), F32),
+            dma((n,)), dma((n,)), dma((n,)), dma((n,)), dma(()), dma(()), dma(()),
+        ] + Reduction.scratch(n, IN_PARTS, width // n // REP),
         compiler_params=pltpu.CompilerParams(collective_id=1, has_side_effects=True, vmem_limit_bytes=LIMIT),
-    )(ig, normed, gp, gate_low, grad_branch, small)
+    )(ig, normed, gp, small)
 
 
 def on_device(
@@ -1184,7 +1338,6 @@
     step_bias, decay_log, skip_gain, gate_norm_weight, out_weight,
 ):
     peers = lax.axis_size("shard")
-    rank = lax.axis_index("shard")
     piece, width = tokens.shape[1:]
 
     def gather(x):
@@ -1198,7 +1351,7 @@
         parts = x.reshape(peers, piece, width)
         return lax.all_to_all(parts, "shard", split_axis=0, concat_axis=0, tiled=True)
 
-    direct = peers == PLANE * PLANE and lax.axis_size("rep") == REP and piece % 16 == 0
+    direct = peers == PLANE * PLANE and lax.axis_size("rep") == REP and peers * piece == PLANE * SPAN
     if direct:
         pieces = (norm_weight[None], conv_weight.T, conv_bias[None], gate_norm_weight[None])
         heads = (step_bias[None], decay_log[None], skip_gain[None])
@@ -1212,17 +1365,20 @@
             gather(gate_norm_weight), gather(out_weight), step_bias, decay_log, skip_gain,
         )
         out, cin, gr, mx, st, sr, normed, gate_low, ar = run_forward(lengths, order, tok, params)
-    output = to_slots(out)
-    ig, gp, gb, few = run_backward(peers, lengths, order, cot, tok, params, (cin, gr, mx, st, sr, ar))
+    kept = (cin, gr, mx, st, sr, ar)
     if direct:
-        input_grad, grad_in, grad_out, few = run_scatter(peers, ig, normed, gp, gate_low, gb, few)
+        results = run_backward_exchange(peers, lengths, order, out, cot, tok, params, kept, gate_low)
+        ig, gp, few, output, grad_out = results[:5]
+        input_grad, grad_in, few = run_scatter(peers, ig, normed, gp, few)
     else:
+        output = to_slots(out)
+        ig, gp, gb, few = run_backward(peers, lengths, order, cot, tok, params, kept)
         input_grad = to_slots(ig)
 
         def scatter(v):
             return lax.psum(lax.psum_scatter(v, "shard", scatter_dimension=0, tiled=True), "rep")
 
-        grad_in, grad_out = scatter(mul_tn(normed, gp)), scatter(mul_tn(gate_low, gb))
+        grad_in, grad_out = scatter(mul_tn(normed, gp)), scatter(mul(gate_low, gb))
         parts = scatter(few[:, : EDGE - 1])
         few = jnp.concatenate([parts[0], lax.psum(few[0, EDGE - 1 :], ("rep", "shard"))])
     few, heads = run_split(few, norm_weight.size, conv_bias.size, gate_norm_weight.size)

time: 288 us -> 268 us (0.931)
  starting transfers between devices: 13.5 us -> 0 us
  Pallas kernels: 269 us -> 261 us
    all_to_all x1 -> x0, starting transfers between devices: 13.5 us -> none  [to_slots(): lax.all_to_all(parts, 'shard', split_axis=0, concat_axis=0, tiled=True)]
    pallas_call x1, Pallas kernels: 76.2 us -> 89.4 us  [run_backward_exchange(): pl.pallas_call(functools.partial(backward_exchange_kernel, n), grid=(coun...]
    pallas_call x1, Pallas kernels: 75.4 us -> 63.7 us  [run_scatter(): pl.pallas_call(functools.partial(scatter_kernel, n), out_shape=[jax.Shape...]
    pallas_call x1, Pallas kernels: 116 us -> 107 us  [run_gather_forward(): pl.pallas_call(functools.partial(gather_forward_kernel, n), grid=(length...]
  transfers between devices with their start and end apart: 1 -> 0, of which waited for: 0 -> 0; matrix products, arithmetic and copies ran while one was open for 0% -> 0% of each run, Pallas kernels for 53% -> 0%
where the time goes in v5:
time: 268 us; the launch traced here: 267 us
  Pallas kernels  261 us (97%)
  local copies, waits for them, and re-layouts  5.07 us (2%)
    pallas_call x1, Pallas kernels, run_gather_forward(): pl.pallas_call(functools.partial(gather_forward_kernel, n), grid=(length...  107 us
    pallas_call x1, Pallas kernels, run_backward_exchange(): pl.pallas_call(functools.partial(backward_exchange_kernel, n), grid=(coun...  89.4 us
    pallas_call x1, Pallas kernels, run_scatter(): pl.pallas_call(functools.partial(scatter_kernel, n), out_shape=[jax.Shape...  63.7 us

profile of v5, /device:TPU:0, one launch (start us, length us, event | category | flops | bytes accessed | tf_op | source)
XLA Modules:
  0.0 267.2 jit_solution(12263969085122079926)
XLA Ops:
  0.6 107.1 %shard_map.212 = (bf16[1024,768]{1,0:T(8,128)(2,1)}, f32[4,264,1792]{2,1,0:T(8,128)}, f32[1024,1536]{1,0:T(8,128)}, f32[1024,1536]{1,0:T(8,128)}, f32[4,128,1536...) custom-call(s32[1,16]{1,0:T(1,128)} %refs_0_.3, ...), custom_call_target="tpu_custom_call" | custom-call | tf_op jit(solution)/shard_map/pallas_call | solution.py:916
  107.7 89.4 %shard_map.213 = (bf16[1024,768]{1,0:T(8,128)(2,1)}, bf16[1024,3352]{1,0:T(8,128)(2,1)}, f32[16,8,128]{2,1,0:T(8,128)}, bf16[16,64,768]{2,1,0:T(8,128)(2,1)}, f3...) custom-call(s32[1,16]{1,0:T(1,128)} %refs_0_.3, s32[1,16]{1,0:T(1,128)} %refs_1_.3, ...), custom_call_target="tpu_custom_call" | custom-call | tf_op jit(solution)/shard_map/pallas_call | solution.py:1220
  197.2 0.0 copy-start
  197.2 63.7 %shard_map.214 = (bf16[16,64,768]{2,1,0:T(8,128)(2,1)}, f32[48,3352]{1,0:T(8,128)}, f32[8,128]{1,0:T(8,128)}) custom-call(bf16[1024,768]{1,0:T(8,128)(2,1)} %get-tuple-element.66.refs_0_, bf16[1024,768]{1,0:T(8,128)(2,1)} %get-tuple-element.67.refs_1_, bf16[1024,3352]{1,0:T(8,128)(2,1)} %get-tuple-element.68.refs_2_, f32[16,8,128]{2,1,0:T(8,128)} %get-tuple-element.69.refs_3_), custom_call_target="tpu_custom_call" | custom-call | tf_op jit(solution)/shard_map/pallas_call | solution.py:1323
  260.9 1.3 shard_map.215
  262.1 0.0 copy-done
  262.1 0.0 copy-start.1
  262.2 1.1 copy.28
  263.3 0.8 copy-done.1
  264.1 0.0 copy-start.2
  264.1 0.0 copy-start.3
  264.1 1.1 copy.29
  265.3 0.4 copy-done.2
  265.7 0.8 copy.30
  266.5 0.0 copy-done.3
  266.5 0.7 copy.31
Async XLA Ops:
  197.2 65.0 %copy-start = (bf16[16,64,768]{2,1,0:T(8,128)(2,1)S(1)}, bf16[16,64,768]{2,1,0:T(8,128)(2,1)}, u32[]{:S(2)}) copy-start(bf16[16,64,768]{2,1,0:T(8,128)(2,1)} %get-tuple-element.92) | copy-start | bytes 4718596
  262.1 2.0 copy-start.1
  264.1 1.5 copy-start.2
  264.1 2.4 copy-start.3

commit v6 on v5

--- a/solution.py
+++ b/solution.py
@@ -19,6 +19,7 @@
 HALF = SPAN // 2
 EDGE = 8
 epsilon = 1e-05
+LOG2E = 1.4426950408889634
 F32 = jnp.float32
 BF16 = jnp.bfloat16
 FULL = lax.Precision.HIGHEST
@@ -76,7 +77,8 @@
     columns = lax.broadcasted_iota(jnp.int32, (SPAN, SPAN), 1)
     lower = (rows >= columns).astype(F32)
     cumul = jnp.dot(lower, log_decay, precision=FULL, preferred_element_type=F32)
-    return shifted, step, cumul, cumul - jnp.log(step)
+    cumul = cumul * LOG2E
+    return shifted, step, cumul, cumul - jnp.log2(step)
 
 
 def own_length(len_ref, ord_ref):
@@ -150,8 +152,8 @@
         last = cum[SPAN - 1 : SPAN, :]
         old = state[:, cols]
         across = mul(query, old.astype(BF16))
-        weighted = (heads_low.astype(F32) * jnp.exp(last - pair_s[j])).astype(BF16)
-        state[:, cols] = jnp.exp(last) * old + mul(key_t, weighted)
+        weighted = (heads_low.astype(F32) * jnp.exp2(last - pair_s[j])).astype(BF16)
+        state[:, cols] = jnp.exp2(last) * old + mul(key_t, weighted)
         zero = jnp.zeros_like(heads_low)
         parts = (jnp.where(low_lanes, heads_low, zero), jnp.where(low_lanes, zero, heads_low))
         top, bottom = [], []
@@ -159,11 +161,11 @@
             col = (cum0, cum1)[h]
             row = row_s[pl.ds(2 * j + h, 1), :]
             first = jnp.where(mask, col[:HALF] - row[:, :HALF], -jnp.inf)
-            top.append((scores[:HALF, :HALF] * jnp.exp(first)).astype(BF16))
+            top.append((scores[:HALF, :HALF] * jnp.exp2(first)).astype(BF16))
             full = col[HALF:] - row[:, :HALF]
-            bottom.append((scores[HALF:, :HALF] * jnp.exp(full)).astype(BF16))
+            bottom.append((scores[HALF:, :HALF] * jnp.exp2(full)).astype(BF16))
             second = jnp.where(mask, col[HALF:] - row[:, HALF:], -jnp.inf)
-            bottom.append((scores[HALF:, HALF:] * jnp.exp(second)).astype(BF16))
+            bottom.append((scores[HALF:, HALF:] * jnp.exp2(second)).astype(BF16))
         tops = jnp.concatenate([p[:HALF] for p in parts], axis=0)
         within = jnp.concatenate(
             [
@@ -172,7 +174,7 @@
             ],
             axis=0,
         )
-        mixed = within + jnp.exp(cum) * across + sk_ref[:, cols] * heads_in
+        mixed = within + jnp.exp2(cum) * across + sk_ref[:, cols] * heads_in
         mx_ref[:, cols] = mixed
         gate = gr_ref[:, cols]
         value = mixed * (gate * sigmoid(gate))
@@ -305,13 +307,13 @@
         gp_ref[:, cols] = (grad_gated * mixed * (part * (1.0 + gate * (1.0 - part)))).astype(BF16)
         gsk_ref[:, cols] += fold(grad_scan * heads_in)
         cum = pair_t[j]
-        growth = jnp.exp(cum)
+        growth = jnp.exp2(cum)
         last = cum[SPAN - 1 : SPAN, :]
         grad_low = grad_scan.astype(BF16)
         scaled = growth * grad_scan
         grad_across = scaled.astype(BF16)
         col0, col1 = col_s[2 * j], col_s[2 * j + 1]
-        carry_weight = jnp.exp(last - jnp.where(low_lanes, col0, col1))
+        carry_weight = jnp.exp2(last - jnp.where(low_lanes, col0, col1))
         weighted = (heads_float * carry_weight).astype(BF16)
         after = later[:, cols]
         after_low = after.astype(BF16)
@@ -320,7 +322,7 @@
         across = mul(query, before_low)
         acc_k[...] += mul_nt(weighted, after_low)
         acc_q[...] += mul_nt(grad_across, before_low)
-        grow_last = jnp.exp(last)
+        grow_last = jnp.exp2(last)
         carried = mul(key, after_low) * carry_weight
         last_sum = fold(carried * heads_float) + fold(after * before) * grow_last
         later[:, cols] = mul(query_t, grad_across) + grow_last * after
@@ -332,13 +334,13 @@
             row = row_t[pl.ds(2 * j + h, 1), :]
             mixed_top = mul_nt(heads_low[:HALF], parts[h])
             mixed_low = mul_nt(heads_low[HALF:], parts[h][HALF:])
-            factor = jnp.exp(jnp.where(mask, row[:, :HALF] - col[:HALF], -jnp.inf))
+            factor = jnp.exp2(jnp.where(mask, row[:, :HALF] - col[:HALF], -jnp.inf))
             top.append((scores[:HALF, :HALF] * factor).astype(BF16))
             grad_scores[:HALF, :HALF] += mixed_top[:, :HALF] * factor
-            factor = jnp.exp(row[:, HALF:] - col[:HALF])
+            factor = jnp.exp2(row[:, HALF:] - col[:HALF])
             top.append((scores[:HALF, HALF:] * factor).astype(BF16))
             grad_scores[:HALF, HALF:] += mixed_top[:, HALF:] * factor
-            factor = jnp.exp(jnp.where(mask, row[:, HALF:] - col[HALF:], -jnp.inf))
+            factor = jnp.exp2(jnp.where(mask, row[:, HALF:] - col[HALF:], -jnp.inf))
             bottom.append((scores[HALF:, HALF:] * factor).astype(BF16))
             grad_scores[HALF:, HALF:] += mixed_low * factor
         lows = jnp.concatenate([p[HALF:] for p in parts], axis=0)
@@ -844,9 +846,14 @@
         pass_on(0, 0)
         forward_start(w_v, own_scratch[0], own_scratch[4], blocks[1])
 
-    @pl.when(block + 1 < planes)
+    @pl.when(block < 2)
     def _():
         pass_on(0, block + 1)
+
+    @pl.when(block == 1)
+    def _():
+        for zz in range(3, planes):
+            pass_on(0, zz)
 
     landed(0, block)
 

time: 268 us -> 266 us (level)
  no operation moved by 1% of the time
where the time goes in v6:
time: 266 us; the launch traced here: 265 us
  Pallas kernels  259 us (97%)
  local copies, waits for them, and re-layouts  5.07 us (2%)
    pallas_call x1, Pallas kernels, run_gather_forward(): pl.pallas_call(functools.partial(gather_forward_kernel, n), grid=(length...  105 us
    pallas_call x1, Pallas kernels, run_backward_exchange(): pl.pallas_call(functools.partial(backward_exchange_kernel, n), grid=(coun...  89.5 us
    pallas_call x1, Pallas kernels, run_scatter(): pl.pallas_call(functools.partial(scatter_kernel, n), out_shape=[jax.Shape...  63.5 us

profile of v6, /device:TPU:0, one launch (start us, length us, event | category | flops | bytes accessed | tf_op | source)
XLA Modules:
  0.0 264.7 jit_solution(3592421557796583537)
XLA Ops:
  0.6 104.7 %shard_map.212 = (bf16[1024,768]{1,0:T(8,128)(2,1)}, f32[4,264,1792]{2,1,0:T(8,128)}, f32[1024,1536]{1,0:T(8,128)}, f32[1024,1536]{1,0:T(8,128)}, f32[4,128,1536...) custom-call(s32[1,16]{1,0:T(1,128)} %refs_0_.3, ...), custom_call_target="tpu_custom_call" | custom-call | tf_op jit(solution)/shard_map/pallas_call | solution.py:923
  105.3 89.5 %shard_map.213 = (bf16[1024,768]{1,0:T(8,128)(2,1)}, bf16[1024,3352]{1,0:T(8,128)(2,1)}, f32[16,8,128]{2,1,0:T(8,128)}, bf16[16,64,768]{2,1,0:T(8,128)(2,1)}, f3...) custom-call(s32[1,16]{1,0:T(1,128)} %refs_0_.3, s32[1,16]{1,0:T(1,128)} %refs_1_.3, ...), custom_call_target="tpu_custom_call" | custom-call | tf_op jit(solution)/shard_map/pallas_call | solution.py:1227
  194.9 0.0 copy-start
  194.9 63.5 %shard_map.214 = (bf16[16,64,768]{2,1,0:T(8,128)(2,1)}, f32[48,3352]{1,0:T(8,128)}, f32[8,128]{1,0:T(8,128)}) custom-call(bf16[1024,768]{1,0:T(8,128)(2,1)} %get-tuple-element.66.refs_0_, bf16[1024,768]{1,0:T(8,128)(2,1)} %get-tuple-element.67.refs_1_, bf16[1024,3352]{1,0:T(8,128)(2,1)} %get-tuple-element.68.refs_2_, f32[16,8,128]{2,1,0:T(8,128)} %get-tuple-element.69.refs_3_), custom_call_target="tpu_custom_call" | custom-call | tf_op jit(solution)/shard_map/pallas_call | solution.py:1330
  258.4 1.3 shard_map.215
  259.7 0.0 copy-done
  259.7 0.0 copy-start.1
  259.7 1.1 copy.28
  260.8 0.8 copy-done.1
  261.6 0.0 copy-start.2
  261.6 0.0 copy-start.3
  261.6 1.1 copy.29
  262.8 0.4 copy-done.2
  263.2 0.8 copy.30
  264.0 0.0 copy-done.3
  264.0 0.7 copy.31
Async XLA Ops:
  194.9 64.8 %copy-start = (bf16[16,64,768]{2,1,0:T(8,128)(2,1)S(1)}, bf16[16,64,768]{2,1,0:T(8,128)(2,1)}, u32[]{:S(2)}) copy-start(bf16[16,64,768]{2,1,0:T(8,128)(2,1)} %get-tuple-element.92) | copy-start | bytes 4718596
  259.7 2.0 copy-start.1
  261.6 1.5 copy-start.2
  261.6 2.4 copy-start.3
